TPU v7x, 256 devices: a whole 4x4x8 slice. The times are simulated.
256 devices in a mesh: role: 4 (over y), dom: 64 (over x, z, core).
Axes of the slice: x: 4, y: 4, z: 8, core: 2. Of those that a mesh axis runs over, the one named last changes fastest.
Arguments:
- node_feats: bfloat16 [32768, 512], P(('role', 'dom')), may hold values from -6 to 6
- hub_feats: bfloat16 [1024, 512], P(('role', 'dom')), may hold values from -6 to 6
- weight: bfloat16 [1024, 512], replicated, may hold values from -0.1875 to 0.1875
- edge_src: int32 [256, 1024], P(('role', 'dom')), may hold values from 0 to 1183, as said below
- edge_dst: int32 [256, 1024], P(('role', 'dom')), may hold values from 0 to 127, as said below
- bound_rows: int32 [256, 16], P(('role', 'dom')), may hold values from 0 to 127
- hub_edge_src: int32 [256, 1024], P(('role', 'dom')), may hold values from 0 to 127
- hub_edge_slot: int32 [256, 1024], P(('role', 'dom')), may hold values from 0 to 511, as said below
- slot_hub: int32 [256, 512], P(('role', 'dom')), may hold values from 0 to 3, as said below
Outputs:
- node_out: bfloat16 [32768, 512], P(('role', 'dom'))
- hub_out: bfloat16 [1024, 512], P(('role', 'dom'))
Inputs may be any that keep to these rules, and one draw needn't show every extreme that they name: `edge_src`: row indices into the source table of the device: its own nodes, then 16 rows of the device before it along dom, then 16 of the device after it, then the 1024 hubs. `edge_dst`: each node of a device is the destination of at least one of the device's edges. `hub_edge_slot`: every slot of a device receives at least one of its hub edges; slot s belongs to the owner numbered s // 2. `slot_hub`: every hub of every owner is fed by at least one slot of some device.
All inputs are finite; a program needn't handle non-finite values.
Results may differ from a plain program's by a relative error of at most 0.0027.
Values may be sent and summed in bfloat16 or wider, within the bound.
No kernel may reach another device: no remote copies, remote signals or barrier semaphores. Data moves between devices by JAX's collectives and lax.ppermute only.
A program may use at most 64 MiB of HBM per device.

v0:
```python
import math

import jax
import jax.numpy as jnp
from jax import lax
from jax.sharding import Mesh
from jax.sharding import PartitionSpec as P

DOM = ("dom_0", "dom_1", "dom_2")
ROLE_DOM = ("role", "dom_0", "dom_1", "dom_2")


epsilon = 1e-06


def extended(block, sides, width):
    for axis, dim in sides:
        count = lax.axis_size(axis)
        forward = [(i, i + 1) for i in range(count - 1)]
        forward.append((count - 1, 0))
        backward = [(target, source) for source, target in forward]
        low = lax.ppermute(
            lax.slice_in_dim(block, block.shape[dim] - width, None, axis=dim), axis, forward
        )
        high = lax.ppermute(lax.slice_in_dim(block, 0, width, axis=dim), axis, backward)
        block = jnp.concatenate([low, block, high], axis=dim)
    return block


def from_everyone(value, axis):
    count = lax.axis_size(axis)
    return lax.all_to_all(
        jnp.broadcast_to(value[None], (count, *value.shape)), axis, 0, 0, tiled=True
    )


def laid_out(parts, dim):
    dims = list(parts.shape[1:])
    dims[dim] *= parts.shape[0]
    return jnp.moveaxis(parts, 0, dim).reshape(dims)


def gather_axes(value, axes, dim):
    far, near = axes
    first = from_everyone(value, far)
    parts = jnp.swapaxes(from_everyone(first, near), 0, 1)
    return laid_out(parts.reshape(-1, *value.shape), dim)


def cut_along(value, dim, count):
    before, after = (value.shape[:dim], value.shape[dim + 1 :])
    return jnp.moveaxis(value.reshape(*before, count, -1, *after), dim, 0)


def one_exchange(value, axis, axes, splits, concats):
    sizes = [lax.axis_size(a) for a in axes]
    parts = cut_along(value, splits[0], sizes[0])
    parts = jnp.moveaxis(cut_along(parts, splits[1] + 1, sizes[1]), 0, 1)
    inside = parts.shape[2:]
    parts = parts.reshape(-1, *inside)
    parts = lax.all_to_all(parts, axis, split_axis=0, concat_axis=0, tiled=True)
    parts = laid_out(parts.reshape(*sizes, *inside), concats[0] + 1)
    return laid_out(parts, concats[1])


def sage_update(self_rows, mean_rows, weight):
    feature_width = self_rows.shape[1]
    linear = jnp.dot(self_rows, weight[:feature_width], preferred_element_type=jnp.float32)
    linear = linear + jnp.dot(mean_rows, weight[feature_width:], preferred_element_type=jnp.float32)
    rectified = jnp.maximum(linear, 0.0)
    inverse_norm = lax.rsqrt(jnp.mean(rectified * rectified, axis=1, keepdims=True) + epsilon)
    return (rectified * inverse_norm).astype(jnp.bfloat16)


def on_device(
    node_feats,
    hub_feats,
    weight,
    edge_src,
    edge_dst,
    bound_rows,
    hub_edge_src,
    hub_edge_slot,
    slot_hub,
):
    feature_width = node_feats.shape[1]
    local_nodes = node_feats.shape[0]
    hub_local = hub_feats.shape[0]
    exports = node_feats[bound_rows[0]]
    bound_size = exports.shape[0]
    widened = extended(exports, ((DOM, 0),), bound_size)
    hub_table = gather_axes(hub_feats, ("role", ("dom_0", "dom_1", "dom_2")), 0)
    source_table = jnp.concatenate(
        [node_feats, widened[:bound_size], widened[2 * bound_size :], hub_table], axis=0
    )
    sources = edge_src[0]
    targets = edge_dst[0]
    edge_block = math.gcd(sources.shape[0], 2048)

    def add_block(sums, indices):
        node_sums, node_degree = sums
        block_sources, block_targets = indices
        picked = source_table[block_sources].astype(jnp.float32)
        return (
            (node_sums.at[block_targets].add(picked), node_degree.at[block_targets].add(1.0)),
            None,
        )

    initial = (
        jnp.zeros((local_nodes, feature_width), jnp.float32),
        jnp.zeros((local_nodes,), jnp.float32),
    )
    (node_sums, node_degree), unused = lax.scan(
        add_block, initial, (sources.reshape(-1, edge_block), targets.reshape(-1, edge_block))
    )
    hub_sources = hub_edge_src[0]
    hub_slots = hub_edge_slot[0]
    slot_table = slot_hub[0]
    slot_total = slot_table.shape[0]
    role_count = lax.axis_size("role")
    dom_count = lax.axis_size(DOM)
    per_owner = slot_total // (role_count * dom_count)
    partial_value = (
        jnp.zeros((slot_total, feature_width), jnp.float32)
        .at[hub_slots]
        .add(node_feats[hub_sources].astype(jnp.float32))
    )
    slot_counts = jnp.zeros((slot_total,), jnp.float32).at[hub_slots].add(1.0)
    outgoing = (
        partial_value.reshape(role_count, dom_count, per_owner, feature_width),
        slot_counts.reshape(role_count, dom_count, per_owner),
        slot_table.astype(jnp.float32).reshape(role_count, dom_count, per_owner),
    )
    incoming_rows, incoming_counts, incoming_hubs = (
        one_exchange(outgoing[0], ROLE_DOM, ("role", DOM), (0, 1), (0, 1)),
        one_exchange(outgoing[1], ROLE_DOM, ("role", DOM), (0, 1), (0, 1)),
        one_exchange(outgoing[2], ROLE_DOM, ("role", DOM), (0, 1), (0, 1)),
    )
    incoming_rows = incoming_rows.reshape(-1, feature_width)
    onehot = (
        incoming_hubs.reshape(-1)[:, None] == jnp.arange(hub_local, dtype=jnp.float32)[None, :]
    ).astype(jnp.float32)
    hub_sums = jnp.dot(
        onehot.T, incoming_rows, precision=lax.Precision.HIGHEST, preferred_element_type=jnp.float32
    )
    hub_degree = jnp.dot(
        incoming_counts.reshape(-1),
        onehot,
        precision=lax.Precision.HIGHEST,
        preferred_element_type=jnp.float32,
    )
    node_mean = (node_sums / node_degree[:, None]).astype(jnp.bfloat16)
    node_out = sage_update(node_feats, node_mean, weight)
    hub_mean = (hub_sums / hub_degree[:, None]).astype(jnp.bfloat16)
    hub_out = sage_update(hub_feats, hub_mean, weight)
    return (node_out, hub_out)


def solution(mesh):
    finer = Mesh(
        mesh.devices.reshape(mesh.shape["role"], 4, 8, 2), ("role", "dom_0", "dom_1", "dom_2")
    )
    in_specs = (
        P(ROLE_DOM, None),
        P(ROLE_DOM, None),
        P(),
        P(ROLE_DOM, None),
        P(ROLE_DOM, None),
        P(ROLE_DOM, None),
        P(ROLE_DOM, None),
        P(ROLE_DOM, None),
        P(ROLE_DOM, None),
    )
    out_specs = (P(ROLE_DOM, None), P(ROLE_DOM, None))
    return jax.shard_map(
        on_device, mesh=finer, in_specs=in_specs, out_specs=out_specs, check_vma=False
    )
```

profile of v0, /device:TPU:1, one launch (start us, length us, event | category | flops | bytes accessed | tf_op | source)
XLA Modules:
  0.0 142.8 jit_solution(16411755716449356093)
XLA Ops:
  0.6 0.7 compare_select_fusion.1
  1.3 7.6 %scatter_custom_fusion.3 = f32[512]{0:T(512)S(1)} fusion(s32[1024]{0:T(1024)S(1)} %bitcast.64, f32[1024]{0:T(1024)S(1)} %broadcast.143, f32[]{:T(128)} %constant.9.clone.1), kind=kCustom, calls=%fused_computation.45 | custom fusion | flops 1024 | bytes 2052 | tf_op jit(solution)/shard_map/scatter-add | solution.py:128
  8.9 0.8 reshape_transpose_transpose_reshape_reshape_reshape.8
  9.7 15.6 %all-to-all-start.4 = ((f32[256,1,1,2]{3,2,1,0:T(1,128)}), f32[256,1,1,2]{3,2,1,0:T(1,128)S(1)}, u32[]{:S(2)}, u32[]{:S(2)}) async-start(f32[256,1,1,2]{3,2,1,0:T(1,128)} %bitcast.20), calls=%async_computation.4 | async-start | bytes 262144 | tf_op jit(solution)/shard_map/all_to_all | solution.py:61
  25.4 0.7 convert_reduce_fusion
  26.1 0.1 convert_element_type.37
  26.2 12.0 %all-to-all-done.4 = f32[256,1,1,2]{3,2,1,0:T(1,128)S(1)} async-done(((f32[256,1,1,2]{3,2,1,0:T(1,128)}), f32[256,1,1,2]{3,2,1,0:T(1,128)S(1)}, u32[]{:S(2)}, u32[]{:S(2)}) %all-to-all-start.4) | async-done | bytes 2080 | tf_op jit(solution)/shard_map/all_to_all | solution.py:61
  38.2 19.6 %all_to_all.25 = f32[256,1,1,2]{3,2,1,0:T(1,128)} all-to-all(f32[256,1,1,2]{3,2,1,0:T(1,128)S(1)} %bitcast.61), channel_id=1, replica_groups=mesh['role'=4,'dom_0'=4,'dom_1'=8,'dom_2'=2] {'role','dom_0','dom_1','do..., dimensions={0} | all-to-all | bytes 4096 | tf_op jit(solution)/shard_map/all_to_all | solution.py:61
  57.8 0.7 broadcast_in_dim.12
  58.5 6.5 %all_to_all.26 = bf16[4,4,512]{2,1,0:T(4,128)(2,1)S(1)} all-to-all(bf16[4,4,512]{2,1,0:T(4,128)(2,1)S(1)} %broadcast_in_dim.12), channel_id=1, replica_groups=mesh['role'=4,'dom_0'=4,'dom_1'=8,'dom_2'=2] {'role'}, dimensions={0} | all-to-all | bytes 32768 | tf_op jit(solution)/shard_map/all_to_all | solution.py:32
  65.1 1.5 %broadcast_in_dim.13 = bf16[64,4,4,512]{3,2,1,0:T(4,128)(2,1)} broadcast(bf16[4,4,512]{2,1,0:T(4,128)(2,1)S(1)} %all_to_all.26), dimensions={1,2,3} | broadcast | bytes 1064960 | tf_op jit(solution)/shard_map/broadcast_in_dim | solution.py:33
  66.6 6.0 %all-to-all-start.1 = ((bf16[64,4,4,512]{3,2,1,0:T(4,128)(2,1)}), bf16[64,4,4,512]{3,2,1,0:T(4,128)(2,1)S(1)}, u32[]{:S(2)}, u32[]{:S(2)}) async-start(bf16[64,4,4,512]{3,2,1,0:T(4,128)(2,1)} %broadcast_in_dim.13), calls=%async_computation.1 | async-start | bytes 2097152 | tf_op jit(solution)/shard_map/all_to_all | solution.py:32
  72.6 0.0 copy-done.8
  72.7 0.0 copy-done.3
  72.7 0.6 gather_fusion
  73.3 1.7 %collective-permute-start = (bf16[16,512]{1,0:T(8,128)(2,1)S(1)}, bf16[16,512]{1,0:T(8,128)(2,1)S(1)}, u32[]{:S(2)}, u32[]{:S(2)}) collective-permute-start(bf16[16,512]{1,0:T(8,128)(2,1)S(1)} %gather_fusion), channel_id=1, source_target_pairs={{0,1},{1,2},{2,3},{3,4},{4,5},{5,6},{6,7},{7,8},{8,9},{9,10},{10,1... | collective-permute-start | bytes 49160 | tf_op jit(solution)/shard_map/ppermute | solution.py:22
  75.0 0.0 collective-permute-start.1
  75.0 0.0 copy-done.5
  75.0 11.7 %scatter_custom_fusion.2 = f32[512,512]{1,0:T(8,128)S(1)} fusion(s32[1024]{0:T(1024)S(1)} %bitcast.65, f32[]{:T(128)} %constant.9.clone.1, bf16[128,512]{1,0:T(8,128)(2,1)S(1)} %copy-done.3, s32[1024]{0:T(1024)S(1)} %broadcast_clamp_fusion.1), kind=kCustom, calls=%fused_computation.7 | custom fusion | flops 1048576 | bytes 1183748 | tf_op jit(solution)/shard_map/scatter-add | solution.py:126
  86.8 1.6 %reshape_transpose_transpose_reshape_reshape_reshape.7 = f32[256,1,1,2,512]{4,3,2,1,0:T(2,128)} reshape(f32[512,512]{1,0:T(8,128)S(1)} %scatter_custom_fusion.2) | data formatting | bytes 2097152 | tf_op jit(solution)/shard_map/reshape;transpose;transpose;reshape;reshape;reshape | solution.py:60
  88.4 13.0 %all-to-all-done.1 = bf16[64,4,4,512]{3,2,1,0:T(4,128)(2,1)S(1)} async-done(((bf16[64,4,4,512]{3,2,1,0:T(4,128)(2,1)}), bf16[64,4,4,512]{3,2,1,0:T(4,128)(2,1)S(1)}, u32[]{:S(2)}, u32[]{:S(2)}) %all-to-all-start.1) | async-done | bytes 1048608 | tf_op jit(solution)/shard_map/all_to_all | solution.py:32
  101.4 6.8 %all-to-all-start.3 = ((f32[256,1,1,2,512]{4,3,2,1,0:T(2,128)}), f32[256,1,1,2,512]{4,3,2,1,0:T(2,128)S(1)}, u32[]{:S(2)}, u32[]{:S(2)}) async-start(f32[256,1,1,2,512]{4,3,2,1,0:T(2,128)} %reshape_transpose_transpose_reshape_reshape_reshape.7), calls=%async_computation.3 | async-start | bytes 2097152 | tf_op jit(solution)/shard_map/all_to_all | solution.py:61
  108.1 0.0 copy-done.6
  108.1 7.8 %scatter_custom_fusion.1 = f32[128]{0:T(128)S(1)} fusion(s32[1024]{0:T(1024)S(1)} %bitcast.66, f32[1024]{0:T(1024)S(1)} %broadcast.143, f32[]{:T(128)} %constant.9.clone.1), kind=kCustom, calls=%fused_computation.50 | custom fusion | flops 1024 | bytes 516 | tf_op jit(solution)/shard_map/while/body/eval_jaxpr/scatter-add | solution.py:105
  116.0 0.0 copy-done.7
  116.0 0.0 copy-done
  116.0 0.0 copy-done.4
  116.0 0.2 fusion.10
  116.2 1.0 fusion.12
  117.2 0.1 reshape.256
  117.3 1.0 eq.15
  118.4 0.3 convolution_bitcast_fusion
  118.6 0.4 copy.11
  119.0 0.3 reshape_reshape.9
  119.3 0.0 collective-permute-done
  119.3 0.0 collective-permute-done.1
  119.3 0.1 pad_maximum_fusion
  119.4 0.0 copy-start.1
  119.4 12.2 %scatter_custom_fusion = f32[128,512]{1,0:T(8,128)} fusion(s32[1024]{0:T(1024)S(1)} %bitcast.67, f32[]{:T(128)} %constant.9.clone.1, bf16[1184,512]{1,0:T(8,128)(2,1)S(1)} %pad_maximum_fusion, s32[1024]{0:T(1024)S(1)} %broadcast_clamp_fusion), kind=kCustom, calls=%fused_computation.9 | custom fusion | flops 1048576 | bytes 1478660 | tf_op jit(solution)/shard_map/while/body/eval_jaxpr/scatter-add | solution.py:105
  131.6 0.0 copy-done.1
  131.6 1.4 multiply_reduce_fusion
  133.0 0.8 multiply_convert_fusion
  133.8 6.8 %all-to-all-done.3 = f32[256,1,1,2,512]{4,3,2,1,0:T(2,128)S(1)} async-done(((f32[256,1,1,2,512]{4,3,2,1,0:T(2,128)}), f32[256,1,1,2,512]{4,3,2,1,0:T(2,128)S(1)}, u32[]{:S(2)}, u32[]{:S(2)}) %all-to-all-start.3) | async-done | bytes 1048608 | tf_op jit(solution)/shard_map/all_to_all | solution.py:61
  140.6 0.7 reshape_reshape.10
  141.3 0.5 fusion.6
  141.8 0.0 copy-done.2
  141.8 0.3 multiply_reduce_fusion.1
  142.1 0.7 multiply_convert_fusion.1
  (18 shorter events, 0.1 us)
Async XLA Ops:
  9.7 28.5 %all-to-all-start.4 = ((f32[256,1,1,2]{3,2,1,0:T(1,128)}), f32[256,1,1,2]{3,2,1,0:T(1,128)S(1)}, u32[]{:S(2)}, u32[]{:S(2)}) async-start(f32[256,1,1,2]{3,2,1,0:T(1,128)} %bitcast.20), calls=%async_computation.4 | async-start | bytes 262144 | tf_op jit(solution)/shard_map/all_to_all | solution.py:61
  66.6 6.0 %copy-start.8 = (s32[1,16]{1,0:T(1,128)S(1)}, s32[1,16]{1,0:T(1,128)}, u32[]{:S(2)}) copy-start(s32[1,16]{1,0:T(1,128)} %param.14) | copy-start | bytes 196
  66.6 6.0 %copy-start.3 = (bf16[128,512]{1,0:T(8,128)(2,1)S(1)}, bf16[128,512]{1,0:T(8,128)(2,1)}, u32[]{:S(2)}) copy-start(bf16[128,512]{1,0:T(8,128)(2,1)} %param.9) | copy-start | bytes 393220
  66.6 8.4 %copy-start.5 = (s32[1,1024]{1,0:T(1,128)S(1)}, s32[1,1024]{1,0:T(1,128)}, u32[]{:S(2)}) copy-start(s32[1,1024]{1,0:T(1,128)} %param.15) | copy-start | bytes 12292
  66.6 34.7 %all-to-all-start.1 = ((bf16[64,4,4,512]{3,2,1,0:T(4,128)(2,1)}), bf16[64,4,4,512]{3,2,1,0:T(4,128)(2,1)S(1)}, u32[]{:S(2)}, u32[]{:S(2)}) async-start(bf16[64,4,4,512]{3,2,1,0:T(4,128)(2,1)} %broadcast_in_dim.13), calls=%async_computation.1 | async-start | bytes 2097152 | tf_op jit(solution)/shard_map/all_to_all | solution.py:32
  73.3 46.1 %collective-permute-start = (bf16[16,512]{1,0:T(8,128)(2,1)S(1)}, bf16[16,512]{1,0:T(8,128)(2,1)S(1)}, u32[]{:S(2)}, u32[]{:S(2)}) collective-permute-start(bf16[16,512]{1,0:T(8,128)(2,1)S(1)} %gather_fusion), channel_id=1, source_target_pairs={{0,1},{1,2},{2,3},{3,4},{4,5},{5,6},{6,7},{7,8},{8,9},{9,10},{10,1... | collective-permute-start | bytes 49160 | tf_op jit(solution)/shard_map/ppermute | solution.py:22
  75.0 44.4 %collective-permute-start.1 = (bf16[16,512]{1,0:T(8,128)(2,1)S(1)}, bf16[16,512]{1,0:T(8,128)(2,1)S(1)}, u32[]{:S(2)}, u32[]{:S(2)}) collective-permute-start(bf16[16,512]{1,0:T(8,128)(2,1)S(1)} %gather_fusion), channel_id=1, source_target_pairs={{1,0},{2,1},{3,2},{4,3},{5,4},{6,5},{7,6},{8,7},{9,8},{10,9},{11,1... | collective-permute-start | bytes 49160 | tf_op jit(solution)/shard_map/ppermute | solution.py:25
  88.4 19.7 %copy-start.6 = (s32[1,1024]{1,0:T(1,128)S(1)}, s32[1,1024]{1,0:T(1,128)}, u32[]{:S(2)}) copy-start(s32[1,1024]{1,0:T(1,128)} %param.13) | copy-start | bytes 12292
  88.4 27.6 %copy-start.7 = (s32[1,1024]{1,0:T(1,128)S(1)}, s32[1,1024]{1,0:T(1,128)}, u32[]{:S(2)}) copy-start(s32[1,1024]{1,0:T(1,128)} %param.12) | copy-start | bytes 12292
  88.4 27.6 %copy-start = (bf16[1024,512]{1,0:T(8,128)(2,1)S(1)}, bf16[1024,512]{1,0:T(8,128)(2,1)}, u32[]{:S(2)}) copy-start(bf16[1024,512]{1,0:T(8,128)(2,1)} %param.11) | copy-start | bytes 3145732
  88.4 27.6 %copy-start.4 = (bf16[4,512]{1,0:T(4,128)(2,1)S(1)}, bf16[4,512]{1,0:T(4,128)(2,1)}, u32[]{:S(2)}) copy-start(bf16[4,512]{1,0:T(4,128)(2,1)} %param.10) | copy-start | bytes 12292
  101.4 39.2 %all-to-all-start.3 = ((f32[256,1,1,2,512]{4,3,2,1,0:T(2,128)}), f32[256,1,1,2,512]{4,3,2,1,0:T(2,128)S(1)}, u32[]{:S(2)}, u32[]{:S(2)}) async-start(f32[256,1,1,2,512]{4,3,2,1,0:T(2,128)} %reshape_transpose_transpose_reshape_reshape_reshape.7), calls=%async_computation.3 | async-start | bytes 2097152 | tf_op jit(solution)/shard_map/all_to_all | solution.py:61
  119.4 12.2 %copy-start.1 = (bf16[1024,512]{1,0:T(8,128)(2,1)S(1)}, bf16[1024,512]{1,0:T(8,128)(2,1)}, u32[]{:S(2)}) copy-start(bf16[1024,512]{1,0:T(8,128)(2,1)} %param.11) | copy-start | bytes 3145732
  140.6 1.3 copy-start.2
where the time goes:
time: 143 us
  other arithmetic  42.3 us (30%)
  waiting for transfers between devices  31.7 us (22%)
  starting transfers between devices  30.1 us (21%)
  blocking collectives  26.2 us (18%)
  local copies, waits for them, and re-layouts  7.97 us (6%)
  matrix products  3.62 us (3%)
    all_to_all x2, starting transfers between devices, one_exchange(): parts = lax.all_to_all(parts, axis, split_axis=0, concat_axis=0, tiled=True)  22.4 us
    all_to_all x1, blocking collectives, one_exchange(): parts = lax.all_to_all(parts, axis, split_axis=0, concat_axis=0, tiled=True)  19.6 us
    all_to_all x2, waiting for transfers between devices, one_exchange(): parts = lax.all_to_all(parts, axis, split_axis=0, concat_axis=0, tiled=True)  18.7 us
    all_to_all x1, waiting for transfers between devices, from_everyone(): lax.all_to_all(jnp.broadcast_to(value[None], (count, *value.shape)), axis...  13 us
    scatter-add x1, other arithmetic, add_block(): node_sums.at[block_targets].add(picked)  12.2 us
    scatter-add x1, other arithmetic, on_device(): partial_value = jnp.zeros((slot_total, feature_width), jnp.float32).at[hu...  11.7 us
    scatter-add x1, other arithmetic, add_block(): node_degree.at[block_targets].add(1.0)  7.83 us
    scatter-add x1, other arithmetic, on_device(): slot_counts = jnp.zeros((slot_total,), jnp.float32).at[hub_slots].add(1.0)  7.61 us
  transfers between devices with their start and end apart: 5, of which 3 were waited for; matrix products, arithmetic and copies ran while one was open for 28% of the time, Pallas kernels for 0%

commit v1 on v0

v1 whole, which is shorter than its diff:
```python
import functools

import jax
import jax.numpy as jnp
from jax import lax
from jax.experimental import pallas as pl
from jax.experimental.pallas import tpu as pltpu
from jax.sharding import Mesh
from jax.sharding import PartitionSpec as P

INNER = ("dom_1", "dom_2")
OUTER = ("role", "dom_0")
DOM = ("dom_0", "dom_1", "dom_2")
ROLE_DOM = ("role", "dom_0", "dom_1", "dom_2")

epsilon = 1e-06
F32 = jnp.float32
BF16 = jnp.bfloat16
I32 = jnp.int32
NT = (((1,), (1,)), ((), ()))
TN = (((0,), (0,)), ((), ()))
MIB = 1 << 20


def dot(a, b):
    return jnp.dot(a, b, preferred_element_type=F32)


def onehot(rows, index, first=0):
    shape = (rows, index.shape[1])
    return jnp.where(lax.broadcasted_iota(I32, shape, 0) + first == index, 1.0, 0.0).astype(BF16)


def split_count(count):
    high = jnp.floor(count * (1.0 / 256.0))
    return count - high * 256.0, high


def normalized(linear):
    rectified = jnp.maximum(linear, 0.0)
    mean = jnp.mean(rectified * rectified, axis=1, keepdims=True)
    return (rectified * lax.rsqrt(mean + epsilon)).astype(BF16)


def export_body(bound_ref, feats_ref, out_ref):
    picks = onehot(feats_ref.shape[0], bound_ref[...])
    out_ref[...] = lax.dot_general(picks, feats_ref[...], TN, preferred_element_type=F32).astype(BF16)


def slots_body(where_ref, src_ref, slot_ref, hub_ref, feats_ref, mid_ref):
    feats = feats_ref[...]
    outer = where_ref[0]
    slot = slot_ref[...]
    picks = onehot(128, src_ref[...])

    def chunk(i, carry):
        count = lax.dot_general(
            onehot(128, slot, i * 128), picks, NT, preferred_element_type=F32
        )
        low, high = split_count(count)
        sums = dot(low.astype(BF16), feats) + dot((high * 256.0).astype(BF16), feats)
        sums = sums.astype(BF16)
        for k in range(4):
            mid_ref[i * 4 + k, 32:64, :] = sums[k * 32 : (k + 1) * 32, :]
        return carry

    lax.fori_loop(0, 4, chunk, 0)
    count = lax.dot_general(
        onehot(16, slot >> 5), onehot(512, (slot & 31) + outer * 32), NT, preferred_element_type=F32
    )
    low, high = split_count(count)
    lane = lax.broadcasted_iota(I32, (1, 512), 1)
    hubs = hub_ref[...].astype(F32)
    which = (onehot(16, lane >> 5).astype(F32) * hubs).astype(BF16)
    hub = lax.dot_general(
        which, onehot(512, (lane & 31) + outer * 32), NT, preferred_element_type=F32
    )
    row = lax.broadcasted_iota(I32, (8, 512), 0)
    for t in range(16):
        about = jnp.where(row == 0, low[t : t + 1], 0.0)
        about = jnp.where(row == 1, high[t : t + 1], about)
        about = jnp.where(row == 2, hub[t : t + 1], about)
        mid_ref[t, 64:72, :] = about.astype(BF16)


def fill_body(where_ref, rows_ref, mid_in, mid_ref, wide, block, sems):
    del mid_in
    half = where_ref[1]
    for k in range(8):
        wide[4 * k : 4 * k + 4, :] = rows_ref[half * 8 + k].astype(F32)
    block[...] = wide[...].astype(BF16)
    copies = [
        pltpu.make_async_copy(block, mid_ref.at[t, pl.ds(0, 32)], sems.at[t]) for t in range(16)
    ]
    for copy in copies:
        copy.start()
    for copy in copies:
        copy.wait()


def reduce_body(mid_ref, out_ref, table_ref):
    about = jnp.zeros((8, 512), F32)
    for t in range(16):
        about = about + mid_ref[t, 64:72, :].astype(F32)
    count = about[0:1] + 256.0 * about[1:2]
    lane = lax.broadcasted_iota(I32, (1, 512), 1)
    target = ((lane & 31) >> 1) * 4 + about[2:3].astype(I32)
    picks = onehot(64, target)
    slots = mid_ref[:, 32:64, :].reshape(512, 512)
    sums = dot(picks, slots)
    degree = jnp.sum(picks.astype(F32) * count, axis=1, keepdims=True)
    low, high = split_count(degree)
    extra_lane = lax.broadcasted_iota(I32, (64, 128), 1)
    extra = jnp.where(extra_lane == 0, low, jnp.where(extra_lane == 1, high, 0.0))
    for g in range(16):
        out_ref[g, :, 0:512] = sums[4 * g : 4 * g + 4].astype(BF16)
        out_ref[g, :, 512:640] = extra[4 * g : 4 * g + 4].astype(BF16)
    table_ref[...] = mid_ref[:, 0:32, :].reshape(512, 512)


def counts_body(
    where_ref, src_ref, dst_ref, feats_ref, hub_ref, weight_ref,
    low_ref, high_ref, degree_ref, linear_ref, hub_linear_ref,
):
    half = where_ref[1]
    src = src_ref[...]
    targets = onehot(128, dst_ref[...])
    hub = src - 160
    column = 256 + (((hub >> 5) & 1) ^ half) * 512 + (hub >> 6) * 32 + (hub & 31)
    column = jnp.where(src < 160, src, column)
    degree_ref[...] = jnp.broadcast_to(
        jnp.sum(targets.astype(F32), axis=1, keepdims=True), degree_ref.shape
    )

    def chunk(i, carry):
        count = lax.dot_general(
            targets, onehot(256, column, i * 256), NT, preferred_element_type=F32
        )
        low, high = split_count(count)
        place = pl.ds(pl.multiple_of(i * 256, 256), 256)
        low_ref[:, place] = low.astype(BF16)
        high_ref[:, place] = (high * 256.0).astype(BF16)
        return carry

    lax.fori_loop(0, 5, chunk, 0)
    linear_ref[...] = dot(feats_ref[...], weight_ref[...])
    hub_linear_ref[...] = dot(hub_ref[...], weight_ref[...])


def nodes_body(
    low_ref, high_ref, degree_ref, linear_ref, feats_ref, before_ref, after_ref,
    mine_ref, other_ref, weight_ref, out_ref,
):
    def rows(ref):
        total = dot(ref[:, 0:128], feats_ref[...])
        total = total + dot(ref[:, 128:144], before_ref[...])
        total = total + dot(ref[:, 144:160], after_ref[...])
        total = total + dot(ref[:, 256:768], mine_ref[...])
        return total + dot(ref[:, 768:1280], other_ref[...])

    mean = ((rows(low_ref) + rows(high_ref)) / degree_ref[:, 0:1]).astype(BF16)
    out_ref[...] = normalized(linear_ref[...] + dot(mean, weight_ref[...]))


def hubs_body(parts_ref, linear_ref, weight_ref, out_ref):
    total = jnp.zeros((4, 640), F32)
    for g in range(16):
        total = total + parts_ref[g].astype(F32)
    degree = total[:, 512:513] + 256.0 * total[:, 513:514]
    mean = (total[:, 0:512] / degree).astype(BF16)
    out_ref[...] = normalized(linear_ref[...] + dot(mean, weight_ref[...]))


VMEM = pl.BlockSpec(memory_space=pltpu.VMEM)
SMEM = pl.BlockSpec(memory_space=pltpu.SMEM)
ANY = pl.BlockSpec(memory_space=pl.ANY)


def call(body, name, out, specs, flops, nbytes, limit=16, **more):
    out_specs = more.pop("out_specs", jax.tree.map(lambda _: VMEM, out))
    return pl.pallas_call(
        body,
        name=name,
        out_shape=out,
        in_specs=specs,
        out_specs=out_specs,
        compiler_params=pltpu.CompilerParams(vmem_limit_bytes=limit * MIB),
        cost_estimate=pl.CostEstimate(flops=flops, bytes_accessed=nbytes, transcendentals=0),
        **more,
    )


def shape(*dims, dtype=BF16):
    return jax.ShapeDtypeStruct(dims, dtype)


def on_device(
    node_feats, hub_feats, weight, edge_src, edge_dst, bound_rows,
    hub_edge_src, hub_edge_slot, slot_hub,
):
    outer = lax.axis_index(OUTER)
    where = jnp.stack([outer, lax.axis_index("dom_2")]).astype(I32)
    gathered = lax.all_to_all(
        jnp.broadcast_to(hub_feats[None], (16, 4, 512)), INNER, 0, 0, tiled=True
    )
    exports = call(export_body, "exports", shape(16, 512), [VMEM] * 2, 2 << 20, 150000)(
        bound_rows, node_feats
    )
    count = lax.axis_size(DOM)
    forward = [(i, (i + 1) % count) for i in range(count)]
    backward = [(target, source) for source, target in forward]
    before = lax.ppermute(exports, DOM, forward)
    after = lax.ppermute(exports, DOM, backward)
    mid = call(slots_body, "slots", shape(16, 72, 512), [SMEM] + [VMEM] * 4, 1 << 30, 2 << 20)(
        where, hub_edge_src, hub_edge_slot, slot_hub, node_feats
    )
    mid = call(
        fill_body, "fill", shape(16, 72, 512), [SMEM, VMEM, ANY], 0, 1 << 20,
        out_specs=ANY,
        input_output_aliases={2: 0},
        scratch_shapes=[
            pltpu.VMEM((32, 512), F32),
            pltpu.VMEM((32, 512), BF16),
            pltpu.SemaphoreType.DMA((16,)),
        ],
    )(where, gathered, mid)
    mid = lax.all_to_all(mid, OUTER, 0, 0, tiled=True)
    low, high, degree, linear, hub_linear = call(
        counts_body, "counts",
        (
            shape(128, 1280), shape(128, 1280), shape(128, 128, dtype=F32),
            shape(128, 512, dtype=F32), shape(4, 512, dtype=F32),
        ),
        [SMEM] + [VMEM] * 5, 1 << 30, 2 << 20,
    )(where, edge_src, edge_dst, node_feats, hub_feats, weight[:512])
    parts, mine = call(
        reduce_body, "reduce", (shape(16, 4, 640), shape(512, 512)), [VMEM], 1 << 26, 2 << 20
    )(mid)
    other = lax.ppermute(mine, "dom_2", [(0, 1), (1, 0)])
    parts = lax.all_to_all(parts, INNER, 0, 0, tiled=True)
    node_out = call(nodes_body, "nodes", shape(128, 512), [VMEM] * 10, 1 << 29, 2 << 20)(
        low, high, degree, linear, node_feats, before, after, mine, other, weight[512:]
    )
    hub_out = call(hubs_body, "hubs", shape(4, 512), [VMEM] * 3, 1 << 22, 1 << 19)(
        parts, hub_linear, weight[512:]
    )
    return (node_out, hub_out)


def solution(mesh):
    finer = Mesh(mesh.devices.reshape(4, 4, 8, 2), ROLE_DOM)
    rows = P(ROLE_DOM, None)
    in_specs = (rows, rows, P(), rows, rows, rows, rows, rows, rows)
    return jax.shard_map(
        on_device, mesh=finer, in_specs=in_specs, out_specs=(rows, rows), check_vma=False
    )
```

time: 143 us -> 67.8 us (0.47)
  other arithmetic: 42.3 us -> 0.07 us
  waiting for transfers between devices: 31.7 us -> 5.85 us
  Pallas kernels: 0 us -> 10.7 us
  starting transfers between devices: 30.1 us -> 19.6 us
  matrix products: 3.62 us -> 0 us
  local copies, waits for them, and re-layouts: 7.97 us -> 5.58 us
    scatter-add x4 -> x0, other arithmetic: 39.4 us -> none  [the longest x1 12.2 us: add_block(): node_sums.at[block_targets].add(picked)]
    all_to_all x3 -> x2, waiting for transfers between devices: 31.7 us -> 5.85 us  [the longest x1 4.26 us: on_device(): parts = lax.all_to_all(parts, INNER, 0, 0, tiled=True)]
    pallas_call x0 -> x7, Pallas kernels: none -> 10.7 us  [the longest x1 3.14 us: on_device(): call(slots_body, 'slots', shape(16, 72, 512), [SMEM] + [VMEM] * 4, 1 << 3...]
    all_to_all x3 -> x2, starting transfers between devices: 28.4 us -> 17.9 us  [the longest x1 9.97 us: on_device(): lax.all_to_all(jnp.broadcast_to(hub_feats[None], (16, 4, 512)), INNER, 0,...]
    dot_general x6 -> x0, matrix products: 3.62 us -> none  [the longest x2 1.68 us: sage_update(): jnp.dot(mean_rows, weight[feature_width:], preferred_element_type=jnp.flo...]
    another operation x6 -> x0, local copies, waits for them, and re-layouts: 3.55 us -> none  [the longest x2 2.41 us: one_exchange(): parts = parts.reshape(-1, *inside)]
    unnamed x18, local copies, waits for them, and re-layouts: 0.04 us -> 2.98 us
    convert_element_type x3 -> x0, other arithmetic: 2.13 us -> none  [the longest x2 1.43 us: sage_update(): return (rectified * inverse_norm).astype(jnp.bfloat16)]
  transfers between devices with their start and end apart: 5 -> 5, of which waited for: 3 -> 2; matrix products, arithmetic and copies ran while one was open for 28% -> 2% of each run, Pallas kernels for 0% -> 10%
where the time goes in v1:
time: 67.8 us; the launch traced here: 67.4 us
  blocking collectives  24.9 us (37%)
  starting transfers between devices  19.6 us (29%)
  Pallas kernels  10.7 us (16%)
  waiting for transfers between devices  5.85 us (9%)
  local copies, waits for them, and re-layouts  5.58 us (8%)
  between operations  0.69 us (1%)
    all_to_all x1, blocking collectives, on_device(): mid = lax.all_to_all(mid, OUTER, 0, 0, tiled=True)  24.9 us
    all_to_all x1, starting transfers between devices, on_device(): lax.all_to_all(jnp.broadcast_to(hub_feats[None], (16, 4, 512)), INNER, 0,...  9.97 us
    all_to_all x1, starting transfers between devices, on_device(): parts = lax.all_to_all(parts, INNER, 0, 0, tiled=True)  7.89 us
    all_to_all x1, waiting for transfers between devices, on_device(): parts = lax.all_to_all(parts, INNER, 0, 0, tiled=True)  4.26 us
    pallas_call x1, Pallas kernels, on_device(): call(slots_body, 'slots', shape(16, 72, 512), [SMEM] + [VMEM] * 4, 1 << 3...  3.14 us
    unnamed x18, local copies, waits for them, and re-layouts  2.98 us
    pallas_call x1, Pallas kernels, on_device(): call(counts_body, 'counts', (shape(128, 1280), shape(128, 1280), shape(12...  2.59 us
    all_to_all x1, waiting for transfers between devices, on_device(): lax.all_to_all(jnp.broadcast_to(hub_feats[None], (16, 4, 512)), INNER, 0,...  1.59 us
  transfers between devices with their start and end apart: 5, of which 2 were waited for; matrix products, arithmetic and copies ran while one was open for 2% of the time, Pallas kernels for 10%

profile of v1, /device:TPU:1, one launch (start us, length us, event | category | flops | bytes accessed | tf_op | source)
XLA Modules:
  0.0 67.4 jit_solution(5518370695120206585)
XLA Ops:
  0.6 1.3 %broadcast_in_dim.2 = bf16[16,4,512]{2,1,0:T(4,128)(2,1)} broadcast(bf16[4,512]{1,0:T(4,128)(2,1)} %hub_ref.2), dimensions={1,2} | broadcast | bytes 69632 | tf_op jit(solution)/shard_map/broadcast_in_dim | solution.py:204
  2.0 10.0 %all-to-all-start = ((bf16[16,4,512]{2,1,0:T(4,128)(2,1)}), bf16[16,4,512]{2,1,0:T(4,128)(2,1)S(1)}, u32[]{:S(2)}, u32[]{:S(2)}) async-start(bf16[16,4,512]{2,1,0:T(4,128)(2,1)} %broadcast_in_dim.2), calls=%async_computation | async-start | bytes 131072 | tf_op jit(solution)/shard_map/all_to_all | solution.py:203
  11.9 0.1 pad_add_fusion.where_ref
  12.0 0.0 copy-start
  12.0 0.9 %copy-done = bf16[128,512]{1,0:T(8,128)(2,1)S(1)} copy-done((bf16[128,512]{1,0:T(8,128)(2,1)S(1)}, bf16[128,512]{1,0:T(8,128)(2,1)}, u32[]{:S(2)}) %copy-start) | copy-done | bytes 131096
  12.9 0.0 copy-start.4
  12.9 0.7 %copy-done.4 = s32[1,1024]{1,0:T(1,128)S(1)} copy-done((s32[1,1024]{1,0:T(1,128)S(1)}, s32[1,1024]{1,0:T(1,128)}, u32[]{:S(2)}) %copy-start.4) | copy-done | bytes 4120
  13.6 0.0 copy-start.5
  13.6 0.7 %copy-done.5 = s32[1,1024]{1,0:T(1,128)S(1)} copy-done((s32[1,1024]{1,0:T(1,128)S(1)}, s32[1,1024]{1,0:T(1,128)}, u32[]{:S(2)}) %copy-start.5) | copy-done | bytes 4120
  14.3 0.0 copy-start.8
  14.3 0.7 %copy-done.8 = s32[1,512]{1,0:T(1,128)S(1)} copy-done((s32[1,512]{1,0:T(1,128)S(1)}, s32[1,512]{1,0:T(1,128)}, u32[]{:S(2)}) %copy-start.8) | copy-done | bytes 2072
  15.0 3.1 %slots.1.mid_in = bf16[16,72,512]{2,1,0:T(8,128)(2,1)S(1)} custom-call(s32[2]{0:T(128)S(1)} %pad_add_fusion.where_ref, s32[1,1024]{1,0:T(1,128)S(1)} %copy-done.4, s32[1,1024]{1,0:T(1,128)S(1)} %copy-done.5, s32[1,512]{1,0:T(1,128)S(1)} %copy-done.8, bf16[128,512]{1,0:T(8,128)(2,1)S(1)} %copy-done), custom_call_target="tpu_custom_call" | custom-call | flops 1073741824 | bytes 2097152 | tf_op jit(solution)/shard_map/slots/pallas_call | solution.py:214
  18.1 1.6 %all-to-all-done.rows_ref = bf16[16,4,512]{2,1,0:T(4,128)(2,1)S(1)} async-done(((bf16[16,4,512]{2,1,0:T(4,128)(2,1)}), bf16[16,4,512]{2,1,0:T(4,128)(2,1)S(1)}, u32[]{:S(2)}, u32[]{:S(2)}) %all-to-all-start) | async-done | bytes 65568 | tf_op jit(solution)/shard_map/all_to_all | solution.py:203
  19.7 1.4 %fill.1 = bf16[16,72,512]{2,1,0:T(8,128)(2,1)S(1)} custom-call(s32[2]{0:T(128)S(1)} %pad_add_fusion.where_ref, bf16[16,4,512]{2,1,0:T(4,128)(2,1)S(1)} %all-to-all-done.rows_ref, bf16[16,72,512]{2,1,0:T(8,128)(2,1)S(1)} %slots.1.mid_in), custom_call_target="tpu_custom_call", output_to_operand_aliasing={{}: (2, {})} | custom-call | bytes 1048576 | tf_op jit(solution)/shard_map/fill/pallas_call | solution.py:217
  21.1 24.9 %all_to_all.15.mid_ref = bf16[16,72,512]{2,1,0:T(8,128)(2,1)S(1)} all-to-all(bf16[16,72,512]{2,1,0:T(8,128)(2,1)S(1)} %fill.1), channel_id=1, replica_groups=mesh['role'=4,'dom_0'=4,'dom_1'=8,'dom_2'=2] {'role','dom_0'}, dimensions={0} | all-to-all | bytes 2359296 | tf_op jit(solution)/shard_map/all_to_all | solution.py:227
  46.0 0.0 copy-start.1
  46.0 0.0 copy-start.3
  46.0 0.9 %reduce.1 = (bf16[16,4,640]{2,1,0:T(4,128)(2,1)}, bf16[512,512]{1,0:T(8,128)(2,1)S(1)}) custom-call(bf16[16,72,512]{2,1,0:T(8,128)(2,1)S(1)} %all_to_all.15.mid_ref), custom_call_target="tpu_custom_call" | custom-call | flops 67108864 | bytes 2097152 | tf_op jit(solution)/shard_map/reduce/pallas_call | solution.py:236
  46.8 0.0 copy-start.2
  46.8 0.0 copy-start.6
  46.8 0.0 copy-start.7
  46.8 1.3 %collective-permute-start.2 = (bf16[512,512]{1,0:T(8,128)(2,1)S(1)}, bf16[512,512]{1,0:T(8,128)(2,1)S(1)}, u32[]{:S(2)}, u32[]{:S(2)}) collective-permute-start(bf16[512,512]{1,0:T(8,128)(2,1)S(1)} %get-tuple-element.13.mine_ref), channel_id=1, source_target_pairs={{0,1},{1,0},{2,3},{3,2},{4,5},{5,4},{6,7},{7,6},{8,9},{9,8},{10,11... | collective-permute-start | bytes 1572872 | tf_op jit(solution)/shard_map/ppermute | solution.py:239
  48.1 0.0 copy-done.1
  48.1 0.0 copy-done.3
  48.1 0.2 exports.1
  48.3 0.1 collective-permute-start
  48.4 0.4 collective-permute-start.1
  48.8 7.9 %all-to-all-start.2 = ((bf16[16,4,640]{2,1,0:T(4,128)(2,1)}), bf16[16,4,640]{2,1,0:T(4,128)(2,1)S(1)}, u32[]{:S(2)}, u32[]{:S(2)}) async-start(bf16[16,4,640]{2,1,0:T(4,128)(2,1)} %get-tuple-element.14), calls=%async_computation.2 | async-start | bytes 163840 | tf_op jit(solution)/shard_map/all_to_all | solution.py:240
  56.7 1.3 %fusion = (bf16[512,512]{1,0:T(8,128)(2,1)S(1)}, bf16[512,512]{1,0:T(8,128)(2,1)S(1)}) fusion(bf16[1024,512]{1,0:T(8,128)(2,1)} %param.11), kind=kLoop, calls=%fused_computation.1 | loop fusion | bytes 2097152 | tf_op jit(solution)/shard_map/slice | solution.py:242
  58.0 0.0 copy-done.2
  58.0 0.0 copy-done.6
  58.0 0.0 copy-done.7
  58.0 2.6 %counts.1 = (bf16[128,1280]{1,0:T(8,128)(2,1)S(1)}, bf16[128,1280]{1,0:T(8,128)(2,1)S(1)}, f32[128,128]{1,0:T(8,128)S(1)}, f32[128,512]{1,0:T(8,128)S(1)}, f32[4,512]{1,0:T(4,128)S(1)}) custom-call(s32[2]{0:T(128)S(1)} %pad_add_fusion.where_ref, s32[1,1024]{1,0:T(1,128)S(1)} %copy-done.6, s32[1,1024]{1,0:T(1,128)S(1)} %copy-done.7, ...), custom_call_target="tpu_custom_call" | custom-call | flops 1073741824 | bytes 2097152 | tf_op jit(solution)/shard_map/counts/pallas_call | solution.py:228
  60.6 4.3 %all-to-all-done.2.parts_ref = bf16[16,4,640]{2,1,0:T(4,128)(2,1)S(1)} async-done(((bf16[16,4,640]{2,1,0:T(4,128)(2,1)}), bf16[16,4,640]{2,1,0:T(4,128)(2,1)S(1)}, u32[]{:S(2)}, u32[]{:S(2)}) %all-to-all-start.2) | async-done | bytes 81952 | tf_op jit(solution)/shard_map/all_to_all | solution.py:240
  64.8 1.0 %hubs.1 = bf16[4,512]{1,0:T(4,128)(2,1)} custom-call(bf16[16,4,640]{2,1,0:T(4,128)(2,1)S(1)} %all-to-all-done.2.parts_ref, f32[4,512]{1,0:T(4,128)S(1)} %get-tuple-element.15.linear_ref, bf16[512,512]{1,0:T(8,128)(2,1)S(1)} %get-tuple-element.16.weight_ref), custom_call_target="tpu_custom_call" | custom-call | flops 4194304 | bytes 524288 | tf_op jit(solution)/shard_map/hubs/pallas_call | solution.py:244
  65.8 0.0 collective-permute-done.before_ref
  65.8 0.0 collective-permute-done.1.after_ref
  65.8 0.0 collective-permute-done.2.other_ref
  65.8 1.5 %nodes.1 = bf16[128,512]{1,0:T(8,128)(2,1)} custom-call(bf16[128,1280]{1,0:T(8,128)(2,1)S(1)} %get-tuple-element.9.low_ref, bf16[128,1280]{1,0:T(8,128)(2,1)S(1)} %get-tuple-element.10.high_ref, f32[128,128]{1,0:T(8,128)S(1)} %get-tuple-element.11.degree_ref, f32[128,512]{1,0:T(8,128)S(1)} %get-tuple-element.12.linear_ref, bf16[128,512]{1,0:T(8,128)(2,1)S(1)} %copy-done.1, ...), custom_call_target="tpu_custom_call" | custom-call | flops 536870912 | bytes 2097152 | tf_op jit(solution)/shard_map/nodes/pallas_call | solution.py:241
Async XLA Ops:
  2.0 17.7 %all-to-all-start = ((bf16[16,4,512]{2,1,0:T(4,128)(2,1)}), bf16[16,4,512]{2,1,0:T(4,128)(2,1)S(1)}, u32[]{:S(2)}, u32[]{:S(2)}) async-start(bf16[16,4,512]{2,1,0:T(4,128)(2,1)} %broadcast_in_dim.2), calls=%async_computation | async-start | bytes 131072 | tf_op jit(solution)/shard_map/all_to_all | solution.py:203
  12.0 0.9 %copy-start = (bf16[128,512]{1,0:T(8,128)(2,1)S(1)}, bf16[128,512]{1,0:T(8,128)(2,1)}, u32[]{:S(2)}) copy-start(bf16[128,512]{1,0:T(8,128)(2,1)} %feats_ref.7) | copy-start | bytes 393220
  12.9 0.7 %copy-start.4 = (s32[1,1024]{1,0:T(1,128)S(1)}, s32[1,1024]{1,0:T(1,128)}, u32[]{:S(2)}) copy-start(s32[1,1024]{1,0:T(1,128)} %src_ref.3) | copy-start | bytes 12292
  13.6 0.7 %copy-start.5 = (s32[1,1024]{1,0:T(1,128)S(1)}, s32[1,1024]{1,0:T(1,128)}, u32[]{:S(2)}) copy-start(s32[1,1024]{1,0:T(1,128)} %slot_ref.1) | copy-start | bytes 12292
  14.3 0.7 %copy-start.8 = (s32[1,512]{1,0:T(1,128)S(1)}, s32[1,512]{1,0:T(1,128)}, u32[]{:S(2)}) copy-start(s32[1,512]{1,0:T(1,128)} %hub_ref.3) | copy-start | bytes 6148
  46.0 2.1 %copy-start.1 = (bf16[128,512]{1,0:T(8,128)(2,1)S(1)}, bf16[128,512]{1,0:T(8,128)(2,1)}, u32[]{:S(2)}) copy-start(bf16[128,512]{1,0:T(8,128)(2,1)} %feats_ref.7) | copy-start | bytes 393220
  46.0 2.1 %copy-start.3 = (s32[1,16]{1,0:T(1,128)S(1)}, s32[1,16]{1,0:T(1,128)}, u32[]{:S(2)}) copy-start(s32[1,16]{1,0:T(1,128)} %bound_ref.1) | copy-start | bytes 196
  46.8 11.1 %copy-start.2 = (bf16[4,512]{1,0:T(4,128)(2,1)S(1)}, bf16[4,512]{1,0:T(4,128)(2,1)}, u32[]{:S(2)}) copy-start(bf16[4,512]{1,0:T(4,128)(2,1)} %hub_ref.2) | copy-start | bytes 12292
  46.8 11.1 %copy-start.6 = (s32[1,1024]{1,0:T(1,128)S(1)}, s32[1,1024]{1,0:T(1,128)}, u32[]{:S(2)}) copy-start(s32[1,1024]{1,0:T(1,128)} %src_ref.2) | copy-start | bytes 12292
  46.8 11.1 %copy-start.7 = (s32[1,1024]{1,0:T(1,128)S(1)}, s32[1,1024]{1,0:T(1,128)}, u32[]{:S(2)}) copy-start(s32[1,1024]{1,0:T(1,128)} %dst_ref.1) | copy-start | bytes 12292
  46.8 19.0 %collective-permute-start.2 = (bf16[512,512]{1,0:T(8,128)(2,1)S(1)}, bf16[512,512]{1,0:T(8,128)(2,1)S(1)}, u32[]{:S(2)}, u32[]{:S(2)}) collective-permute-start(bf16[512,512]{1,0:T(8,128)(2,1)S(1)} %get-tuple-element.13.mine_ref), channel_id=1, source_target_pairs={{0,1},{1,0},{2,3},{3,2},{4,5},{5,4},{6,7},{7,6},{8,9},{9,8},{10,11... | collective-permute-start | bytes 1572872 | tf_op jit(solution)/shard_map/ppermute | solution.py:239
  48.3 17.6 %collective-permute-start = (bf16[16,512]{1,0:T(8,128)(2,1)S(1)}, bf16[16,512]{1,0:T(8,128)(2,1)S(1)}, u32[]{:S(2)}, u32[]{:S(2)}) collective-permute-start(bf16[16,512]{1,0:T(8,128)(2,1)S(1)} %exports.1), channel_id=1, source_target_pairs={{0,1},{1,2},{2,3},{3,4},{4,5},{5,6},{6,7},{7,8},{8,9},{9,10},{10,1... | collective-permute-start | bytes 49160 | tf_op jit(solution)/shard_map/ppermute | solution.py:212
  48.4 17.5 %collective-permute-start.1 = (bf16[16,512]{1,0:T(8,128)(2,1)S(1)}, bf16[16,512]{1,0:T(8,128)(2,1)S(1)}, u32[]{:S(2)}, u32[]{:S(2)}) collective-permute-start(bf16[16,512]{1,0:T(8,128)(2,1)S(1)} %exports.1), channel_id=1, source_target_pairs={{1,0},{2,1},{3,2},{4,3},{5,4},{6,5},{7,6},{8,7},{9,8},{10,9},{11,1... | collective-permute-start | bytes 49160 | tf_op jit(solution)/shard_map/ppermute | solution.py:213
  48.8 16.0 %all-to-all-start.2 = ((bf16[16,4,640]{2,1,0:T(4,128)(2,1)}), bf16[16,4,640]{2,1,0:T(4,128)(2,1)S(1)}, u32[]{:S(2)}, u32[]{:S(2)}) async-start(bf16[16,4,640]{2,1,0:T(4,128)(2,1)} %get-tuple-element.14), calls=%async_computation.2 | async-start | bytes 163840 | tf_op jit(solution)/shard_map/all_to_all | solution.py:240

commit v2 on v1

--- a/solution.py
+++ b/solution.py
@@ -1,5 +1,3 @@
-import functools
-
 import jax
 import jax.numpy as jnp
 from jax import lax
@@ -8,6 +6,7 @@
 from jax.sharding import Mesh
 from jax.sharding import PartitionSpec as P
 
+
 INNER = ("dom_1", "dom_2")
 OUTER = ("role", "dom_0")
 DOM = ("dom_0", "dom_1", "dom_2")
@@ -42,12 +41,35 @@
     return (rectified * lax.rsqrt(mean + epsilon)).astype(BF16)
 
 
+def spread_body(rows_ref, out_ref, sems):
+    copies = [
+        pltpu.make_async_copy(rows_ref, out_ref.at[k], sems.at[k]) for k in range(out_ref.shape[0])
+    ]
+    for copy in copies:
+        copy.start()
+    for copy in copies:
+        copy.wait()
+
+
 def export_body(bound_ref, feats_ref, out_ref):
     picks = onehot(feats_ref.shape[0], bound_ref[...])
     out_ref[...] = lax.dot_general(picks, feats_ref[...], TN, preferred_element_type=F32).astype(BF16)
 
 
-def slots_body(where_ref, src_ref, slot_ref, hub_ref, feats_ref, mid_ref):
+def slots_body(
+    where_ref, src_hbm, slot_hbm, hub_hbm, feats_hbm, mid_ref,
+    src_ref, slot_ref, hub_ref, feats_ref, sems,
+):
+    copies = [
+        pltpu.make_async_copy(source, target, sems.at[k])
+        for k, (source, target) in enumerate(
+            ((src_hbm, src_ref), (slot_hbm, slot_ref), (hub_hbm, hub_ref), (feats_hbm, feats_ref))
+        )
+    ]
+    for copy in copies:
+        copy.start()
+    for copy in copies:
+        copy.wait()
     feats = feats_ref[...]
     outer = where_ref[0]
     slot = slot_ref[...]
@@ -98,7 +120,7 @@
         copy.wait()
 
 
-def reduce_body(mid_ref, out_ref, table_ref):
+def reduce_body(mid_ref, out_hbm, table_ref, out_ref, sem):
     about = jnp.zeros((8, 512), F32)
     for t in range(16):
         about = about + mid_ref[t, 64:72, :].astype(F32)
@@ -115,51 +137,60 @@
     for g in range(16):
         out_ref[g, :, 0:512] = sums[4 * g : 4 * g + 4].astype(BF16)
         out_ref[g, :, 512:640] = extra[4 * g : 4 * g + 4].astype(BF16)
+    copy = pltpu.make_async_copy(out_ref, out_hbm, sem)
+    copy.start()
     table_ref[...] = mid_ref[:, 0:32, :].reshape(512, 512)
+    copy.wait()
 
 
 def counts_body(
-    where_ref, src_ref, dst_ref, feats_ref, hub_ref, weight_ref,
-    low_ref, high_ref, degree_ref, linear_ref, hub_linear_ref,
+    where_ref, src_ref, dst_ref, feats_ref, before_ref, after_ref, hub_ref, weight_ref,
+    low_ref, high_ref, degree_ref, partial_ref, hub_linear_ref,
 ):
     half = where_ref[1]
     src = src_ref[...]
     targets = onehot(128, dst_ref[...])
     hub = src - 160
-    column = 256 + (((hub >> 5) & 1) ^ half) * 512 + (hub >> 6) * 32 + (hub & 31)
-    column = jnp.where(src < 160, src, column)
+    column = (((hub >> 5) & 1) ^ half) * 512 + (hub >> 6) * 32 + (hub & 31)
+    column = jnp.where(hub < 0, -1, column)
     degree_ref[...] = jnp.broadcast_to(
         jnp.sum(targets.astype(F32), axis=1, keepdims=True), degree_ref.shape
     )
 
-    def chunk(i, carry):
+    def counted(index, first):
         count = lax.dot_general(
-            targets, onehot(256, column, i * 256), NT, preferred_element_type=F32
+            targets, onehot(256, index, first), NT, preferred_element_type=F32
         )
         low, high = split_count(count)
+        return low.astype(BF16), (high * 256.0).astype(BF16)
+
+    def chunk(i, carry):
+        low, high = counted(column, i * 256)
         place = pl.ds(pl.multiple_of(i * 256, 256), 256)
-        low_ref[:, place] = low.astype(BF16)
-        high_ref[:, place] = (high * 256.0).astype(BF16)
+        low_ref[:, place] = low
+        high_ref[:, place] = high
         return carry
 
-    lax.fori_loop(0, 5, chunk, 0)
-    linear_ref[...] = dot(feats_ref[...], weight_ref[...])
-    hub_linear_ref[...] = dot(hub_ref[...], weight_ref[...])
+    lax.fori_loop(0, 4, chunk, 0)
+    total = jnp.zeros((128, 512), F32)
+    for part in counted(src, 0):
+        total = total + dot(part[:, 0:128], feats_ref[...])
+        total = total + dot(part[:, 128:144], before_ref[...])
+        total = total + dot(part[:, 144:160], after_ref[...])
+    partial_ref[...] = total
+    hub_linear_ref[...] = dot(hub_ref[...], weight_ref[0:512])
 
 
 def nodes_body(
-    low_ref, high_ref, degree_ref, linear_ref, feats_ref, before_ref, after_ref,
-    mine_ref, other_ref, weight_ref, out_ref,
+    low_ref, high_ref, degree_ref, partial_ref, feats_ref, mine_ref, other_ref, weight_ref, out_ref
 ):
-    def rows(ref):
-        total = dot(ref[:, 0:128], feats_ref[...])
-        total = total + dot(ref[:, 128:144], before_ref[...])
-        total = total + dot(ref[:, 144:160], after_ref[...])
-        total = total + dot(ref[:, 256:768], mine_ref[...])
-        return total + dot(ref[:, 768:1280], other_ref[...])
-
-    mean = ((rows(low_ref) + rows(high_ref)) / degree_ref[:, 0:1]).astype(BF16)
-    out_ref[...] = normalized(linear_ref[...] + dot(mean, weight_ref[...]))
+    linear = dot(feats_ref[...], weight_ref[0:512])
+    total = partial_ref[...]
+    for ref in (low_ref, high_ref):
+        total = total + dot(ref[:, 0:512], mine_ref[...])
+        total = total + dot(ref[:, 512:1024], other_ref[...])
+    mean = (total / degree_ref[:, 0:1]).astype(BF16)
+    out_ref[...] = normalized(linear + dot(mean, weight_ref[512:1024]))
 
 
 def hubs_body(parts_ref, linear_ref, weight_ref, out_ref):
@@ -168,19 +199,19 @@
         total = total + parts_ref[g].astype(F32)
     degree = total[:, 512:513] + 256.0 * total[:, 513:514]
     mean = (total[:, 0:512] / degree).astype(BF16)
-    out_ref[...] = normalized(linear_ref[...] + dot(mean, weight_ref[...]))
+    out_ref[...] = normalized(linear_ref[...] + dot(mean, weight_ref[512:1024]))
 
 
 VMEM = pl.BlockSpec(memory_space=pltpu.VMEM)
 SMEM = pl.BlockSpec(memory_space=pltpu.SMEM)
 ANY = pl.BlockSpec(memory_space=pl.ANY)
-
-
-def call(body, name, out, specs, flops, nbytes, limit=16, **more):
+HBM = pl.BlockSpec(memory_space=pltpu.HBM)
+
+
+def call(body, out, specs, flops, nbytes, limit=16, **more):
     out_specs = more.pop("out_specs", jax.tree.map(lambda _: VMEM, out))
     return pl.pallas_call(
         body,
-        name=name,
         out_shape=out,
         in_specs=specs,
         out_specs=out_specs,
@@ -194,28 +225,34 @@
     return jax.ShapeDtypeStruct(dims, dtype)
 
 
+def in_hbm(*arrays):
+    return [pltpu.with_memory_space_constraint(a, pltpu.HBM) for a in arrays]
+
+
 def on_device(
     node_feats, hub_feats, weight, edge_src, edge_dst, bound_rows,
     hub_edge_src, hub_edge_slot, slot_hub,
 ):
     outer = lax.axis_index(OUTER)
     where = jnp.stack([outer, lax.axis_index("dom_2")]).astype(I32)
-    gathered = lax.all_to_all(
-        jnp.broadcast_to(hub_feats[None], (16, 4, 512)), INNER, 0, 0, tiled=True
-    )
-    exports = call(export_body, "exports", shape(16, 512), [VMEM] * 2, 2 << 20, 150000)(
-        bound_rows, node_feats
-    )
-    count = lax.axis_size(DOM)
-    forward = [(i, (i + 1) % count) for i in range(count)]
-    backward = [(target, source) for source, target in forward]
-    before = lax.ppermute(exports, DOM, forward)
-    after = lax.ppermute(exports, DOM, backward)
-    mid = call(slots_body, "slots", shape(16, 72, 512), [SMEM] + [VMEM] * 4, 1 << 30, 2 << 20)(
-        where, hub_edge_src, hub_edge_slot, slot_hub, node_feats
-    )
+    spread = call(
+        spread_body, pltpu.HBM((16, 4, 512), BF16), [HBM], 0, 70000,
+        out_specs=HBM,
+        scratch_shapes=[pltpu.SemaphoreType.DMA((16,))],
+    )(*in_hbm(hub_feats))
+    gathered = lax.all_to_all(spread, INNER, 0, 0, tiled=True)
     mid = call(
-        fill_body, "fill", shape(16, 72, 512), [SMEM, VMEM, ANY], 0, 1 << 20,
+        slots_body, shape(16, 72, 512), [SMEM] + [HBM] * 4, 1 << 30, 2 << 20,
+        scratch_shapes=[
+            pltpu.VMEM((1, 1024), I32),
+            pltpu.VMEM((1, 1024), I32),
+            pltpu.VMEM((1, 512), I32),
+            pltpu.VMEM((128, 512), BF16),
+            pltpu.SemaphoreType.DMA((4,)),
+        ],
+    )(where, *in_hbm(hub_edge_src, hub_edge_slot, slot_hub, node_feats))
+    mid = call(
+        fill_body, shape(16, 72, 512), [SMEM, VMEM, ANY], 0, 1 << 20,
         out_specs=ANY,
         input_output_aliases={2: 0},
         scratch_shapes=[
@@ -225,24 +262,33 @@
         ],
     )(where, gathered, mid)
     mid = lax.all_to_all(mid, OUTER, 0, 0, tiled=True)
-    low, high, degree, linear, hub_linear = call(
-        counts_body, "counts",
+    exports = call(export_body, shape(16, 512), [VMEM] * 2, 2 << 20, 150000)(bound_rows, node_feats)
+    count = lax.axis_size(DOM)
+    forward = [(i, (i + 1) % count) for i in range(count)]
+    backward = [(target, source) for source, target in forward]
+    before = lax.ppermute(exports, DOM, forward)
+    after = lax.ppermute(exports, DOM, backward)
+    low, high, degree, partial, hub_linear = call(
+        counts_body,
         (
-            shape(128, 1280), shape(128, 1280), shape(128, 128, dtype=F32),
+            shape(128, 1024), shape(128, 1024), shape(128, 128, dtype=F32),
             shape(128, 512, dtype=F32), shape(4, 512, dtype=F32),
         ),
-        [SMEM] + [VMEM] * 5, 1 << 30, 2 << 20,
-    )(where, edge_src, edge_dst, node_feats, hub_feats, weight[:512])
+        [SMEM] + [VMEM] * 7, 1 << 30, 2 << 20,
+    )(where, edge_src, edge_dst, node_feats, before, after, hub_feats, weight)
     parts, mine = call(
-        reduce_body, "reduce", (shape(16, 4, 640), shape(512, 512)), [VMEM], 1 << 26, 2 << 20
+        reduce_body, (pltpu.HBM((16, 4, 640), BF16), shape(512, 512)), [VMEM],
+        1 << 26, 2 << 20,
+        out_specs=(HBM, VMEM),
+        scratch_shapes=[pltpu.VMEM((16, 4, 640), BF16), pltpu.SemaphoreType.DMA],
     )(mid)
+    parts = lax.all_to_all(parts, INNER, 0, 0, tiled=True)
     other = lax.ppermute(mine, "dom_2", [(0, 1), (1, 0)])
-    parts = lax.all_to_all(parts, INNER, 0, 0, tiled=True)
-    node_out = call(nodes_body, "nodes", shape(128, 512), [VMEM] * 10, 1 << 29, 2 << 20)(
-        low, high, degree, linear, node_feats, before, after, mine, other, weight[512:]
-    )
-    hub_out = call(hubs_body, "hubs", shape(4, 512), [VMEM] * 3, 1 << 22, 1 << 19)(
-        parts, hub_linear, weight[512:]
+    node_out = call(nodes_body, shape(128, 512), [VMEM] * 8, 1 << 29, 2 << 20)(
+        low, high, degree, partial, node_feats, mine, other, weight
+    )
+    hub_out = call(hubs_body, shape(4, 512), [VMEM] * 3, 1 << 22, 1 << 19)(
+        parts, hub_linear, weight
     )
     return (node_out, hub_out)
 

time: 67.8 us -> 64.6 us (0.953)
  local copies, waits for them, and re-layouts: 5.58 us -> 0.03 us
  Pallas kernels: 10.7 us -> 15.2 us
  starting transfers between devices: 19.6 us -> 16.3 us
  waiting for transfers between devices: 5.85 us -> 7.11 us
    pallas_call x7 -> x8, Pallas kernels: 10.7 us -> 15.2 us  [the longest x1 4.15 us: on_device(): call(slots_body, shape(16, 72, 512), [SMEM] + [HBM] * 4, 1 << 30, 2 << 20...]
    all_to_all x1, starting transfers between devices: 7.89 us -> 3.4 us  [on_device(): parts = lax.all_to_all(parts, INNER, 0, 0, tiled=True)]
    all_to_all x1, waiting for transfers between devices: 4.26 us -> 0.01 us  [on_device(): parts = lax.all_to_all(parts, INNER, 0, 0, tiled=True)]
    unnamed x18 -> x12, local copies, waits for them, and re-layouts: 2.98 us -> 0.03 us
    ppermute x1, waiting for transfers between devices: 0.01 us -> 2.7 us  [on_device(): after = lax.ppermute(exports, DOM, backward)]
    all_to_all x1, waiting for transfers between devices: 1.59 us -> 3.54 us  [on_device(): gathered = lax.all_to_all(spread, INNER, 0, 0, tiled=True)]
    ppermute x1, starting transfers between devices: 0.09 us -> 1.6 us  [on_device(): before = lax.ppermute(exports, DOM, forward)]
    broadcast_in_dim x1 -> x0, local copies, waits for them, and re-layouts: 1.34 us -> none  [on_device(): jnp.broadcast_to(hub_feats[None], (16, 4, 512))]
  transfers between devices with their start and end apart: 5 -> 5, of which waited for: 2 -> 3; matrix products, arithmetic and copies ran while one was open for 2% -> 0% of each run, Pallas kernels for 10% -> 13%
where the time goes in v2:
time: 64.6 us; the launch traced here: 64.3 us
  blocking collectives  24.9 us (39%)
  starting transfers between devices  16.3 us (25%)
  Pallas kernels  15.2 us (24%)
  waiting for transfers between devices  7.11 us (11%)
  between operations  0.74 us (1%)
    all_to_all x1, blocking collectives, on_device(): mid = lax.all_to_all(mid, OUTER, 0, 0, tiled=True)  24.9 us
    all_to_all x1, starting transfers between devices, on_device(): gathered = lax.all_to_all(spread, INNER, 0, 0, tiled=True)  9.98 us
    pallas_call x1, Pallas kernels, on_device(): call(slots_body, shape(16, 72, 512), [SMEM] + [HBM] * 4, 1 << 30, 2 << 20...  4.15 us
    all_to_all x1, waiting for transfers between devices, on_device(): gathered = lax.all_to_all(spread, INNER, 0, 0, tiled=True)  3.54 us
    all_to_all x1, starting transfers between devices, on_device(): parts = lax.all_to_all(parts, INNER, 0, 0, tiled=True)  3.4 us
    pallas_call x1, Pallas kernels, on_device(): call(spread_body, pltpu.HBM((16, 4, 512), BF16), [HBM], 0, 70000, out_spe...  3.23 us
    pallas_call x1, Pallas kernels, on_device(): call(counts_body, (shape(128, 1024), shape(128, 1024), shape(128, 128, dt...  2.92 us
    ppermute x1, waiting for transfers between devices, on_device(): after = lax.ppermute(exports, DOM, backward)  2.7 us
  transfers between devices with their start and end apart: 5, of which 3 were waited for; matrix products, arithmetic and copies ran while one was open for 0% of the time, Pallas kernels for 13%

profile of v2, /device:TPU:1, one launch (start us, length us, event | category | flops | bytes accessed | tf_op | source)
XLA Modules:
  0.0 64.3 jit_solution(15860815934179799847)
XLA Ops:
  0.6 3.2 %shard_map.106 = bf16[16,4,512]{2,1,0:T(4,128)(2,1)} custom-call(bf16[4,512]{1,0:T(4,128)(2,1)} %rows_ref.1), custom_call_target="tpu_custom_call" | custom-call | bytes 70000 | tf_op jit(solution)/shard_map/pallas_call | solution.py:238
  3.9 10.0 %all-to-all-start = ((bf16[16,4,512]{2,1,0:T(4,128)(2,1)}), bf16[16,4,512]{2,1,0:T(4,128)(2,1)S(1)}, u32[]{:S(2)}, u32[]{:S(2)}) async-start(bf16[16,4,512]{2,1,0:T(4,128)(2,1)} %shard_map.106), calls=%async_computation | async-start | bytes 131072 | tf_op jit(solution)/shard_map/all_to_all | solution.py:243
  13.9 0.1 pad_add_fusion.where_ref
  13.9 4.2 %shard_map.107.mid_in = bf16[16,72,512]{2,1,0:T(8,128)(2,1)S(1)} custom-call(s32[2]{0:T(128)S(1)} %pad_add_fusion.where_ref, s32[1,1024]{1,0:T(1,128)} %src_hbm.1, s32[1,1024]{1,0:T(1,128)} %slot_hbm.1, s32[1,512]{1,0:T(1,128)} %hub_hbm.1, bf16[128,512]{1,0:T(8,128)(2,1)} %feats_ref.5), custom_call_target="tpu_custom_call" | custom-call | flops 1073741824 | bytes 2097152 | tf_op jit(solution)/shard_map/pallas_call | solution.py:244
  18.1 3.5 %all-to-all-done.rows_ref = bf16[16,4,512]{2,1,0:T(4,128)(2,1)S(1)} async-done(((bf16[16,4,512]{2,1,0:T(4,128)(2,1)}), bf16[16,4,512]{2,1,0:T(4,128)(2,1)S(1)}, u32[]{:S(2)}, u32[]{:S(2)}) %all-to-all-start) | async-done | bytes 65568 | tf_op jit(solution)/shard_map/all_to_all | solution.py:243
  21.6 1.4 %shard_map.108 = bf16[16,72,512]{2,1,0:T(8,128)(2,1)S(1)} custom-call(s32[2]{0:T(128)S(1)} %pad_add_fusion.where_ref, bf16[16,4,512]{2,1,0:T(4,128)(2,1)S(1)} %all-to-all-done.rows_ref, bf16[16,72,512]{2,1,0:T(8,128)(2,1)S(1)} %shard_map.107.mid_in), custom_call_target="tpu_custom_call", output_to_operand_aliasing={{}: (2, {})} | custom-call | bytes 1048576 | tf_op jit(solution)/shard_map/pallas_call | solution.py:254
  23.0 24.9 %all_to_all.15.mid_ref = bf16[16,72,512]{2,1,0:T(8,128)(2,1)S(1)} all-to-all(bf16[16,72,512]{2,1,0:T(8,128)(2,1)S(1)} %shard_map.108), channel_id=1, replica_groups=mesh['role'=4,'dom_0'=4,'dom_1'=8,'dom_2'=2] {'role','dom_0'}, dimensions={0} | all-to-all | bytes 2359296 | tf_op jit(solution)/shard_map/all_to_all | solution.py:264
  47.9 0.0 copy-start.1
  47.9 0.0 copy-start.3
  47.9 0.0 copy-start
  47.9 0.0 copy-start.2
  47.9 0.0 copy-start.4
  47.9 0.0 copy-start.5
  47.9 0.9 %shard_map.109 = (bf16[16,4,640]{2,1,0:T(4,128)(2,1)}, bf16[512,512]{1,0:T(8,128)(2,1)S(1)}) custom-call(bf16[16,72,512]{2,1,0:T(8,128)(2,1)S(1)} %all_to_all.15.mid_ref), custom_call_target="tpu_custom_call" | custom-call | flops 67108864 | bytes 2097152 | tf_op jit(solution)/shard_map/pallas_call | solution.py:279
  48.8 1.3 %collective-permute-start.2 = (bf16[512,512]{1,0:T(8,128)(2,1)S(1)}, bf16[512,512]{1,0:T(8,128)(2,1)S(1)}, u32[]{:S(2)}, u32[]{:S(2)}) collective-permute-start(bf16[512,512]{1,0:T(8,128)(2,1)S(1)} %get-tuple-element.13.mine_ref), channel_id=1, source_target_pairs={{0,1},{1,0},{2,3},{3,2},{4,5},{5,4},{6,7},{7,6},{8,9},{9,8},{10,11... | collective-permute-start | bytes 1572872 | tf_op jit(solution)/shard_map/ppermute | solution.py:286
  50.1 3.4 %all-to-all-start.2 = ((bf16[16,4,640]{2,1,0:T(4,128)(2,1)}), bf16[16,4,640]{2,1,0:T(4,128)(2,1)S(1)}, u32[]{:S(2)}, u32[]{:S(2)}) async-start(bf16[16,4,640]{2,1,0:T(4,128)(2,1)} %get-tuple-element.14), calls=%async_computation.2 | async-start | bytes 163840 | tf_op jit(solution)/shard_map/all_to_all | solution.py:285
  53.6 0.0 copy-done.1
  53.6 0.0 copy-done.3
  53.6 0.2 shard_map.104
  53.7 1.6 %collective-permute-start = (bf16[16,512]{1,0:T(8,128)(2,1)S(1)}, bf16[16,512]{1,0:T(8,128)(2,1)S(1)}, u32[]{:S(2)}, u32[]{:S(2)}) collective-permute-start(bf16[16,512]{1,0:T(8,128)(2,1)S(1)} %shard_map.104), channel_id=1, source_target_pairs={{0,1},{1,2},{2,3},{3,4},{4,5},{5,6},{6,7},{7,8},{8,9},{9,10},{10,1... | collective-permute-start | bytes 49160 | tf_op jit(solution)/shard_map/ppermute | solution.py:269
  55.3 0.0 collective-permute-start.1
  55.4 0.9 %collective-permute-done.before_ref = bf16[16,512]{1,0:T(8,128)(2,1)S(1)} collective-permute-done((bf16[16,512]{1,0:T(8,128)(2,1)S(1)}, bf16[16,512]{1,0:T(8,128)(2,1)S(1)}, u32[]{:S(2)}, u32[]{:S(2)}) %collective-permute-start) | collective-permute-done | bytes 16416 | tf_op jit(solution)/shard_map/ppermute | solution.py:269
  56.2 2.7 %collective-permute-done.1.after_ref = bf16[16,512]{1,0:T(8,128)(2,1)S(1)} collective-permute-done((bf16[16,512]{1,0:T(8,128)(2,1)S(1)}, bf16[16,512]{1,0:T(8,128)(2,1)S(1)}, u32[]{:S(2)}, u32[]{:S(2)}) %collective-permute-start.1) | collective-permute-done | bytes 16416 | tf_op jit(solution)/shard_map/ppermute | solution.py:270
  58.9 0.0 copy-done
  58.9 0.0 copy-done.2
  58.9 0.0 copy-done.4
  58.9 0.0 copy-done.5
  58.9 2.9 %shard_map.105 = (bf16[128,1024]{1,0:T(8,128)(2,1)S(1)}, bf16[128,1024]{1,0:T(8,128)(2,1)S(1)}, f32[128,128]{1,0:T(8,128)S(1)}, f32[128,512]{1,0:T(8,128)S(1)}, f32[4,512]{1,0:T(4,128)S(1)}) custom-call(s32[2]{0:T(128)S(1)} %pad_add_fusion.where_ref, s32[1,1024]{1,0:T(1,128)S(1)} %copy-done.4, s32[1,1024]{1,0:T(1,128)S(1)} %copy-done.5, ...), custom_call_target="tpu_custom_call" | custom-call | flops 1073741824 | bytes 2097152 | tf_op jit(solution)/shard_map/pallas_call | solution.py:271
  61.9 0.0 all-to-all-done.2.parts_ref
  61.9 1.0 %shard_map.111 = bf16[4,512]{1,0:T(4,128)(2,1)} custom-call(bf16[16,4,640]{2,1,0:T(4,128)(2,1)S(1)} %all-to-all-done.2.parts_ref, f32[4,512]{1,0:T(4,128)S(1)} %get-tuple-element.15.linear_ref, bf16[1024,512]{1,0:T(8,128)(2,1)S(1)} %copy-done), custom_call_target="tpu_custom_call" | custom-call | flops 4194304 | bytes 524288 | tf_op jit(solution)/shard_map/pallas_call | solution.py:290
  62.9 0.0 collective-permute-done.2.other_ref
  62.9 1.5 %shard_map.110 = bf16[128,512]{1,0:T(8,128)(2,1)} custom-call(bf16[128,1024]{1,0:T(8,128)(2,1)S(1)} %get-tuple-element.9.low_ref, bf16[128,1024]{1,0:T(8,128)(2,1)S(1)} %get-tuple-element.10.high_ref, f32[128,128]{1,0:T(8,128)S(1)} %get-tuple-element.11.degree_ref, f32[128,512]{1,0:T(8,128)S(1)} %get-tuple-element.12.partial_ref, ...), custom_call_target="tpu_custom_call" | custom-call | flops 536870912 | bytes 2097152 | tf_op jit(solution)/shard_map/pallas_call | solution.py:287
Async XLA Ops:
  3.9 17.8 %all-to-all-start = ((bf16[16,4,512]{2,1,0:T(4,128)(2,1)}), bf16[16,4,512]{2,1,0:T(4,128)(2,1)S(1)}, u32[]{:S(2)}, u32[]{:S(2)}) async-start(bf16[16,4,512]{2,1,0:T(4,128)(2,1)} %shard_map.106), calls=%async_computation | async-start | bytes 131072 | tf_op jit(solution)/shard_map/all_to_all | solution.py:243
  47.9 5.7 %copy-start.1 = (bf16[128,512]{1,0:T(8,128)(2,1)S(1)}, bf16[128,512]{1,0:T(8,128)(2,1)}, u32[]{:S(2)}) copy-start(bf16[128,512]{1,0:T(8,128)(2,1)} %feats_ref.5) | copy-start | bytes 393220
  47.9 5.7 %copy-start.3 = (s32[1,16]{1,0:T(1,128)S(1)}, s32[1,16]{1,0:T(1,128)}, u32[]{:S(2)}) copy-start(s32[1,16]{1,0:T(1,128)} %bound_ref.1) | copy-start | bytes 196
  47.9 11.0 %copy-start = (bf16[1024,512]{1,0:T(8,128)(2,1)S(1)}, bf16[1024,512]{1,0:T(8,128)(2,1)}, u32[]{:S(2)}) copy-start(bf16[1024,512]{1,0:T(8,128)(2,1)} %weight_ref.5) | copy-start | bytes 3145732
  47.9 11.0 %copy-start.2 = (bf16[4,512]{1,0:T(4,128)(2,1)S(1)}, bf16[4,512]{1,0:T(4,128)(2,1)}, u32[]{:S(2)}) copy-start(bf16[4,512]{1,0:T(4,128)(2,1)} %rows_ref.1) | copy-start | bytes 12292
  47.9 11.0 %copy-start.4 = (s32[1,1024]{1,0:T(1,128)S(1)}, s32[1,1024]{1,0:T(1,128)}, u32[]{:S(2)}) copy-start(s32[1,1024]{1,0:T(1,128)} %src_ref.1) | copy-start | bytes 12292
  47.9 11.0 %copy-start.5 = (s32[1,1024]{1,0:T(1,128)S(1)}, s32[1,1024]{1,0:T(1,128)}, u32[]{:S(2)}) copy-start(s32[1,1024]{1,0:T(1,128)} %dst_ref.1) | copy-start | bytes 12292
  48.8 14.1 %collective-permute-start.2 = (bf16[512,512]{1,0:T(8,128)(2,1)S(1)}, bf16[512,512]{1,0:T(8,128)(2,1)S(1)}, u32[]{:S(2)}, u32[]{:S(2)}) collective-permute-start(bf16[512,512]{1,0:T(8,128)(2,1)S(1)} %get-tuple-element.13.mine_ref), channel_id=1, source_target_pairs={{0,1},{1,0},{2,3},{3,2},{4,5},{5,4},{6,7},{7,6},{8,9},{9,8},{10,11... | collective-permute-start | bytes 1572872 | tf_op jit(solution)/shard_map/ppermute | solution.py:286
  50.1 11.7 %all-to-all-start.2 = ((bf16[16,4,640]{2,1,0:T(4,128)(2,1)}), bf16[16,4,640]{2,1,0:T(4,128)(2,1)S(1)}, u32[]{:S(2)}, u32[]{:S(2)}) async-start(bf16[16,4,640]{2,1,0:T(4,128)(2,1)} %get-tuple-element.14), calls=%async_computation.2 | async-start | bytes 163840 | tf_op jit(solution)/shard_map/all_to_all | solution.py:285
  53.7 2.5 %collective-permute-start = (bf16[16,512]{1,0:T(8,128)(2,1)S(1)}, bf16[16,512]{1,0:T(8,128)(2,1)S(1)}, u32[]{:S(2)}, u32[]{:S(2)}) collective-permute-start(bf16[16,512]{1,0:T(8,128)(2,1)S(1)} %shard_map.104), channel_id=1, source_target_pairs={{0,1},{1,2},{2,3},{3,4},{4,5},{5,6},{6,7},{7,8},{8,9},{9,10},{10,1... | collective-permute-start | bytes 49160 | tf_op jit(solution)/shard_map/ppermute | solution.py:269
  55.3 3.6 %collective-permute-start.1 = (bf16[16,512]{1,0:T(8,128)(2,1)S(1)}, bf16[16,512]{1,0:T(8,128)(2,1)S(1)}, u32[]{:S(2)}, u32[]{:S(2)}) collective-permute-start(bf16[16,512]{1,0:T(8,128)(2,1)S(1)} %shard_map.104), channel_id=1, source_target_pairs={{1,0},{2,1},{3,2},{4,3},{5,4},{6,5},{7,6},{8,7},{9,8},{10,9},{11,1... | collective-permute-start | bytes 49160 | tf_op jit(solution)/shard_map/ppermute | solution.py:270

commit v3 on v2

--- a/solution.py
+++ b/solution.py
@@ -41,23 +41,26 @@
     return (rectified * lax.rsqrt(mean + epsilon)).astype(BF16)
 
 
-def spread_body(rows_ref, out_ref, sems):
-    copies = [
-        pltpu.make_async_copy(rows_ref, out_ref.at[k], sems.at[k]) for k in range(out_ref.shape[0])
-    ]
-    for copy in copies:
-        copy.start()
-    for copy in copies:
-        copy.wait()
-
-
 def export_body(bound_ref, feats_ref, out_ref):
     picks = onehot(feats_ref.shape[0], bound_ref[...])
     out_ref[...] = lax.dot_general(picks, feats_ref[...], TN, preferred_element_type=F32).astype(BF16)
 
 
+def repeated(index):
+    shape = (128, index.shape[1])
+    row = lax.broadcasted_iota(I32, shape, 0) & 31
+    return jnp.where(row == index, 1.0, 0.0).astype(BF16)
+
+
+GATHERED, SLOTS, ABOUT, ROWS = 0, 128, 256, 264
+
+
+def block_of(first, k):
+    return pl.ds(first + 32 * k, 32)
+
+
 def slots_body(
-    where_ref, src_hbm, slot_hbm, hub_hbm, feats_hbm, mid_ref,
+    src_hbm, slot_hbm, hub_hbm, feats_hbm, mid_ref,
     src_ref, slot_ref, hub_ref, feats_ref, sems,
 ):
     copies = [
@@ -71,7 +74,6 @@
     for copy in copies:
         copy.wait()
     feats = feats_ref[...]
-    outer = where_ref[0]
     slot = slot_ref[...]
     picks = onehot(128, src_ref[...])
 
@@ -82,37 +84,39 @@
         low, high = split_count(count)
         sums = dot(low.astype(BF16), feats) + dot((high * 256.0).astype(BF16), feats)
         sums = sums.astype(BF16)
-        for k in range(4):
-            mid_ref[i * 4 + k, 32:64, :] = sums[k * 32 : (k + 1) * 32, :]
+        for t in range(4):
+            for k in range(4):
+                mid_ref[i * 4 + t, block_of(SLOTS, k), :] = sums[
+                    t * 32 : (t + 1) * 32, k * 128 : (k + 1) * 128
+                ]
         return carry
 
     lax.fori_loop(0, 4, chunk, 0)
     count = lax.dot_general(
-        onehot(16, slot >> 5), onehot(512, (slot & 31) + outer * 32), NT, preferred_element_type=F32
+        onehot(16, slot >> 5), repeated(slot & 31), NT, preferred_element_type=F32
     )
     low, high = split_count(count)
     lane = lax.broadcasted_iota(I32, (1, 512), 1)
     hubs = hub_ref[...].astype(F32)
     which = (onehot(16, lane >> 5).astype(F32) * hubs).astype(BF16)
-    hub = lax.dot_general(
-        which, onehot(512, (lane & 31) + outer * 32), NT, preferred_element_type=F32
-    )
-    row = lax.broadcasted_iota(I32, (8, 512), 0)
+    hub = lax.dot_general(which, repeated(lane & 31), NT, preferred_element_type=F32)
+    row = lax.broadcasted_iota(I32, (8, 128), 0)
     for t in range(16):
         about = jnp.where(row == 0, low[t : t + 1], 0.0)
         about = jnp.where(row == 1, high[t : t + 1], about)
         about = jnp.where(row == 2, hub[t : t + 1], about)
-        mid_ref[t, 64:72, :] = about.astype(BF16)
-
-
-def fill_body(where_ref, rows_ref, mid_in, mid_ref, wide, block, sems):
+        mid_ref[t, ABOUT:ROWS, :] = about.astype(BF16)
+
+
+def fill_body(rows_ref, mid_in, mid_ref, wide, block, sems):
     del mid_in
-    half = where_ref[1]
-    for k in range(8):
-        wide[4 * k : 4 * k + 4, :] = rows_ref[half * 8 + k].astype(F32)
-    block[...] = wide[...].astype(BF16)
+    for z in range(8):
+        wide[4 * z : 4 * z + 4, :] = rows_ref[z].astype(F32)
+    for k in range(4):
+        block[32 * k : 32 * k + 32, :] = wide[:, 128 * k : 128 * k + 128].astype(BF16)
     copies = [
-        pltpu.make_async_copy(block, mid_ref.at[t, pl.ds(0, 32)], sems.at[t]) for t in range(16)
+        pltpu.make_async_copy(block, mid_ref.at[t, pl.ds(GATHERED, 128)], sems.at[t])
+        for t in range(16)
     ]
     for copy in copies:
         copy.start()
@@ -121,15 +125,20 @@
 
 
 def reduce_body(mid_ref, out_hbm, table_ref, out_ref, sem):
-    about = jnp.zeros((8, 512), F32)
-    for t in range(16):
-        about = about + mid_ref[t, 64:72, :].astype(F32)
+    lane = lax.broadcasted_iota(I32, (8, 128), 1)
+    blocks = []
+    for k in range(4):
+        block = jnp.zeros((8, 128), F32)
+        for i in range(4):
+            block = jnp.where(lane >> 5 == i, mid_ref[4 * k + i, ABOUT:ROWS, :].astype(F32), block)
+        blocks.append(block)
+    about = jnp.concatenate(blocks, axis=1)
     count = about[0:1] + 256.0 * about[1:2]
     lane = lax.broadcasted_iota(I32, (1, 512), 1)
     target = ((lane & 31) >> 1) * 4 + about[2:3].astype(I32)
     picks = onehot(64, target)
-    slots = mid_ref[:, 32:64, :].reshape(512, 512)
-    sums = dot(picks, slots)
+    slots = [mid_ref[:, block_of(SLOTS, k), :].reshape(512, 128) for k in range(4)]
+    sums = dot(picks, jnp.concatenate(slots, axis=1))
     degree = jnp.sum(picks.astype(F32) * count, axis=1, keepdims=True)
     low, high = split_count(degree)
     extra_lane = lax.broadcasted_iota(I32, (64, 128), 1)
@@ -139,19 +148,20 @@
         out_ref[g, :, 512:640] = extra[4 * g : 4 * g + 4].astype(BF16)
     copy = pltpu.make_async_copy(out_ref, out_hbm, sem)
     copy.start()
-    table_ref[...] = mid_ref[:, 0:32, :].reshape(512, 512)
+    for k in range(4):
+        table_ref[:, 128 * k : 128 * k + 128] = mid_ref[:, block_of(GATHERED, k), :].reshape(512, 128)
     copy.wait()
 
 
 def counts_body(
     where_ref, src_ref, dst_ref, feats_ref, before_ref, after_ref, hub_ref, weight_ref,
-    low_ref, high_ref, degree_ref, partial_ref, hub_linear_ref,
+    low_ref, high_ref, degree_ref, hub_linear_ref, partial_hbm, partial_ref, sem,
 ):
-    half = where_ref[1]
+    half = where_ref[0]
     src = src_ref[...]
     targets = onehot(128, dst_ref[...])
     hub = src - 160
-    column = (((hub >> 5) & 1) ^ half) * 512 + (hub >> 6) * 32 + (hub & 31)
+    column = (((hub >> 2) & 1) ^ half) * 512 + (hub >> 6) * 32 + ((hub & 56) >> 1) + (hub & 3)
     column = jnp.where(hub < 0, -1, column)
     degree_ref[...] = jnp.broadcast_to(
         jnp.sum(targets.astype(F32), axis=1, keepdims=True), degree_ref.shape
@@ -178,17 +188,25 @@
         total = total + dot(part[:, 128:144], before_ref[...])
         total = total + dot(part[:, 144:160], after_ref[...])
     partial_ref[...] = total
+    copy = pltpu.make_async_copy(partial_ref, partial_hbm, sem)
+    copy.start()
     hub_linear_ref[...] = dot(hub_ref[...], weight_ref[0:512])
+    copy.wait()
 
 
 def nodes_body(
-    low_ref, high_ref, degree_ref, partial_ref, feats_ref, mine_ref, other_ref, weight_ref, out_ref
+    low_ref, high_ref, degree_ref, partial_hbm, feats_ref, mine_ref, other_ref, weight_ref, out_ref,
+    partial_ref, sem,
 ):
+    copy = pltpu.make_async_copy(partial_hbm, partial_ref, sem)
+    copy.start()
     linear = dot(feats_ref[...], weight_ref[0:512])
-    total = partial_ref[...]
+    total = jnp.zeros((128, 512), F32)
     for ref in (low_ref, high_ref):
         total = total + dot(ref[:, 0:512], mine_ref[...])
         total = total + dot(ref[:, 512:1024], other_ref[...])
+    copy.wait()
+    total = total + partial_ref[...]
     mean = (total / degree_ref[:, 0:1]).astype(BF16)
     out_ref[...] = normalized(linear + dot(mean, weight_ref[512:1024]))
 
@@ -233,16 +251,12 @@
     node_feats, hub_feats, weight, edge_src, edge_dst, bound_rows,
     hub_edge_src, hub_edge_slot, slot_hub,
 ):
-    outer = lax.axis_index(OUTER)
-    where = jnp.stack([outer, lax.axis_index("dom_2")]).astype(I32)
-    spread = call(
-        spread_body, pltpu.HBM((16, 4, 512), BF16), [HBM], 0, 70000,
-        out_specs=HBM,
-        scratch_shapes=[pltpu.SemaphoreType.DMA((16,))],
-    )(*in_hbm(hub_feats))
-    gathered = lax.all_to_all(spread, INNER, 0, 0, tiled=True)
+    where = lax.axis_index("dom_2").astype(I32).reshape(1)
+    gathered = lax.all_to_all(
+        jnp.broadcast_to(hub_feats[None], (8, 4, 512)), "dom_1", 0, 0, tiled=True
+    )
     mid = call(
-        slots_body, shape(16, 72, 512), [SMEM] + [HBM] * 4, 1 << 30, 2 << 20,
+        slots_body, shape(16, ROWS, 128), [HBM] * 4, 1 << 30, 2 << 20,
         scratch_shapes=[
             pltpu.VMEM((1, 1024), I32),
             pltpu.VMEM((1, 1024), I32),
@@ -250,17 +264,17 @@
             pltpu.VMEM((128, 512), BF16),
             pltpu.SemaphoreType.DMA((4,)),
         ],
-    )(where, *in_hbm(hub_edge_src, hub_edge_slot, slot_hub, node_feats))
+    )(*in_hbm(hub_edge_src, hub_edge_slot, slot_hub, node_feats))
     mid = call(
-        fill_body, shape(16, 72, 512), [SMEM, VMEM, ANY], 0, 1 << 20,
+        fill_body, shape(16, ROWS, 128), [VMEM, ANY], 0, 1 << 20,
         out_specs=ANY,
-        input_output_aliases={2: 0},
+        input_output_aliases={1: 0},
         scratch_shapes=[
             pltpu.VMEM((32, 512), F32),
-            pltpu.VMEM((32, 512), BF16),
+            pltpu.VMEM((128, 128), BF16),
             pltpu.SemaphoreType.DMA((16,)),
         ],
-    )(where, gathered, mid)
+    )(gathered, mid)
     mid = lax.all_to_all(mid, OUTER, 0, 0, tiled=True)
     exports = call(export_body, shape(16, 512), [VMEM] * 2, 2 << 20, 150000)(bound_rows, node_feats)
     count = lax.axis_size(DOM)
@@ -268,13 +282,15 @@
     backward = [(target, source) for source, target in forward]
     before = lax.ppermute(exports, DOM, forward)
     after = lax.ppermute(exports, DOM, backward)
-    low, high, degree, partial, hub_linear = call(
+    low, high, degree, hub_linear, partial = call(
         counts_body,
         (
             shape(128, 1024), shape(128, 1024), shape(128, 128, dtype=F32),
-            shape(128, 512, dtype=F32), shape(4, 512, dtype=F32),
+            shape(4, 512, dtype=F32), pltpu.HBM((128, 512), F32),
         ),
         [SMEM] + [VMEM] * 7, 1 << 30, 2 << 20,
+        out_specs=(VMEM, VMEM, VMEM, VMEM, HBM),
+        scratch_shapes=[pltpu.VMEM((128, 512), F32), pltpu.SemaphoreType.DMA],
     )(where, edge_src, edge_dst, node_feats, before, after, hub_feats, weight)
     parts, mine = call(
         reduce_body, (pltpu.HBM((16, 4, 640), BF16), shape(512, 512)), [VMEM],
@@ -284,9 +300,10 @@
     )(mid)
     parts = lax.all_to_all(parts, INNER, 0, 0, tiled=True)
     other = lax.ppermute(mine, "dom_2", [(0, 1), (1, 0)])
-    node_out = call(nodes_body, shape(128, 512), [VMEM] * 8, 1 << 29, 2 << 20)(
-        low, high, degree, partial, node_feats, mine, other, weight
-    )
+    node_out = call(
+        nodes_body, shape(128, 512), [VMEM] * 3 + [HBM] + [VMEM] * 4, 1 << 29, 2 << 20,
+        scratch_shapes=[pltpu.VMEM((128, 512), F32), pltpu.SemaphoreType.DMA],
+    )(low, high, degree, *in_hbm(partial), node_feats, mine, other, weight)
     hub_out = call(hubs_body, shape(4, 512), [VMEM] * 3, 1 << 22, 1 << 19)(
         parts, hub_linear, weight
     )

time: 64.6 us -> 62.9 us (0.974)
  the two profiles are of different devices: /device:TPU:1 before, /device:TPU:8 now
where the time goes in v3:
time: 62.9 us; the launch traced here: 62.5 us
  blocking collectives  22.5 us (36%)
  starting transfers between devices  15.3 us (24%)
  Pallas kernels  11.6 us (18%)
  waiting for transfers between devices  11.2 us (18%)
  local copies, waits for them, and re-layouts  1.34 us (2%)
  between operations  0.74 us (1%)
    all_to_all x1, blocking collectives, on_device(): mid = lax.all_to_all(mid, OUTER, 0, 0, tiled=True)  22.5 us
    all_to_all x1, starting transfers between devices, on_device(): lax.all_to_all(jnp.broadcast_to(hub_feats[None], (8, 4, 512)), 'dom_1', 0...  8.47 us
    ppermute x1, waiting for transfers between devices, on_device(): before = lax.ppermute(exports, DOM, forward)  5.04 us
    all_to_all x1, waiting for transfers between devices, on_device(): lax.all_to_all(jnp.broadcast_to(hub_feats[None], (8, 4, 512)), 'dom_1', 0...  4.69 us
    all_to_all x1, starting transfers between devices, on_device(): parts = lax.all_to_all(parts, INNER, 0, 0, tiled=True)  3.52 us
    pallas_call x1, Pallas kernels, on_device(): call(slots_body, shape(16, ROWS, 128), [HBM] * 4, 1 << 30, 2 << 20, scrat...  3.33 us
    ppermute x1, starting transfers between devices, on_device(): after = lax.ppermute(exports, DOM, backward)  3.17 us
    pallas_call x1, Pallas kernels, on_device(): call(counts_body, (shape(128, 1024), shape(128, 1024), shape(128, 128, dt...  3.1 us
  transfers between devices with their start and end apart: 5, of which 3 were waited for; matrix products, arithmetic and copies ran while one was open for 0% of the time, Pallas kernels for 12%

profile of v3, /device:TPU:8, one launch (start us, length us, event | category | flops | bytes accessed | tf_op | source)
XLA Modules:
  0.0 62.5 jit_solution(16703548046075156225)
XLA Ops:
  0.6 1.3 %broadcast_in_dim.2 = bf16[8,4,512]{2,1,0:T(4,128)(2,1)} broadcast(bf16[4,512]{1,0:T(4,128)(2,1)} %hub_ref.1), dimensions={1,2} | broadcast | bytes 36864 | tf_op jit(solution)/shard_map/broadcast_in_dim | solution.py:256
  1.9 8.5 %all-to-all-start = ((bf16[8,4,512]{2,1,0:T(4,128)(2,1)}), bf16[8,4,512]{2,1,0:T(4,128)(2,1)S(1)}, u32[]{:S(2)}, u32[]{:S(2)}) async-start(bf16[8,4,512]{2,1,0:T(4,128)(2,1)} %broadcast_in_dim.2), calls=%async_computation | async-start | bytes 65536 | tf_op jit(solution)/shard_map/all_to_all | solution.py:255
  10.4 3.3 %shard_map.106.mid_in = bf16[16,264,128]{2,1,0:T(8,128)(2,1)S(1)} custom-call(s32[1,1024]{1,0:T(1,128)} %src_hbm.1, s32[1,1024]{1,0:T(1,128)} %slot_hbm.1, s32[1,512]{1,0:T(1,128)} %hub_hbm.1, bf16[128,512]{1,0:T(8,128)(2,1)} %feats_ref.5), custom_call_target="tpu_custom_call" | custom-call | flops 1073741824 | bytes 2097152 | tf_op jit(solution)/shard_map/pallas_call | solution.py:258
  13.7 4.7 %all-to-all-done.rows_ref = bf16[8,4,512]{2,1,0:T(4,128)(2,1)S(1)} async-done(((bf16[8,4,512]{2,1,0:T(4,128)(2,1)}), bf16[8,4,512]{2,1,0:T(4,128)(2,1)S(1)}, u32[]{:S(2)}, u32[]{:S(2)}) %all-to-all-start) | async-done | bytes 32800 | tf_op jit(solution)/shard_map/all_to_all | solution.py:255
  18.4 0.9 %shard_map.107 = bf16[16,264,128]{2,1,0:T(8,128)(2,1)S(1)} custom-call(bf16[8,4,512]{2,1,0:T(4,128)(2,1)S(1)} %all-to-all-done.rows_ref, bf16[16,264,128]{2,1,0:T(8,128)(2,1)S(1)} %shard_map.106.mid_in), custom_call_target="tpu_custom_call", output_to_operand_aliasing={{}: (1, {})} | custom-call | bytes 1048576 | tf_op jit(solution)/shard_map/pallas_call | solution.py:268
  19.3 22.5 %all_to_all.15.mid_ref = bf16[16,264,128]{2,1,0:T(8,128)(2,1)S(1)} all-to-all(bf16[16,264,128]{2,1,0:T(8,128)(2,1)S(1)} %shard_map.107), channel_id=1, replica_groups=mesh['role'=4,'dom_0'=4,'dom_1'=8,'dom_2'=2] {'role','dom_0'}, dimensions={0} | all-to-all | bytes 2162688 | tf_op jit(solution)/shard_map/all_to_all | solution.py:278
  41.8 0.0 copy-start.1
  41.8 0.0 copy-start.3
  41.8 0.0 copy-start
  41.8 0.0 copy-start.2
  41.8 0.0 copy-start.4
  41.8 0.0 copy-start.5
  41.8 0.9 %shard_map.108 = (bf16[16,4,640]{2,1,0:T(4,128)(2,1)}, bf16[512,512]{1,0:T(8,128)(2,1)S(1)}) custom-call(bf16[16,264,128]{2,1,0:T(8,128)(2,1)S(1)} %all_to_all.15.mid_ref), custom_call_target="tpu_custom_call" | custom-call | flops 67108864 | bytes 2097152 | tf_op jit(solution)/shard_map/pallas_call | solution.py:295
  42.7 0.1 collective-permute-start.2
  42.8 3.5 %all-to-all-start.2 = ((bf16[16,4,640]{2,1,0:T(4,128)(2,1)}), bf16[16,4,640]{2,1,0:T(4,128)(2,1)S(1)}, u32[]{:S(2)}, u32[]{:S(2)}) async-start(bf16[16,4,640]{2,1,0:T(4,128)(2,1)} %get-tuple-element.14), calls=%async_computation.2 | async-start | bytes 163840 | tf_op jit(solution)/shard_map/all_to_all | solution.py:301
  46.3 0.0 copy-done.1
  46.3 0.0 copy-done.3
  46.3 0.2 shard_map.104
  46.5 3.2 %collective-permute-start.1 = (bf16[16,512]{1,0:T(8,128)(2,1)S(1)}, bf16[16,512]{1,0:T(8,128)(2,1)S(1)}, u32[]{:S(2)}, u32[]{:S(2)}) collective-permute-start(bf16[16,512]{1,0:T(8,128)(2,1)S(1)} %shard_map.104), channel_id=1, source_target_pairs={{1,0},{2,1},{3,2},{4,3},{5,4},{6,5},{7,6},{8,7},{9,8},{10,9},{11,1... | collective-permute-start | bytes 49160 | tf_op jit(solution)/shard_map/ppermute | solution.py:284
  49.7 0.0 collective-permute-start
  49.7 1.4 %collective-permute-done.1.after_ref = bf16[16,512]{1,0:T(8,128)(2,1)S(1)} collective-permute-done((bf16[16,512]{1,0:T(8,128)(2,1)S(1)}, bf16[16,512]{1,0:T(8,128)(2,1)S(1)}, u32[]{:S(2)}, u32[]{:S(2)}) %collective-permute-start.1) | collective-permute-done | bytes 16416 | tf_op jit(solution)/shard_map/ppermute | solution.py:284
  51.1 5.0 %collective-permute-done.before_ref = bf16[16,512]{1,0:T(8,128)(2,1)S(1)} collective-permute-done((bf16[16,512]{1,0:T(8,128)(2,1)S(1)}, bf16[16,512]{1,0:T(8,128)(2,1)S(1)}, u32[]{:S(2)}, u32[]{:S(2)}) %collective-permute-start) | collective-permute-done | bytes 16416 | tf_op jit(solution)/shard_map/ppermute | solution.py:283
  56.1 0.0 copy-done
  56.2 0.0 copy-done.2
  56.2 0.0 copy-done.4
  56.2 0.0 copy-done.5
  56.2 3.1 %shard_map.105 = (bf16[128,1024]{1,0:T(8,128)(2,1)S(1)}, bf16[128,1024]{1,0:T(8,128)(2,1)S(1)}, f32[128,128]{1,0:T(8,128)S(1)}, f32[4,512]{1,0:T(4,128)S(1)}, f32[128,512]{1,0:T(8,128)}) custom-call(s32[1]{0:T(128)} %bitcast.where_ref, s32[1,1024]{1,0:T(1,128)S(1)} %copy-done.4, s32[1,1024]{1,0:T(1,128)S(1)} %copy-done.5, bf16[128,512]{1,0:T(8,128)(2,1)S(1)} %copy-done.1, ...), custom_call_target="tpu_custom_call" | custom-call | flops 1073741824 | bytes 2097152 | tf_op jit(solution)/shard_map/pallas_call | solution.py:285
  59.3 0.0 all-to-all-done.2.parts_ref
  59.3 1.0 %shard_map.110 = bf16[4,512]{1,0:T(4,128)(2,1)} custom-call(bf16[16,4,640]{2,1,0:T(4,128)(2,1)S(1)} %all-to-all-done.2.parts_ref, f32[4,512]{1,0:T(4,128)S(1)} %get-tuple-element.15.linear_ref, bf16[1024,512]{1,0:T(8,128)(2,1)S(1)} %copy-done), custom_call_target="tpu_custom_call" | custom-call | flops 4194304 | bytes 524288 | tf_op jit(solution)/shard_map/pallas_call | solution.py:307
  60.3 0.0 collective-permute-done.2.other_ref
  60.3 2.2 %shard_map.109 = bf16[128,512]{1,0:T(8,128)(2,1)} custom-call(bf16[128,1024]{1,0:T(8,128)(2,1)S(1)} %get-tuple-element.9.low_ref, bf16[128,1024]{1,0:T(8,128)(2,1)S(1)} %get-tuple-element.10.high_ref, f32[128,128]{1,0:T(8,128)S(1)} %get-tuple-element.11.degree_ref, f32[128,512]{1,0:T(8,128)} %get-tuple-element.12.partial_hbm, ...), custom_call_target="tpu_custom_call" | custom-call | flops 536870912 | bytes 2097152 | tf_op jit(solution)/shard_map/pallas_call | solution.py:303
Async XLA Ops:
  1.9 16.5 %all-to-all-start = ((bf16[8,4,512]{2,1,0:T(4,128)(2,1)}), bf16[8,4,512]{2,1,0:T(4,128)(2,1)S(1)}, u32[]{:S(2)}, u32[]{:S(2)}) async-start(bf16[8,4,512]{2,1,0:T(4,128)(2,1)} %broadcast_in_dim.2), calls=%async_computation | async-start | bytes 65536 | tf_op jit(solution)/shard_map/all_to_all | solution.py:255
  41.8 4.5 %copy-start.1 = (bf16[128,512]{1,0:T(8,128)(2,1)S(1)}, bf16[128,512]{1,0:T(8,128)(2,1)}, u32[]{:S(2)}) copy-start(bf16[128,512]{1,0:T(8,128)(2,1)} %feats_ref.5) | copy-start | bytes 393220
  41.8 4.5 %copy-start.3 = (s32[1,16]{1,0:T(1,128)S(1)}, s32[1,16]{1,0:T(1,128)}, u32[]{:S(2)}) copy-start(s32[1,16]{1,0:T(1,128)} %bound_ref.1) | copy-start | bytes 196
  41.8 14.4 %copy-start = (bf16[1024,512]{1,0:T(8,128)(2,1)S(1)}, bf16[1024,512]{1,0:T(8,128)(2,1)}, u32[]{:S(2)}) copy-start(bf16[1024,512]{1,0:T(8,128)(2,1)} %weight_ref.5) | copy-start | bytes 3145732
  41.8 14.4 %copy-start.2 = (bf16[4,512]{1,0:T(4,128)(2,1)S(1)}, bf16[4,512]{1,0:T(4,128)(2,1)}, u32[]{:S(2)}) copy-start(bf16[4,512]{1,0:T(4,128)(2,1)} %hub_ref.1) | copy-start | bytes 12292
  41.8 14.4 %copy-start.4 = (s32[1,1024]{1,0:T(1,128)S(1)}, s32[1,1024]{1,0:T(1,128)}, u32[]{:S(2)}) copy-start(s32[1,1024]{1,0:T(1,128)} %src_ref.1) | copy-start | bytes 12292
  41.8 14.4 %copy-start.5 = (s32[1,1024]{1,0:T(1,128)S(1)}, s32[1,1024]{1,0:T(1,128)}, u32[]{:S(2)}) copy-start(s32[1,1024]{1,0:T(1,128)} %dst_ref.1) | copy-start | bytes 12292
  42.7 17.6 %collective-permute-start.2 = (bf16[512,512]{1,0:T(8,128)(2,1)S(1)}, bf16[512,512]{1,0:T(8,128)(2,1)S(1)}, u32[]{:S(2)}, u32[]{:S(2)}) collective-permute-start(bf16[512,512]{1,0:T(8,128)(2,1)S(1)} %get-tuple-element.13.mine_ref), channel_id=1, source_target_pairs={{0,1},{1,0},{2,3},{3,2},{4,5},{5,4},{6,7},{7,6},{8,9},{9,8},{10,11... | collective-permute-start | bytes 1572872 | tf_op jit(solution)/shard_map/ppermute | solution.py:302
  42.8 16.5 %all-to-all-start.2 = ((bf16[16,4,640]{2,1,0:T(4,128)(2,1)}), bf16[16,4,640]{2,1,0:T(4,128)(2,1)S(1)}, u32[]{:S(2)}, u32[]{:S(2)}) async-start(bf16[16,4,640]{2,1,0:T(4,128)(2,1)} %get-tuple-element.14), calls=%async_computation.2 | async-start | bytes 163840 | tf_op jit(solution)/shard_map/all_to_all | solution.py:301
  46.5 4.6 %collective-permute-start.1 = (bf16[16,512]{1,0:T(8,128)(2,1)S(1)}, bf16[16,512]{1,0:T(8,128)(2,1)S(1)}, u32[]{:S(2)}, u32[]{:S(2)}) collective-permute-start(bf16[16,512]{1,0:T(8,128)(2,1)S(1)} %shard_map.104), channel_id=1, source_target_pairs={{1,0},{2,1},{3,2},{4,3},{5,4},{6,5},{7,6},{8,7},{9,8},{10,9},{11,1... | collective-permute-start | bytes 49160 | tf_op jit(solution)/shard_map/ppermute | solution.py:284
  49.7 6.5 %collective-permute-start = (bf16[16,512]{1,0:T(8,128)(2,1)S(1)}, bf16[16,512]{1,0:T(8,128)(2,1)S(1)}, u32[]{:S(2)}, u32[]{:S(2)}) collective-permute-start(bf16[16,512]{1,0:T(8,128)(2,1)S(1)} %shard_map.104), channel_id=1, source_target_pairs={{0,1},{1,2},{2,3},{3,4},{4,5},{5,6},{6,7},{7,8},{8,9},{9,10},{10,1... | collective-permute-start | bytes 49160 | tf_op jit(solution)/shard_map/ppermute | solution.py:283

commit v4 on v3

--- a/solution.py
+++ b/solution.py
@@ -7,10 +7,10 @@
 from jax.sharding import PartitionSpec as P
 
 
-INNER = ("dom_1", "dom_2")
-OUTER = ("role", "dom_0")
-DOM = ("dom_0", "dom_1", "dom_2")
-ROLE_DOM = ("role", "dom_0", "dom_1", "dom_2")
+INNER = ("pair", "side", "core")
+OUTER = ("role", "x")
+DOM = ("x", "pair", "side", "core")
+ROLE_DOM = ("role", "x", "pair", "side", "core")
 
 epsilon = 1e-06
 F32 = jnp.float32
@@ -52,11 +52,12 @@
     return jnp.where(row == index, 1.0, 0.0).astype(BF16)
 
 
-GATHERED, SLOTS, ABOUT, ROWS = 0, 128, 256, 264
+GATHERED, SLOTS, ABOUT, ROWS = 0, 64, 192, 200
 
 
 def block_of(first, k):
-    return pl.ds(first + 32 * k, 32)
+    size = (SLOTS if first == GATHERED else ABOUT - SLOTS) // 4
+    return pl.ds(first + size * k, size)
 
 
 def slots_body(
@@ -110,12 +111,12 @@
 
 def fill_body(rows_ref, mid_in, mid_ref, wide, block, sems):
     del mid_in
-    for z in range(8):
+    for z in range(4):
         wide[4 * z : 4 * z + 4, :] = rows_ref[z].astype(F32)
     for k in range(4):
-        block[32 * k : 32 * k + 32, :] = wide[:, 128 * k : 128 * k + 128].astype(BF16)
+        block[16 * k : 16 * k + 16, :] = wide[:, 128 * k : 128 * k + 128].astype(BF16)
     copies = [
-        pltpu.make_async_copy(block, mid_ref.at[t, pl.ds(GATHERED, 128)], sems.at[t])
+        pltpu.make_async_copy(block, mid_ref.at[t, pl.ds(GATHERED, 64)], sems.at[t])
         for t in range(16)
     ]
     for copy in copies:
@@ -149,19 +150,21 @@
     copy = pltpu.make_async_copy(out_ref, out_hbm, sem)
     copy.start()
     for k in range(4):
-        table_ref[:, 128 * k : 128 * k + 128] = mid_ref[:, block_of(GATHERED, k), :].reshape(512, 128)
+        table_ref[:, 128 * k : 128 * k + 128] = mid_ref[:, block_of(GATHERED, k), :].reshape(256, 128)
     copy.wait()
 
 
 def counts_body(
     where_ref, src_ref, dst_ref, feats_ref, before_ref, after_ref, hub_ref, weight_ref,
-    low_ref, high_ref, degree_ref, hub_linear_ref, partial_hbm, partial_ref, sem,
+    low_ref, high_ref, degree_ref, hub_linear_ref, partial_ref,
 ):
-    half = where_ref[0]
+    core = where_ref[0]
+    side = where_ref[1]
     src = src_ref[...]
     targets = onehot(128, dst_ref[...])
     hub = src - 160
-    column = (((hub >> 2) & 1) ^ half) * 512 + (hub >> 6) * 32 + ((hub & 56) >> 1) + (hub & 3)
+    table = (((hub >> 2) & 1) ^ core) * 2 + (((hub >> 3) & 1) ^ side)
+    column = table * 256 + (hub >> 6) * 16 + ((hub >> 2) & 12) + (hub & 3)
     column = jnp.where(hub < 0, -1, column)
     degree_ref[...] = jnp.broadcast_to(
         jnp.sum(targets.astype(F32), axis=1, keepdims=True), degree_ref.shape
@@ -188,25 +191,18 @@
         total = total + dot(part[:, 128:144], before_ref[...])
         total = total + dot(part[:, 144:160], after_ref[...])
     partial_ref[...] = total
-    copy = pltpu.make_async_copy(partial_ref, partial_hbm, sem)
-    copy.start()
     hub_linear_ref[...] = dot(hub_ref[...], weight_ref[0:512])
-    copy.wait()
 
 
 def nodes_body(
-    low_ref, high_ref, degree_ref, partial_hbm, feats_ref, mine_ref, other_ref, weight_ref, out_ref,
-    partial_ref, sem,
+    low_ref, high_ref, degree_ref, partial_ref, feats_ref,
+    table_0, table_1, table_2, table_3, weight_ref, out_ref,
 ):
-    copy = pltpu.make_async_copy(partial_hbm, partial_ref, sem)
-    copy.start()
     linear = dot(feats_ref[...], weight_ref[0:512])
-    total = jnp.zeros((128, 512), F32)
-    for ref in (low_ref, high_ref):
-        total = total + dot(ref[:, 0:512], mine_ref[...])
-        total = total + dot(ref[:, 512:1024], other_ref[...])
-    copy.wait()
-    total = total + partial_ref[...]
+    total = partial_ref[...]
+    for k, table in enumerate((table_0, table_1, table_2, table_3)):
+        for ref in (low_ref, high_ref):
+            total = total + dot(ref[:, 256 * k : 256 * k + 256], table[...])
     mean = (total / degree_ref[:, 0:1]).astype(BF16)
     out_ref[...] = normalized(linear + dot(mean, weight_ref[512:1024]))
 
@@ -251,9 +247,9 @@
     node_feats, hub_feats, weight, edge_src, edge_dst, bound_rows,
     hub_edge_src, hub_edge_slot, slot_hub,
 ):
-    where = lax.axis_index("dom_2").astype(I32).reshape(1)
+    where = jnp.stack([lax.axis_index("core"), lax.axis_index("side")]).astype(I32)
     gathered = lax.all_to_all(
-        jnp.broadcast_to(hub_feats[None], (8, 4, 512)), "dom_1", 0, 0, tiled=True
+        jnp.broadcast_to(hub_feats[None], (4, 4, 512)), "pair", 0, 0, tiled=True
     )
     mid = call(
         slots_body, shape(16, ROWS, 128), [HBM] * 4, 1 << 30, 2 << 20,
@@ -270,8 +266,8 @@
         out_specs=ANY,
         input_output_aliases={1: 0},
         scratch_shapes=[
-            pltpu.VMEM((32, 512), F32),
-            pltpu.VMEM((128, 128), BF16),
+            pltpu.VMEM((16, 512), F32),
+            pltpu.VMEM((64, 128), BF16),
             pltpu.SemaphoreType.DMA((16,)),
         ],
     )(gathered, mid)
@@ -286,24 +282,24 @@
         counts_body,
         (
             shape(128, 1024), shape(128, 1024), shape(128, 128, dtype=F32),
-            shape(4, 512, dtype=F32), pltpu.HBM((128, 512), F32),
+            shape(4, 512, dtype=F32), shape(128, 512, dtype=F32),
         ),
         [SMEM] + [VMEM] * 7, 1 << 30, 2 << 20,
-        out_specs=(VMEM, VMEM, VMEM, VMEM, HBM),
-        scratch_shapes=[pltpu.VMEM((128, 512), F32), pltpu.SemaphoreType.DMA],
     )(where, edge_src, edge_dst, node_feats, before, after, hub_feats, weight)
-    parts, mine = call(
-        reduce_body, (pltpu.HBM((16, 4, 640), BF16), shape(512, 512)), [VMEM],
+    parts, table_0 = call(
+        reduce_body, (pltpu.HBM((16, 4, 640), BF16), shape(256, 512)), [VMEM],
         1 << 26, 2 << 20,
         out_specs=(HBM, VMEM),
         scratch_shapes=[pltpu.VMEM((16, 4, 640), BF16), pltpu.SemaphoreType.DMA],
     )(mid)
+    swap = [(0, 1), (1, 0)]
+    table_1 = lax.ppermute(table_0, "side", swap)
     parts = lax.all_to_all(parts, INNER, 0, 0, tiled=True)
-    other = lax.ppermute(mine, "dom_2", [(0, 1), (1, 0)])
-    node_out = call(
-        nodes_body, shape(128, 512), [VMEM] * 3 + [HBM] + [VMEM] * 4, 1 << 29, 2 << 20,
-        scratch_shapes=[pltpu.VMEM((128, 512), F32), pltpu.SemaphoreType.DMA],
-    )(low, high, degree, *in_hbm(partial), node_feats, mine, other, weight)
+    table_2 = lax.ppermute(table_0, "core", swap)
+    table_3 = lax.ppermute(table_1, "core", swap)
+    node_out = call(nodes_body, shape(128, 512), [VMEM] * 10, 1 << 29, 2 << 20)(
+        low, high, degree, partial, node_feats, table_0, table_1, table_2, table_3, weight
+    )
     hub_out = call(hubs_body, shape(4, 512), [VMEM] * 3, 1 << 22, 1 << 19)(
         parts, hub_linear, weight
     )
@@ -311,7 +307,7 @@
 
 
 def solution(mesh):
-    finer = Mesh(mesh.devices.reshape(4, 4, 8, 2), ROLE_DOM)
+    finer = Mesh(mesh.devices.reshape(4, 4, 4, 2, 2), ROLE_DOM)
     rows = P(ROLE_DOM, None)
     in_specs = (rows, rows, P(), rows, rows, rows, rows, rows, rows)
     return jax.shard_map(

time: 62.9 us -> 64.7 us (1.029)
  the two profiles are of different devices: /device:TPU:8 before, /device:TPU:1 now
where the time goes in v4:
time: 64.7 us; the launch traced here: 64.3 us
  starting transfers between devices  23.6 us (36%)
  blocking collectives  19.1 us (30%)
  Pallas kernels  10.2 us (16%)
  waiting for transfers between devices  8.7 us (13%)
  local copies, waits for them, and re-layouts  1.89 us (3%)
  between operations  0.71 us (1%)
    all_to_all x1, blocking collectives, on_device(): mid = lax.all_to_all(mid, OUTER, 0, 0, tiled=True)  19.1 us
    all_to_all x1, starting transfers between devices, on_device(): lax.all_to_all(jnp.broadcast_to(hub_feats[None], (4, 4, 512)), 'pair', 0,...  9 us
    all_to_all x1, waiting for transfers between devices, on_device(): parts = lax.all_to_all(parts, INNER, 0, 0, tiled=True)  4.51 us
    ppermute x1, starting transfers between devices, on_device(): table_3 = lax.ppermute(table_1, 'core', swap)  4.46 us
    all_to_all x1, starting transfers between devices, on_device(): parts = lax.all_to_all(parts, INNER, 0, 0, tiled=True)  4 us
    ppermute x1, starting transfers between devices, on_device(): table_2 = lax.ppermute(table_0, 'core', swap)  3.59 us
    pallas_call x1, Pallas kernels, on_device(): call(slots_body, shape(16, ROWS, 128), [HBM] * 4, 1 << 30, 2 << 20, scrat...  3.33 us
    all_to_all x1, waiting for transfers between devices, on_device(): lax.all_to_all(jnp.broadcast_to(hub_feats[None], (4, 4, 512)), 'pair', 0,...  3.29 us
  transfers between devices with their start and end apart: 7, of which 3 were waited for; matrix products, arithmetic and copies ran while one was open for 0% of the time, Pallas kernels for 12%

profile of v4, /device:TPU:1, one launch (start us, length us, event | category | flops | bytes accessed | tf_op | source)
XLA Modules:
  0.0 64.3 jit_solution(860950897985384184)
XLA Ops:
  0.6 1.3 %broadcast_in_dim.2 = bf16[4,4,512]{2,1,0:T(4,128)(2,1)} broadcast(bf16[4,512]{1,0:T(4,128)(2,1)} %hub_ref.1), dimensions={1,2} | broadcast | bytes 20480 | tf_op jit(solution)/shard_map/broadcast_in_dim | solution.py:252
  1.9 9.0 %all-to-all-start = ((bf16[4,4,512]{2,1,0:T(4,128)(2,1)}), bf16[4,4,512]{2,1,0:T(4,128)(2,1)S(1)}, u32[]{:S(2)}, u32[]{:S(2)}) async-start(bf16[4,4,512]{2,1,0:T(4,128)(2,1)} %broadcast_in_dim.2), calls=%async_computation | async-start | bytes 32768 | tf_op jit(solution)/shard_map/all_to_all | solution.py:251
  10.9 3.3 %shard_map.106.mid_in = bf16[16,200,128]{2,1,0:T(8,128)(2,1)S(1)} custom-call(s32[1,1024]{1,0:T(1,128)} %src_hbm.1, s32[1,1024]{1,0:T(1,128)} %slot_hbm.1, s32[1,512]{1,0:T(1,128)} %hub_hbm.1, bf16[128,512]{1,0:T(8,128)(2,1)} %feats_ref.5), custom_call_target="tpu_custom_call" | custom-call | flops 1073741824 | bytes 2097152 | tf_op jit(solution)/shard_map/pallas_call | solution.py:254
  14.3 3.3 %all-to-all-done.rows_ref = bf16[4,4,512]{2,1,0:T(4,128)(2,1)S(1)} async-done(((bf16[4,4,512]{2,1,0:T(4,128)(2,1)}), bf16[4,4,512]{2,1,0:T(4,128)(2,1)S(1)}, u32[]{:S(2)}, u32[]{:S(2)}) %all-to-all-start) | async-done | bytes 16416 | tf_op jit(solution)/shard_map/all_to_all | solution.py:251
  17.6 0.5 shard_map.107
  18.1 0.0 copy-start
  18.1 19.1 %all_to_all.15.mid_ref = bf16[16,200,128]{2,1,0:T(8,128)(2,1)S(1)} all-to-all(bf16[16,200,128]{2,1,0:T(8,128)(2,1)S(1)} %shard_map.107), channel_id=1, replica_groups=mesh['role'=4,'x'=4,'pair'=4,'side'=2,'core'=2] {'role','x'}, dimensions={0} | all-to-all | bytes 1638400 | tf_op jit(solution)/shard_map/all_to_all | solution.py:274
  37.2 0.0 copy-start.1
  37.2 0.9 %shard_map.108 = (bf16[16,4,640]{2,1,0:T(4,128)(2,1)}, bf16[256,512]{1,0:T(8,128)(2,1)S(1)}) custom-call(bf16[16,200,128]{2,1,0:T(8,128)(2,1)S(1)} %all_to_all.15.mid_ref), custom_call_target="tpu_custom_call" | custom-call | flops 67108864 | bytes 2097152 | tf_op jit(solution)/shard_map/pallas_call | solution.py:289
  38.0 0.0 copy-start.3
  38.0 0.8 %collective-permute-start.2 = (bf16[256,512]{1,0:T(8,128)(2,1)S(1)}, bf16[256,512]{1,0:T(8,128)(2,1)S(1)}, u32[]{:S(2)}, u32[]{:S(2)}) collective-permute-start(bf16[256,512]{1,0:T(8,128)(2,1)S(1)} %get-tuple-element.13.table_0), channel_id=1, source_target_pairs={{0,2},{2,0},{1,3},{3,1},{4,6},{6,4},{5,7},{7,5},{8,10},{10,8},{9,1... | collective-permute-start | bytes 786440 | tf_op jit(solution)/shard_map/ppermute | solution.py:296
  38.9 3.6 %collective-permute-start.3 = (bf16[256,512]{1,0:T(8,128)(2,1)S(1)}, bf16[256,512]{1,0:T(8,128)(2,1)S(1)}, u32[]{:S(2)}, u32[]{:S(2)}) collective-permute-start(bf16[256,512]{1,0:T(8,128)(2,1)S(1)} %get-tuple-element.13.table_0), channel_id=1, source_target_pairs={{0,1},{1,0},{2,3},{3,2},{4,5},{5,4},{6,7},{7,6},{8,9},{9,8},{10,11... | collective-permute-start | bytes 786440 | tf_op jit(solution)/shard_map/ppermute | solution.py:298
  42.5 0.9 %collective-permute-done.2.table_1 = bf16[256,512]{1,0:T(8,128)(2,1)S(1)} collective-permute-done((bf16[256,512]{1,0:T(8,128)(2,1)S(1)}, bf16[256,512]{1,0:T(8,128)(2,1)S(1)}, u32[]{:S(2)}, u32[]{:S(2)}) %collective-permute-start.2) | collective-permute-done | bytes 262176 | tf_op jit(solution)/shard_map/ppermute | solution.py:296
  43.3 4.5 %collective-permute-start.4 = (bf16[256,512]{1,0:T(8,128)(2,1)S(1)}, bf16[256,512]{1,0:T(8,128)(2,1)S(1)}, u32[]{:S(2)}, u32[]{:S(2)}) collective-permute-start(bf16[256,512]{1,0:T(8,128)(2,1)S(1)} %collective-permute-done.2.table_1), channel_id=1, source_target_pairs={{0,1},{1,0},{2,3},{3,2},{4,5},{5,4},{6,7},{7,6},{8,9},{9,8},{10,11... | collective-permute-start | bytes 786440 | tf_op jit(solution)/shard_map/ppermute | solution.py:299
  47.8 0.0 copy-done.1
  47.8 0.0 copy-done.3
  47.8 0.2 shard_map.104
  48.0 0.0 collective-permute-start.1
  48.0 1.7 %collective-permute-start = (bf16[16,512]{1,0:T(8,128)(2,1)S(1)}, bf16[16,512]{1,0:T(8,128)(2,1)S(1)}, u32[]{:S(2)}, u32[]{:S(2)}) collective-permute-start(bf16[16,512]{1,0:T(8,128)(2,1)S(1)} %shard_map.104), channel_id=1, source_target_pairs={{0,1},{1,2},{2,3},{3,4},{4,5},{5,6},{6,7},{7,8},{8,9},{9,10},{10,1... | collective-permute-start | bytes 49160 | tf_op jit(solution)/shard_map/ppermute | solution.py:279
  49.7 0.0 copy-start.4
  49.7 0.0 copy-start.5
  49.7 4.0 %all-to-all-start.2 = ((bf16[16,4,640]{2,1,0:T(4,128)(2,1)}), bf16[16,4,640]{2,1,0:T(4,128)(2,1)S(1)}, u32[]{:S(2)}, u32[]{:S(2)}) async-start(bf16[16,4,640]{2,1,0:T(4,128)(2,1)} %get-tuple-element.14), calls=%async_computation.2 | async-start | bytes 163840 | tf_op jit(solution)/shard_map/all_to_all | solution.py:297
  53.7 0.0 copy-start.2
  53.8 0.1 pad_add_fusion.where_ref
  53.8 0.0 collective-permute-done.1.after_ref
  53.8 0.0 collective-permute-done.before_ref
  53.8 0.0 copy-done
  53.8 0.0 copy-done.4
  53.9 0.0 copy-done.5
  53.9 0.6 copy-done.2
  54.4 2.9 %shard_map.105 = (bf16[128,1024]{1,0:T(8,128)(2,1)S(1)}, bf16[128,1024]{1,0:T(8,128)(2,1)S(1)}, f32[128,128]{1,0:T(8,128)S(1)}, f32[4,512]{1,0:T(4,128)S(1)}, f32[128,512]{1,0:T(8,128)S(1)}) custom-call(s32[2]{0:T(128)S(1)} %pad_add_fusion.where_ref, s32[1,1024]{1,0:T(1,128)S(1)} %copy-done.4, s32[1,1024]{1,0:T(1,128)S(1)} %copy-done.5, ...), custom_call_target="tpu_custom_call" | custom-call | flops 1073741824 | bytes 2097152 | tf_op jit(solution)/shard_map/pallas_call | solution.py:281
  57.4 4.5 %all-to-all-done.2.parts_ref = bf16[16,4,640]{2,1,0:T(4,128)(2,1)S(1)} async-done(((bf16[16,4,640]{2,1,0:T(4,128)(2,1)}), bf16[16,4,640]{2,1,0:T(4,128)(2,1)S(1)}, u32[]{:S(2)}, u32[]{:S(2)}) %all-to-all-start.2) | async-done | bytes 81952 | tf_op jit(solution)/shard_map/all_to_all | solution.py:297
  61.9 1.0 %shard_map.110 = bf16[4,512]{1,0:T(4,128)(2,1)} custom-call(bf16[16,4,640]{2,1,0:T(4,128)(2,1)S(1)} %all-to-all-done.2.parts_ref, f32[4,512]{1,0:T(4,128)S(1)} %get-tuple-element.15.linear_ref, bf16[1024,512]{1,0:T(8,128)(2,1)S(1)} %copy-done), custom_call_target="tpu_custom_call" | custom-call | flops 4194304 | bytes 524288 | tf_op jit(solution)/shard_map/pallas_call | solution.py:303
  62.9 0.0 collective-permute-done.3.table_2
  62.9 0.0 collective-permute-done.4.table_3
  62.9 1.5 %shard_map.109 = bf16[128,512]{1,0:T(8,128)(2,1)} custom-call(bf16[128,1024]{1,0:T(8,128)(2,1)S(1)} %get-tuple-element.9.low_ref, bf16[128,1024]{1,0:T(8,128)(2,1)S(1)} %get-tuple-element.10.high_ref, f32[128,128]{1,0:T(8,128)S(1)} %get-tuple-element.11.degree_ref, f32[128,512]{1,0:T(8,128)S(1)} %get-tuple-element.12.partial_ref, ...), custom_call_target="tpu_custom_call" | custom-call | flops 536870912 | bytes 2097152 | tf_op jit(solution)/shard_map/pallas_call | solution.py:300
Async XLA Ops:
  1.9 15.6 %all-to-all-start = ((bf16[4,4,512]{2,1,0:T(4,128)(2,1)}), bf16[4,4,512]{2,1,0:T(4,128)(2,1)S(1)}, u32[]{:S(2)}, u32[]{:S(2)}) async-start(bf16[4,4,512]{2,1,0:T(4,128)(2,1)} %broadcast_in_dim.2), calls=%async_computation | async-start | bytes 32768 | tf_op jit(solution)/shard_map/all_to_all | solution.py:251
  18.1 35.8 %copy-start = (bf16[1024,512]{1,0:T(8,128)(2,1)S(1)}, bf16[1024,512]{1,0:T(8,128)(2,1)}, u32[]{:S(2)}) copy-start(bf16[1024,512]{1,0:T(8,128)(2,1)} %weight_ref.5) | copy-start | bytes 3145732
  37.2 10.7 %copy-start.1 = (bf16[128,512]{1,0:T(8,128)(2,1)S(1)}, bf16[128,512]{1,0:T(8,128)(2,1)}, u32[]{:S(2)}) copy-start(bf16[128,512]{1,0:T(8,128)(2,1)} %feats_ref.5) | copy-start | bytes 393220
  38.0 9.8 %copy-start.3 = (s32[1,16]{1,0:T(1,128)S(1)}, s32[1,16]{1,0:T(1,128)}, u32[]{:S(2)}) copy-start(s32[1,16]{1,0:T(1,128)} %bound_ref.1) | copy-start | bytes 196
  38.0 5.3 %collective-permute-start.2 = (bf16[256,512]{1,0:T(8,128)(2,1)S(1)}, bf16[256,512]{1,0:T(8,128)(2,1)S(1)}, u32[]{:S(2)}, u32[]{:S(2)}) collective-permute-start(bf16[256,512]{1,0:T(8,128)(2,1)S(1)} %get-tuple-element.13.table_0), channel_id=1, source_target_pairs={{0,2},{2,0},{1,3},{3,1},{4,6},{6,4},{5,7},{7,5},{8,10},{10,8},{9,1... | collective-permute-start | bytes 786440 | tf_op jit(solution)/shard_map/ppermute | solution.py:296
  38.9 24.0 %collective-permute-start.3 = (bf16[256,512]{1,0:T(8,128)(2,1)S(1)}, bf16[256,512]{1,0:T(8,128)(2,1)S(1)}, u32[]{:S(2)}, u32[]{:S(2)}) collective-permute-start(bf16[256,512]{1,0:T(8,128)(2,1)S(1)} %get-tuple-element.13.table_0), channel_id=1, source_target_pairs={{0,1},{1,0},{2,3},{3,2},{4,5},{5,4},{6,7},{7,6},{8,9},{9,8},{10,11... | collective-permute-start | bytes 786440 | tf_op jit(solution)/shard_map/ppermute | solution.py:298
  43.3 19.5 %collective-permute-start.4 = (bf16[256,512]{1,0:T(8,128)(2,1)S(1)}, bf16[256,512]{1,0:T(8,128)(2,1)S(1)}, u32[]{:S(2)}, u32[]{:S(2)}) collective-permute-start(bf16[256,512]{1,0:T(8,128)(2,1)S(1)} %collective-permute-done.2.table_1), channel_id=1, source_target_pairs={{0,1},{1,0},{2,3},{3,2},{4,5},{5,4},{6,7},{7,6},{8,9},{9,8},{10,11... | collective-permute-start | bytes 786440 | tf_op jit(solution)/shard_map/ppermute | solution.py:299
  48.0 5.8 %collective-permute-start.1 = (bf16[16,512]{1,0:T(8,128)(2,1)S(1)}, bf16[16,512]{1,0:T(8,128)(2,1)S(1)}, u32[]{:S(2)}, u32[]{:S(2)}) collective-permute-start(bf16[16,512]{1,0:T(8,128)(2,1)S(1)} %shard_map.104), channel_id=1, source_target_pairs={{1,0},{2,1},{3,2},{4,3},{5,4},{6,5},{7,6},{8,7},{9,8},{10,9},{11,1... | collective-permute-start | bytes 49160 | tf_op jit(solution)/shard_map/ppermute | solution.py:280
  48.0 5.8 %collective-permute-start = (bf16[16,512]{1,0:T(8,128)(2,1)S(1)}, bf16[16,512]{1,0:T(8,128)(2,1)S(1)}, u32[]{:S(2)}, u32[]{:S(2)}) collective-permute-start(bf16[16,512]{1,0:T(8,128)(2,1)S(1)} %shard_map.104), channel_id=1, source_target_pairs={{0,1},{1,2},{2,3},{3,4},{4,5},{5,6},{6,7},{7,8},{8,9},{9,10},{10,1... | collective-permute-start | bytes 49160 | tf_op jit(solution)/shard_map/ppermute | solution.py:279
  49.7 4.1 %copy-start.4 = (s32[1,1024]{1,0:T(1,128)S(1)}, s32[1,1024]{1,0:T(1,128)}, u32[]{:S(2)}) copy-start(s32[1,1024]{1,0:T(1,128)} %src_ref.1) | copy-start | bytes 12292
  49.7 4.1 %copy-start.5 = (s32[1,1024]{1,0:T(1,128)S(1)}, s32[1,1024]{1,0:T(1,128)}, u32[]{:S(2)}) copy-start(s32[1,1024]{1,0:T(1,128)} %dst_ref.1) | copy-start | bytes 12292
  49.7 12.1 %all-to-all-start.2 = ((bf16[16,4,640]{2,1,0:T(4,128)(2,1)}), bf16[16,4,640]{2,1,0:T(4,128)(2,1)S(1)}, u32[]{:S(2)}, u32[]{:S(2)}) async-start(bf16[16,4,640]{2,1,0:T(4,128)(2,1)} %get-tuple-element.14), calls=%async_computation.2 | async-start | bytes 163840 | tf_op jit(solution)/shard_map/all_to_all | solution.py:297
  53.7 0.7 %copy-start.2 = (bf16[4,512]{1,0:T(4,128)(2,1)S(1)}, bf16[4,512]{1,0:T(4,128)(2,1)}, u32[]{:S(2)}) copy-start(bf16[4,512]{1,0:T(4,128)(2,1)} %hub_ref.1) | copy-start | bytes 12292

commit v5 on v4

--- a/solution.py
+++ b/solution.py
@@ -61,8 +61,8 @@
 
 
 def slots_body(
-    src_hbm, slot_hbm, hub_hbm, feats_hbm, mid_ref,
-    src_ref, slot_ref, hub_ref, feats_ref, sems,
+    src_hbm, slot_hbm, hub_hbm, feats_hbm, mid_hbm,
+    src_ref, slot_ref, hub_ref, feats_ref, sems, mid_ref, out_sems,
 ):
     copies = [
         pltpu.make_async_copy(source, target, sems.at[k])
@@ -77,22 +77,6 @@
     feats = feats_ref[...]
     slot = slot_ref[...]
     picks = onehot(128, src_ref[...])
-
-    def chunk(i, carry):
-        count = lax.dot_general(
-            onehot(128, slot, i * 128), picks, NT, preferred_element_type=F32
-        )
-        low, high = split_count(count)
-        sums = dot(low.astype(BF16), feats) + dot((high * 256.0).astype(BF16), feats)
-        sums = sums.astype(BF16)
-        for t in range(4):
-            for k in range(4):
-                mid_ref[i * 4 + t, block_of(SLOTS, k), :] = sums[
-                    t * 32 : (t + 1) * 32, k * 128 : (k + 1) * 128
-                ]
-        return carry
-
-    lax.fori_loop(0, 4, chunk, 0)
     count = lax.dot_general(
         onehot(16, slot >> 5), repeated(slot & 31), NT, preferred_element_type=F32
     )
@@ -106,13 +90,36 @@
         about = jnp.where(row == 0, low[t : t + 1], 0.0)
         about = jnp.where(row == 1, high[t : t + 1], about)
         about = jnp.where(row == 2, hub[t : t + 1], about)
-        mid_ref[t, ABOUT:ROWS, :] = about.astype(BF16)
-
-
-def fill_body(rows_ref, mid_in, mid_ref, wide, block, sems):
+        mid_ref[t, ABOUT - SLOTS : ROWS - SLOTS, :] = about.astype(BF16)
+    copies = []
+    for i in range(4):
+        count = lax.dot_general(
+            onehot(128, slot, i * 128), picks, NT, preferred_element_type=F32
+        )
+        low, high = split_count(count)
+        sums = dot(low.astype(BF16), feats) + dot((high * 256.0).astype(BF16), feats)
+        sums = sums.astype(BF16)
+        for t in range(4):
+            for k in range(4):
+                mid_ref[i * 4 + t, 32 * k : 32 * k + 32, :] = sums[
+                    t * 32 : (t + 1) * 32, k * 128 : (k + 1) * 128
+                ]
+        copies.append(
+            pltpu.make_async_copy(
+                mid_ref.at[pl.ds(4 * i, 4)],
+                mid_hbm.at[pl.ds(4 * i, 4), pl.ds(SLOTS, ROWS - SLOTS)],
+                out_sems.at[i],
+            )
+        )
+        copies[-1].start()
+    for copy in copies:
+        copy.wait()
+
+
+def fill_body(rows_0, rows_1, rows_2, rows_3, mid_in, mid_ref, wide, block, sems):
     del mid_in
-    for z in range(4):
-        wide[4 * z : 4 * z + 4, :] = rows_ref[z].astype(F32)
+    for k, rows in enumerate((rows_0, rows_1, rows_2, rows_3)):
+        wide[4 * k : 4 * k + 4, :] = rows[...].astype(F32)
     for k in range(4):
         block[16 * k : 16 * k + 16, :] = wide[:, 128 * k : 128 * k + 128].astype(BF16)
     copies = [
@@ -155,16 +162,17 @@
 
 
 def counts_body(
-    where_ref, src_ref, dst_ref, feats_ref, before_ref, after_ref, hub_ref, weight_ref,
+    where_ref, src_ref, dst_ref, feats_ref, hub_ref, weight_ref,
     low_ref, high_ref, degree_ref, hub_linear_ref, partial_ref,
 ):
     core = where_ref[0]
     side = where_ref[1]
+    pair = where_ref[2]
     src = src_ref[...]
     targets = onehot(128, dst_ref[...])
     hub = src - 160
     table = (((hub >> 2) & 1) ^ core) * 2 + (((hub >> 3) & 1) ^ side)
-    column = table * 256 + (hub >> 6) * 16 + ((hub >> 2) & 12) + (hub & 3)
+    column = table * 256 + (hub >> 6) * 16 + (((hub >> 4) - pair) & 3) * 4 + (hub & 3)
     column = jnp.where(hub < 0, -1, column)
     degree_ref[...] = jnp.broadcast_to(
         jnp.sum(targets.astype(F32), axis=1, keepdims=True), degree_ref.shape
@@ -186,25 +194,34 @@
 
     lax.fori_loop(0, 4, chunk, 0)
     total = jnp.zeros((128, 512), F32)
-    for part in counted(src, 0):
+    for part, ref in zip(counted(src, 0), (low_ref, high_ref)):
         total = total + dot(part[:, 0:128], feats_ref[...])
-        total = total + dot(part[:, 128:144], before_ref[...])
-        total = total + dot(part[:, 144:160], after_ref[...])
+        ref[:, 1024:1152] = part[:, 128:256]
     partial_ref[...] = total
     hub_linear_ref[...] = dot(hub_ref[...], weight_ref[0:512])
 
 
 def nodes_body(
-    low_ref, high_ref, degree_ref, partial_ref, feats_ref,
-    table_0, table_1, table_2, table_3, weight_ref, out_ref,
-):
-    linear = dot(feats_ref[...], weight_ref[0:512])
+    low_ref, high_ref, partial_ref, feats_ref, before_ref, after_ref, table_0, table_1, weight_ref,
+    total_ref, linear_ref,
+):
+    linear_ref[...] = dot(feats_ref[...], weight_ref[0:512])
     total = partial_ref[...]
-    for k, table in enumerate((table_0, table_1, table_2, table_3)):
-        for ref in (low_ref, high_ref):
-            total = total + dot(ref[:, 256 * k : 256 * k + 256], table[...])
+    for ref in (low_ref, high_ref):
+        total = total + dot(ref[:, 1024:1040], before_ref[...])
+        total = total + dot(ref[:, 1040:1056], after_ref[...])
+        total = total + dot(ref[:, 0:256], table_0[...]) + dot(ref[:, 256:512], table_1[...])
+    total_ref[...] = total
+
+
+def finish_body(
+    low_ref, high_ref, degree_ref, total_ref, linear_ref, table_2, table_3, weight_ref, out_ref
+):
+    total = total_ref[...]
+    for ref in (low_ref, high_ref):
+        total = total + dot(ref[:, 512:768], table_2[...]) + dot(ref[:, 768:1024], table_3[...])
     mean = (total / degree_ref[:, 0:1]).astype(BF16)
-    out_ref[...] = normalized(linear + dot(mean, weight_ref[512:1024]))
+    out_ref[...] = normalized(linear_ref[...] + dot(mean, weight_ref[512:1024]))
 
 
 def hubs_body(parts_ref, linear_ref, weight_ref, out_ref):
@@ -247,30 +264,36 @@
     node_feats, hub_feats, weight, edge_src, edge_dst, bound_rows,
     hub_edge_src, hub_edge_slot, slot_hub,
 ):
-    where = jnp.stack([lax.axis_index("core"), lax.axis_index("side")]).astype(I32)
-    gathered = lax.all_to_all(
-        jnp.broadcast_to(hub_feats[None], (4, 4, 512)), "pair", 0, 0, tiled=True
-    )
+    axes = ("core", "side", "pair")
+    where = jnp.stack([lax.axis_index(axis) for axis in axes]).astype(I32)
+    pairs = lax.axis_size("pair")
+    gathered = []
+    for k in (1, 2, 3):
+        ring = [(i, (i - k) % pairs) for i in range(pairs)]
+        gathered.append(lax.ppermute(hub_feats, "pair", ring))
     mid = call(
-        slots_body, shape(16, ROWS, 128), [HBM] * 4, 1 << 30, 2 << 20,
+        slots_body, pltpu.HBM((16, ROWS, 128), BF16), [HBM] * 4, 1 << 30, 2 << 20,
+        out_specs=HBM,
         scratch_shapes=[
             pltpu.VMEM((1, 1024), I32),
             pltpu.VMEM((1, 1024), I32),
             pltpu.VMEM((1, 512), I32),
             pltpu.VMEM((128, 512), BF16),
             pltpu.SemaphoreType.DMA((4,)),
+            pltpu.VMEM((16, ROWS - SLOTS, 128), BF16),
+            pltpu.SemaphoreType.DMA((4,)),
         ],
     )(*in_hbm(hub_edge_src, hub_edge_slot, slot_hub, node_feats))
     mid = call(
-        fill_body, shape(16, ROWS, 128), [VMEM, ANY], 0, 1 << 20,
-        out_specs=ANY,
-        input_output_aliases={1: 0},
+        fill_body, pltpu.HBM((16, ROWS, 128), BF16), [VMEM] * 4 + [HBM], 0, 1 << 20,
+        out_specs=HBM,
+        input_output_aliases={4: 0},
         scratch_shapes=[
             pltpu.VMEM((16, 512), F32),
             pltpu.VMEM((64, 128), BF16),
             pltpu.SemaphoreType.DMA((16,)),
         ],
-    )(gathered, mid)
+    )(hub_feats, *gathered, mid)
     mid = lax.all_to_all(mid, OUTER, 0, 0, tiled=True)
     exports = call(export_body, shape(16, 512), [VMEM] * 2, 2 << 20, 150000)(bound_rows, node_feats)
     count = lax.axis_size(DOM)
@@ -281,11 +304,11 @@
     low, high, degree, hub_linear, partial = call(
         counts_body,
         (
-            shape(128, 1024), shape(128, 1024), shape(128, 128, dtype=F32),
+            shape(128, 1152), shape(128, 1152), shape(128, 128, dtype=F32),
             shape(4, 512, dtype=F32), shape(128, 512, dtype=F32),
         ),
-        [SMEM] + [VMEM] * 7, 1 << 30, 2 << 20,
-    )(where, edge_src, edge_dst, node_feats, before, after, hub_feats, weight)
+        [SMEM] + [VMEM] * 5, 1 << 30, 2 << 20,
+    )(where, edge_src, edge_dst, node_feats, hub_feats, weight)
     parts, table_0 = call(
         reduce_body, (pltpu.HBM((16, 4, 640), BF16), shape(256, 512)), [VMEM],
         1 << 26, 2 << 20,
@@ -297,8 +320,12 @@
     parts = lax.all_to_all(parts, INNER, 0, 0, tiled=True)
     table_2 = lax.ppermute(table_0, "core", swap)
     table_3 = lax.ppermute(table_1, "core", swap)
-    node_out = call(nodes_body, shape(128, 512), [VMEM] * 10, 1 << 29, 2 << 20)(
-        low, high, degree, partial, node_feats, table_0, table_1, table_2, table_3, weight
+    wide = shape(128, 512, dtype=F32)
+    total, linear = call(nodes_body, (wide, wide), [VMEM] * 9, 1 << 28, 1 << 20)(
+        low, high, partial, node_feats, before, after, table_0, table_1, weight
+    )
+    node_out = call(finish_body, shape(128, 512), [VMEM] * 8, 1 << 28, 1 << 20)(
+        low, high, degree, total, linear, table_2, table_3, weight
     )
     hub_out = call(hubs_body, shape(4, 512), [VMEM] * 3, 1 << 22, 1 << 19)(
         parts, hub_linear, weight

time: 64.7 us -> 63.5 us (0.981)
  waiting for transfers between devices: 8.7 us -> 5.68 us
  starting transfers between devices: 23.6 us -> 26.6 us
  local copies, waits for them, and re-layouts: 1.89 us -> 0.62 us
    ppermute x0 -> x3, starting transfers between devices: none -> 10.2 us  [on_device(): gathered.append(lax.ppermute(hub_feats, 'pair', ring))]
    all_to_all x1 -> x0, starting transfers between devices: 9 us -> none  [on_device(): lax.all_to_all(jnp.broadcast_to(hub_feats[None], (4, 4, 512)), 'pair', 0,...]
    all_to_all x1 -> x0, waiting for transfers between devices: 3.29 us -> none  [on_device(): lax.all_to_all(jnp.broadcast_to(hub_feats[None], (4, 4, 512)), 'pair', 0,...]
    all_to_all x1, starting transfers between devices: 4 us -> 6.01 us  [on_device(): parts = lax.all_to_all(parts, INNER, 0, 0, tiled=True)]
    broadcast_in_dim x1 -> x0, local copies, waits for them, and re-layouts: 1.3 us -> none  [on_device(): jnp.broadcast_to(hub_feats[None], (4, 4, 512))]
    pallas_call x4 -> x5, Pallas kernels: 8.21 us -> 8.04 us  [the longest x1 2.75 us: on_device(): call(counts_body, (shape(128, 1152), shape(128, 1152), shape(128, 128, dt...]
  transfers between devices with their start and end apart: 7 -> 9, of which waited for: 3 -> 2; matrix products, arithmetic and copies ran while one was open for 0% -> 0% of each run, Pallas kernels for 12% -> 11%
where the time goes in v5:
time: 63.5 us; the launch traced here: 63.2 us
  starting transfers between devices  26.6 us (42%)
  blocking collectives  19.4 us (31%)
  Pallas kernels  10.1 us (16%)
  waiting for transfers between devices  5.68 us (9%)
  between operations  0.75 us (1%)
    all_to_all x1, blocking collectives, on_device(): mid = lax.all_to_all(mid, OUTER, 0, 0, tiled=True)  19.4 us
    ppermute x3, starting transfers between devices, on_device(): gathered.append(lax.ppermute(hub_feats, 'pair', ring))  10.2 us
    all_to_all x1, starting transfers between devices, on_device(): parts = lax.all_to_all(parts, INNER, 0, 0, tiled=True)  6.01 us
    all_to_all x1, waiting for transfers between devices, on_device(): parts = lax.all_to_all(parts, INNER, 0, 0, tiled=True)  4.68 us
    ppermute x1, starting transfers between devices, on_device(): table_3 = lax.ppermute(table_1, 'core', swap)  4.36 us
    ppermute x1, starting transfers between devices, on_device(): table_2 = lax.ppermute(table_0, 'core', swap)  3.75 us
    pallas_call x1, Pallas kernels, on_device(): call(counts_body, (shape(128, 1152), shape(128, 1152), shape(128, 128, dt...  2.75 us
    pallas_call x1, Pallas kernels, on_device(): call(slots_body, pltpu.HBM((16, ROWS, 128), BF16), [HBM] * 4, 1 << 30, 2...  2.65 us
  transfers between devices with their start and end apart: 9, of which 2 were waited for; matrix products, arithmetic and copies ran while one was open for 0% of the time, Pallas kernels for 11%

profile of v5, /device:TPU:1, one launch (start us, length us, event | category | flops | bytes accessed | tf_op | source)
XLA Modules:
  0.0 63.2 jit_solution(46055228545388447)
XLA Ops:
  0.6 0.0 copy-start.2
  0.6 7.8 %collective-permute-start.3 = (bf16[4,512]{1,0:T(4,128)(2,1)}, bf16[4,512]{1,0:T(4,128)(2,1)S(1)}, u32[]{:S(2)}, u32[]{:S(2)}) collective-permute-start(bf16[4,512]{1,0:T(4,128)(2,1)} %rows_0.1), channel_id=1, source_target_pairs={{0,8},{4,12},{8,0},{12,4},{1,9},{5,13},{9,1},{13,5},{2,10},{6,14},... | collective-permute-start | bytes 12296 | tf_op jit(solution)/shard_map/ppermute | solution.py:273
  8.5 0.0 collective-permute-start.2
  8.5 2.4 %collective-permute-start.4 = (bf16[4,512]{1,0:T(4,128)(2,1)}, bf16[4,512]{1,0:T(4,128)(2,1)S(1)}, u32[]{:S(2)}, u32[]{:S(2)}) collective-permute-start(bf16[4,512]{1,0:T(4,128)(2,1)} %rows_0.1), channel_id=1, source_target_pairs={{0,4},{4,8},{8,12},{12,0},{1,5},{5,9},{9,13},{13,1},{2,6},{6,10},{... | collective-permute-start | bytes 12296 | tf_op jit(solution)/shard_map/ppermute | solution.py:273
  10.8 2.6 %shard_map.106.mid_in = bf16[16,200,128]{2,1,0:T(8,128)(2,1)} custom-call(s32[1,1024]{1,0:T(1,128)} %src_hbm.1, s32[1,1024]{1,0:T(1,128)} %slot_hbm.1, s32[1,512]{1,0:T(1,128)} %hub_hbm.1, bf16[128,512]{1,0:T(8,128)(2,1)} %feats_ref.5), custom_call_target="tpu_custom_call" | custom-call | flops 1073741824 | bytes 2097152 | tf_op jit(solution)/shard_map/pallas_call | solution.py:274
  13.5 0.0 collective-permute-done.3.rows_2
  13.5 0.0 collective-permute-done.2.rows_1
  13.5 0.0 collective-permute-done.4.rows_3
  13.5 0.0 copy-done.2
  13.5 0.9 %shard_map.107 = bf16[16,200,128]{2,1,0:T(8,128)(2,1)} custom-call(bf16[4,512]{1,0:T(4,128)(2,1)S(1)} %copy-done.2, bf16[4,512]{1,0:T(4,128)(2,1)S(1)} %collective-permute-done.2.rows_1, bf16[4,512]{1,0:T(4,128)(2,1)S(1)} %collective-permute-done.3.rows_2, bf16[4,512]{1,0:T(4,128)(2,1)S(1)} %collective-permute-done.4.rows_3, ...), custom_call_target="tpu_custom_call", output_to_operand_aliasing={{}: (4, {})} | custom-call | bytes 1048576 | tf_op jit(solution)/shard_map/pallas_call | solution.py:287
  14.4 0.0 copy-start
  14.4 19.4 %all_to_all.10.mid_ref = bf16[16,200,128]{2,1,0:T(8,128)(2,1)S(1)} all-to-all(bf16[16,200,128]{2,1,0:T(8,128)(2,1)} %shard_map.107), channel_id=1, replica_groups=mesh['role'=4,'x'=4,'pair'=4,'side'=2,'core'=2] {'role','x'}, dimensions={0} | all-to-all | bytes 1638400 | tf_op jit(solution)/shard_map/all_to_all | solution.py:297
  33.8 0.0 copy-start.1
  33.8 0.9 %shard_map.108 = (bf16[16,4,640]{2,1,0:T(4,128)(2,1)}, bf16[256,512]{1,0:T(8,128)(2,1)S(1)}) custom-call(bf16[16,200,128]{2,1,0:T(8,128)(2,1)S(1)} %all_to_all.10.mid_ref), custom_call_target="tpu_custom_call" | custom-call | flops 67108864 | bytes 2097152 | tf_op jit(solution)/shard_map/pallas_call | solution.py:312
  34.7 0.0 copy-start.3
  34.7 0.6 collective-permute-start.5
  35.3 3.7 %collective-permute-start.6 = (bf16[256,512]{1,0:T(8,128)(2,1)S(1)}, bf16[256,512]{1,0:T(8,128)(2,1)S(1)}, u32[]{:S(2)}, u32[]{:S(2)}) collective-permute-start(bf16[256,512]{1,0:T(8,128)(2,1)S(1)} %get-tuple-element.15.table_0), channel_id=1, source_target_pairs={{0,1},{1,0},{2,3},{3,2},{4,5},{5,4},{6,7},{7,6},{8,9},{9,8},{10,11... | collective-permute-start | bytes 786440 | tf_op jit(solution)/shard_map/ppermute | solution.py:321
  39.0 1.0 %collective-permute-done.5.table_1 = bf16[256,512]{1,0:T(8,128)(2,1)S(1)} collective-permute-done((bf16[256,512]{1,0:T(8,128)(2,1)S(1)}, bf16[256,512]{1,0:T(8,128)(2,1)S(1)}, u32[]{:S(2)}, u32[]{:S(2)}) %collective-permute-start.5) | collective-permute-done | bytes 262176 | tf_op jit(solution)/shard_map/ppermute | solution.py:319
  40.0 4.4 %collective-permute-start.7 = (bf16[256,512]{1,0:T(8,128)(2,1)S(1)}, bf16[256,512]{1,0:T(8,128)(2,1)S(1)}, u32[]{:S(2)}, u32[]{:S(2)}) collective-permute-start(bf16[256,512]{1,0:T(8,128)(2,1)S(1)} %collective-permute-done.5.table_1), channel_id=1, source_target_pairs={{0,1},{1,0},{2,3},{3,2},{4,5},{5,4},{6,7},{7,6},{8,9},{9,8},{10,11... | collective-permute-start | bytes 786440 | tf_op jit(solution)/shard_map/ppermute | solution.py:322
  44.4 0.0 copy-done.1
  44.4 0.0 copy-done.3
  44.4 0.2 shard_map.105
  44.5 0.0 collective-permute-start.1
  44.6 1.7 %collective-permute-start = (bf16[16,512]{1,0:T(8,128)(2,1)S(1)}, bf16[16,512]{1,0:T(8,128)(2,1)S(1)}, u32[]{:S(2)}, u32[]{:S(2)}) collective-permute-start(bf16[16,512]{1,0:T(8,128)(2,1)S(1)} %shard_map.105), channel_id=1, source_target_pairs={{0,1},{1,2},{2,3},{3,4},{4,5},{5,6},{6,7},{7,8},{8,9},{9,10},{10,1... | collective-permute-start | bytes 49160 | tf_op jit(solution)/shard_map/ppermute | solution.py:302
  46.3 0.0 copy-start.5
  46.3 6.0 %all-to-all-start.1 = ((bf16[16,4,640]{2,1,0:T(4,128)(2,1)}), bf16[16,4,640]{2,1,0:T(4,128)(2,1)S(1)}, u32[]{:S(2)}, u32[]{:S(2)}) async-start(bf16[16,4,640]{2,1,0:T(4,128)(2,1)} %get-tuple-element.18), calls=%async_computation.1 | async-start | bytes 163840 | tf_op jit(solution)/shard_map/all_to_all | solution.py:320
  52.3 0.0 copy-start.4
  52.3 0.1 pad_add_fusion.where_ref
  52.4 0.0 copy-done
  52.4 0.0 copy-done.5
  52.4 0.6 copy-done.4
  53.0 2.7 %shard_map.104 = (bf16[128,1152]{1,0:T(8,128)(2,1)S(1)}, bf16[128,1152]{1,0:T(8,128)(2,1)S(1)}, f32[128,128]{1,0:T(8,128)S(1)}, f32[4,512]{1,0:T(4,128)S(1)}, f32[128,512]{1,0:T(8,128)S(1)}) custom-call(s32[3]{0:T(128)S(1)} %pad_add_fusion.where_ref, s32[1,1024]{1,0:T(1,128)S(1)} %copy-done.4, s32[1,1024]{1,0:T(1,128)S(1)} %copy-done.5, ...), custom_call_target="tpu_custom_call" | custom-call | flops 1073741824 | bytes 2097152 | tf_op jit(solution)/shard_map/pallas_call | solution.py:304
  55.8 4.7 %all-to-all-done.1.parts_ref = bf16[16,4,640]{2,1,0:T(4,128)(2,1)S(1)} async-done(((bf16[16,4,640]{2,1,0:T(4,128)(2,1)}), bf16[16,4,640]{2,1,0:T(4,128)(2,1)S(1)}, u32[]{:S(2)}, u32[]{:S(2)}) %all-to-all-start.1) | async-done | bytes 81952 | tf_op jit(solution)/shard_map/all_to_all | solution.py:320
  60.4 1.0 %shard_map.111 = bf16[4,512]{1,0:T(4,128)(2,1)} custom-call(bf16[16,4,640]{2,1,0:T(4,128)(2,1)S(1)} %all-to-all-done.1.parts_ref, f32[4,512]{1,0:T(4,128)S(1)} %get-tuple-element.19.linear_ref, bf16[1024,512]{1,0:T(8,128)(2,1)S(1)} %copy-done), custom_call_target="tpu_custom_call" | custom-call | flops 4194304 | bytes 524288 | tf_op jit(solution)/shard_map/pallas_call | solution.py:330
  61.4 0.0 collective-permute-done.1.after_ref
  61.4 0.0 collective-permute-done.before_ref
  61.4 0.5 shard_map.109
  61.9 0.0 collective-permute-done.6.table_2
  62.0 0.0 collective-permute-done.7.table_3
  62.0 1.2 %shard_map.110 = bf16[128,512]{1,0:T(8,128)(2,1)} custom-call(bf16[128,1152]{1,0:T(8,128)(2,1)S(1)} %get-tuple-element.11.low_ref, bf16[128,1152]{1,0:T(8,128)(2,1)S(1)} %get-tuple-element.12.high_ref, f32[128,128]{1,0:T(8,128)S(1)} %get-tuple-element.13.degree_ref, f32[128,512]{1,0:T(8,128)S(1)} %get-tuple-element.16.total_ref, ...), custom_call_target="tpu_custom_call" | custom-call | flops 268435456 | bytes 1048576 | tf_op jit(solution)/shard_map/pallas_call | solution.py:327
Async XLA Ops:
  0.6 12.9 %copy-start.2 = (bf16[4,512]{1,0:T(4,128)(2,1)S(1)}, bf16[4,512]{1,0:T(4,128)(2,1)}, u32[]{:S(2)}) copy-start(bf16[4,512]{1,0:T(4,128)(2,1)} %rows_0.1) | copy-start | bytes 12292
  0.6 12.8 %collective-permute-start.3 = (bf16[4,512]{1,0:T(4,128)(2,1)}, bf16[4,512]{1,0:T(4,128)(2,1)S(1)}, u32[]{:S(2)}, u32[]{:S(2)}) collective-permute-start(bf16[4,512]{1,0:T(4,128)(2,1)} %rows_0.1), channel_id=1, source_target_pairs={{0,8},{4,12},{8,0},{12,4},{1,9},{5,13},{9,1},{13,5},{2,10},{6,14},... | collective-permute-start | bytes 12296 | tf_op jit(solution)/shard_map/ppermute | solution.py:273
  8.5 5.0 %collective-permute-start.2 = (bf16[4,512]{1,0:T(4,128)(2,1)}, bf16[4,512]{1,0:T(4,128)(2,1)S(1)}, u32[]{:S(2)}, u32[]{:S(2)}) collective-permute-start(bf16[4,512]{1,0:T(4,128)(2,1)} %rows_0.1), channel_id=1, source_target_pairs={{0,12},{4,0},{8,4},{12,8},{1,13},{5,1},{9,5},{13,9},{2,14},{6,2},{... | collective-permute-start | bytes 12296 | tf_op jit(solution)/shard_map/ppermute | solution.py:273
  8.5 5.0 %collective-permute-start.4 = (bf16[4,512]{1,0:T(4,128)(2,1)}, bf16[4,512]{1,0:T(4,128)(2,1)S(1)}, u32[]{:S(2)}, u32[]{:S(2)}) collective-permute-start(bf16[4,512]{1,0:T(4,128)(2,1)} %rows_0.1), channel_id=1, source_target_pairs={{0,4},{4,8},{8,12},{12,0},{1,5},{5,9},{9,13},{13,1},{2,6},{6,10},{... | collective-permute-start | bytes 12296 | tf_op jit(solution)/shard_map/ppermute | solution.py:273
  14.4 38.0 %copy-start = (bf16[1024,512]{1,0:T(8,128)(2,1)S(1)}, bf16[1024,512]{1,0:T(8,128)(2,1)}, u32[]{:S(2)}) copy-start(bf16[1024,512]{1,0:T(8,128)(2,1)} %weight_ref.7) | copy-start | bytes 3145732
  33.8 10.6 %copy-start.1 = (bf16[128,512]{1,0:T(8,128)(2,1)S(1)}, bf16[128,512]{1,0:T(8,128)(2,1)}, u32[]{:S(2)}) copy-start(bf16[128,512]{1,0:T(8,128)(2,1)} %feats_ref.5) | copy-start | bytes 393220
  34.7 9.7 %copy-start.3 = (s32[1,16]{1,0:T(1,128)S(1)}, s32[1,16]{1,0:T(1,128)}, u32[]{:S(2)}) copy-start(s32[1,16]{1,0:T(1,128)} %bound_ref.1) | copy-start | bytes 196
  34.7 5.3 %collective-permute-start.5 = (bf16[256,512]{1,0:T(8,128)(2,1)S(1)}, bf16[256,512]{1,0:T(8,128)(2,1)S(1)}, u32[]{:S(2)}, u32[]{:S(2)}) collective-permute-start(bf16[256,512]{1,0:T(8,128)(2,1)S(1)} %get-tuple-element.15.table_0), channel_id=1, source_target_pairs={{0,2},{2,0},{1,3},{3,1},{4,6},{6,4},{5,7},{7,5},{8,10},{10,8},{9,1... | collective-permute-start | bytes 786440 | tf_op jit(solution)/shard_map/ppermute | solution.py:319
  35.3 26.7 %collective-permute-start.6 = (bf16[256,512]{1,0:T(8,128)(2,1)S(1)}, bf16[256,512]{1,0:T(8,128)(2,1)S(1)}, u32[]{:S(2)}, u32[]{:S(2)}) collective-permute-start(bf16[256,512]{1,0:T(8,128)(2,1)S(1)} %get-tuple-element.15.table_0), channel_id=1, source_target_pairs={{0,1},{1,0},{2,3},{3,2},{4,5},{5,4},{6,7},{7,6},{8,9},{9,8},{10,11... | collective-permute-start | bytes 786440 | tf_op jit(solution)/shard_map/ppermute | solution.py:321
  40.0 22.0 %collective-permute-start.7 = (bf16[256,512]{1,0:T(8,128)(2,1)S(1)}, bf16[256,512]{1,0:T(8,128)(2,1)S(1)}, u32[]{:S(2)}, u32[]{:S(2)}) collective-permute-start(bf16[256,512]{1,0:T(8,128)(2,1)S(1)} %collective-permute-done.5.table_1), channel_id=1, source_target_pairs={{0,1},{1,0},{2,3},{3,2},{4,5},{5,4},{6,7},{7,6},{8,9},{9,8},{10,11... | collective-permute-start | bytes 786440 | tf_op jit(solution)/shard_map/ppermute | solution.py:322
  44.5 16.9 %collective-permute-start.1 = (bf16[16,512]{1,0:T(8,128)(2,1)S(1)}, bf16[16,512]{1,0:T(8,128)(2,1)S(1)}, u32[]{:S(2)}, u32[]{:S(2)}) collective-permute-start(bf16[16,512]{1,0:T(8,128)(2,1)S(1)} %shard_map.105), channel_id=1, source_target_pairs={{1,0},{2,1},{3,2},{4,3},{5,4},{6,5},{7,6},{8,7},{9,8},{10,9},{11,1... | collective-permute-start | bytes 49160 | tf_op jit(solution)/shard_map/ppermute | solution.py:303
  44.6 16.9 %collective-permute-start = (bf16[16,512]{1,0:T(8,128)(2,1)S(1)}, bf16[16,512]{1,0:T(8,128)(2,1)S(1)}, u32[]{:S(2)}, u32[]{:S(2)}) collective-permute-start(bf16[16,512]{1,0:T(8,128)(2,1)S(1)} %shard_map.105), channel_id=1, source_target_pairs={{0,1},{1,2},{2,3},{3,4},{4,5},{5,6},{6,7},{7,8},{8,9},{9,10},{10,1... | collective-permute-start | bytes 49160 | tf_op jit(solution)/shard_map/ppermute | solution.py:302
  46.3 6.1 %copy-start.5 = (s32[1,1024]{1,0:T(1,128)S(1)}, s32[1,1024]{1,0:T(1,128)}, u32[]{:S(2)}) copy-start(s32[1,1024]{1,0:T(1,128)} %dst_ref.1) | copy-start | bytes 12292
  46.3 14.1 %all-to-all-start.1 = ((bf16[16,4,640]{2,1,0:T(4,128)(2,1)}), bf16[16,4,640]{2,1,0:T(4,128)(2,1)S(1)}, u32[]{:S(2)}, u32[]{:S(2)}) async-start(bf16[16,4,640]{2,1,0:T(4,128)(2,1)} %get-tuple-element.18), calls=%async_computation.1 | async-start | bytes 163840 | tf_op jit(solution)/shard_map/all_to_all | solution.py:320
  52.3 0.7 %copy-start.4 = (s32[1,1024]{1,0:T(1,128)S(1)}, s32[1,1024]{1,0:T(1,128)}, u32[]{:S(2)}) copy-start(s32[1,1024]{1,0:T(1,128)} %src_ref.1) | copy-start | bytes 12292

commit v6 on v5

--- a/solution.py
+++ b/solution.py
@@ -7,10 +7,10 @@
 from jax.sharding import PartitionSpec as P
 
 
-INNER = ("pair", "side", "core")
+INNER = ("far", "near", "side", "core")
 OUTER = ("role", "x")
-DOM = ("x", "pair", "side", "core")
-ROLE_DOM = ("role", "x", "pair", "side", "core")
+DOM = ("x", "far", "near", "side", "core")
+ROLE_DOM = ("role", "x", "far", "near", "side", "core")
 
 epsilon = 1e-06
 F32 = jnp.float32
@@ -52,7 +52,7 @@
     return jnp.where(row == index, 1.0, 0.0).astype(BF16)
 
 
-GATHERED, SLOTS, ABOUT, ROWS = 0, 64, 192, 200
+GATHERED, SLOTS, ABOUT, ROWS = 0, 32, 160, 168
 
 
 def block_of(first, k):
@@ -116,14 +116,14 @@
         copy.wait()
 
 
-def fill_body(rows_0, rows_1, rows_2, rows_3, mid_in, mid_ref, wide, block, sems):
+def fill_body(rows_0, rows_1, mid_in, mid_ref, wide, block, sems):
     del mid_in
-    for k, rows in enumerate((rows_0, rows_1, rows_2, rows_3)):
+    for k, rows in enumerate((rows_0, rows_1)):
         wide[4 * k : 4 * k + 4, :] = rows[...].astype(F32)
     for k in range(4):
-        block[16 * k : 16 * k + 16, :] = wide[:, 128 * k : 128 * k + 128].astype(BF16)
+        block[8 * k : 8 * k + 8, :] = wide[:, 128 * k : 128 * k + 128].astype(BF16)
     copies = [
-        pltpu.make_async_copy(block, mid_ref.at[t, pl.ds(GATHERED, 64)], sems.at[t])
+        pltpu.make_async_copy(block, mid_ref.at[t, pl.ds(GATHERED, 32)], sems.at[t])
         for t in range(16)
     ]
     for copy in copies:
@@ -157,7 +157,7 @@
     copy = pltpu.make_async_copy(out_ref, out_hbm, sem)
     copy.start()
     for k in range(4):
-        table_ref[:, 128 * k : 128 * k + 128] = mid_ref[:, block_of(GATHERED, k), :].reshape(256, 128)
+        table_ref[:, 128 * k : 128 * k + 128] = mid_ref[:, block_of(GATHERED, k), :].reshape(128, 128)
     copy.wait()
 
 
@@ -167,12 +167,13 @@
 ):
     core = where_ref[0]
     side = where_ref[1]
-    pair = where_ref[2]
+    near = where_ref[2]
+    far = where_ref[3]
     src = src_ref[...]
     targets = onehot(128, dst_ref[...])
     hub = src - 160
-    table = (((hub >> 2) & 1) ^ core) * 2 + (((hub >> 3) & 1) ^ side)
-    column = table * 256 + (hub >> 6) * 16 + (((hub >> 4) - pair) & 3) * 4 + (hub & 3)
+    table = (((hub >> 2) & 1) ^ core) * 4 + (((hub >> 4) & 1) ^ near) * 2 + (((hub >> 3) & 1) ^ side)
+    column = table * 128 + (hub >> 6) * 8 + (((hub >> 5) & 1) ^ far) * 4 + (hub & 3)
     column = jnp.where(hub < 0, -1, column)
     degree_ref[...] = jnp.broadcast_to(
         jnp.sum(targets.astype(F32), axis=1, keepdims=True), degree_ref.shape
@@ -202,24 +203,28 @@
 
 
 def nodes_body(
-    low_ref, high_ref, partial_ref, feats_ref, before_ref, after_ref, table_0, table_1, weight_ref,
+    low_ref, high_ref, partial_ref, feats_ref, before_ref, after_ref,
+    table_0, table_1, table_2, table_3, weight_ref,
     total_ref, linear_ref,
 ):
     linear_ref[...] = dot(feats_ref[...], weight_ref[0:512])
     total = partial_ref[...]
+    tables = jnp.concatenate([t[...] for t in (table_0, table_1, table_2, table_3)], axis=0)
     for ref in (low_ref, high_ref):
         total = total + dot(ref[:, 1024:1040], before_ref[...])
         total = total + dot(ref[:, 1040:1056], after_ref[...])
-        total = total + dot(ref[:, 0:256], table_0[...]) + dot(ref[:, 256:512], table_1[...])
+        total = total + dot(ref[:, 0:512], tables)
     total_ref[...] = total
 
 
 def finish_body(
-    low_ref, high_ref, degree_ref, total_ref, linear_ref, table_2, table_3, weight_ref, out_ref
+    low_ref, high_ref, degree_ref, total_ref, linear_ref,
+    table_4, table_5, table_6, table_7, weight_ref, out_ref,
 ):
     total = total_ref[...]
+    tables = jnp.concatenate([t[...] for t in (table_4, table_5, table_6, table_7)], axis=0)
     for ref in (low_ref, high_ref):
-        total = total + dot(ref[:, 512:768], table_2[...]) + dot(ref[:, 768:1024], table_3[...])
+        total = total + dot(ref[:, 512:1024], tables)
     mean = (total / degree_ref[:, 0:1]).astype(BF16)
     out_ref[...] = normalized(linear_ref[...] + dot(mean, weight_ref[512:1024]))
 
@@ -264,13 +269,10 @@
     node_feats, hub_feats, weight, edge_src, edge_dst, bound_rows,
     hub_edge_src, hub_edge_slot, slot_hub,
 ):
-    axes = ("core", "side", "pair")
+    axes = ("core", "side", "near", "far")
     where = jnp.stack([lax.axis_index(axis) for axis in axes]).astype(I32)
-    pairs = lax.axis_size("pair")
-    gathered = []
-    for k in (1, 2, 3):
-        ring = [(i, (i - k) % pairs) for i in range(pairs)]
-        gathered.append(lax.ppermute(hub_feats, "pair", ring))
+    swap = [(0, 1), (1, 0)]
+    gathered = lax.ppermute(hub_feats, "far", swap)
     mid = call(
         slots_body, pltpu.HBM((16, ROWS, 128), BF16), [HBM] * 4, 1 << 30, 2 << 20,
         out_specs=HBM,
@@ -285,15 +287,15 @@
         ],
     )(*in_hbm(hub_edge_src, hub_edge_slot, slot_hub, node_feats))
     mid = call(
-        fill_body, pltpu.HBM((16, ROWS, 128), BF16), [VMEM] * 4 + [HBM], 0, 1 << 20,
+        fill_body, pltpu.HBM((16, ROWS, 128), BF16), [VMEM] * 2 + [HBM], 0, 1 << 20,
         out_specs=HBM,
-        input_output_aliases={4: 0},
+        input_output_aliases={2: 0},
         scratch_shapes=[
-            pltpu.VMEM((16, 512), F32),
-            pltpu.VMEM((64, 128), BF16),
+            pltpu.VMEM((8, 512), F32),
+            pltpu.VMEM((32, 128), BF16),
             pltpu.SemaphoreType.DMA((16,)),
         ],
-    )(hub_feats, *gathered, mid)
+    )(hub_feats, gathered, mid)
     mid = lax.all_to_all(mid, OUTER, 0, 0, tiled=True)
     exports = call(export_body, shape(16, 512), [VMEM] * 2, 2 << 20, 150000)(bound_rows, node_feats)
     count = lax.axis_size(DOM)
@@ -310,22 +312,25 @@
         [SMEM] + [VMEM] * 5, 1 << 30, 2 << 20,
     )(where, edge_src, edge_dst, node_feats, hub_feats, weight)
     parts, table_0 = call(
-        reduce_body, (pltpu.HBM((16, 4, 640), BF16), shape(256, 512)), [VMEM],
+        reduce_body, (pltpu.HBM((16, 4, 640), BF16), shape(128, 512)), [VMEM],
         1 << 26, 2 << 20,
         out_specs=(HBM, VMEM),
         scratch_shapes=[pltpu.VMEM((16, 4, 640), BF16), pltpu.SemaphoreType.DMA],
     )(mid)
-    swap = [(0, 1), (1, 0)]
     table_1 = lax.ppermute(table_0, "side", swap)
+    table_2 = lax.ppermute(table_0, "near", swap)
+    table_3 = lax.ppermute(table_0, ("near", "side"), [(i, i ^ 3) for i in range(4)])
     parts = lax.all_to_all(parts, INNER, 0, 0, tiled=True)
-    table_2 = lax.ppermute(table_0, "core", swap)
-    table_3 = lax.ppermute(table_1, "core", swap)
+    tables = [table_0, table_1, table_2, table_3]
+    others = []
+    for table in tables:
+        others.append(lax.ppermute(table, "core", swap))
     wide = shape(128, 512, dtype=F32)
-    total, linear = call(nodes_body, (wide, wide), [VMEM] * 9, 1 << 28, 1 << 20)(
-        low, high, partial, node_feats, before, after, table_0, table_1, weight
-    )
-    node_out = call(finish_body, shape(128, 512), [VMEM] * 8, 1 << 28, 1 << 20)(
-        low, high, degree, total, linear, table_2, table_3, weight
+    total, linear = call(nodes_body, (wide, wide), [VMEM] * 11, 1 << 28, 1 << 20)(
+        low, high, partial, node_feats, before, after, *tables, weight
+    )
+    node_out = call(finish_body, shape(128, 512), [VMEM] * 10, 1 << 28, 1 << 20)(
+        low, high, degree, total, linear, *others, weight
     )
     hub_out = call(hubs_body, shape(4, 512), [VMEM] * 3, 1 << 22, 1 << 19)(
         parts, hub_linear, weight
@@ -334,7 +339,7 @@
 
 
 def solution(mesh):
-    finer = Mesh(mesh.devices.reshape(4, 4, 4, 2, 2), ROLE_DOM)
+    finer = Mesh(mesh.devices.reshape(4, 4, 2, 2, 2, 2), ROLE_DOM)
     rows = P(ROLE_DOM, None)
     in_specs = (rows, rows, P(), rows, rows, rows, rows, rows, rows)
     return jax.shard_map(

time: 63.5 us -> 55.6 us (0.88)
  starting transfers between devices: 26.6 us -> 22.7 us
  waiting for transfers between devices: 5.68 us -> 2.82 us
    ppermute x5 -> x7, starting transfers between devices: 18.3 us -> 12.3 us  [the longest x1 7.81 us: on_device(): gathered = lax.ppermute(hub_feats, 'far', swap)]
    all_to_all x1, waiting for transfers between devices: 4.68 us -> 2.56 us  [on_device(): parts = lax.all_to_all(parts, INNER, 0, 0, tiled=True)]
    ppermute x1, starting transfers between devices: 1.74 us -> 2.92 us  [on_device(): before = lax.ppermute(exports, DOM, forward)]
    ppermute x1, waiting for transfers between devices: 0.99 us -> 0.01 us  [on_device(): table_1 = lax.ppermute(table_0, 'side', swap)]
  transfers between devices with their start and end apart: 9 -> 11, of which waited for: 2 -> 2; matrix products, arithmetic and copies ran while one was open for 0% -> 0% of each run, Pallas kernels for 11% -> 13%
where the time goes in v6:
time: 55.6 us; the launch traced here: 55.3 us
  starting transfers between devices  22.7 us (41%)
  blocking collectives  18.8 us (34%)
  Pallas kernels  10 us (18%)
  waiting for transfers between devices  2.82 us (5%)
  between operations  0.74 us (1%)
    all_to_all x1, blocking collectives, on_device(): mid = lax.all_to_all(mid, OUTER, 0, 0, tiled=True)  18.8 us
    ppermute x1, starting transfers between devices, on_device(): gathered = lax.ppermute(hub_feats, 'far', swap)  7.81 us
    all_to_all x1, starting transfers between devices, on_device(): parts = lax.all_to_all(parts, INNER, 0, 0, tiled=True)  6.15 us
    ppermute x1, starting transfers between devices, on_device(): before = lax.ppermute(exports, DOM, forward)  2.92 us
    pallas_call x1, Pallas kernels, on_device(): call(counts_body, (shape(128, 1152), shape(128, 1152), shape(128, 128, dt...  2.75 us
    pallas_call x1, Pallas kernels, on_device(): call(slots_body, pltpu.HBM((16, ROWS, 128), BF16), [HBM] * 4, 1 << 30, 2...  2.66 us
    all_to_all x1, waiting for transfers between devices, on_device(): parts = lax.all_to_all(parts, INNER, 0, 0, tiled=True)  2.56 us
    ppermute x1, starting transfers between devices, on_device(): lax.ppermute(table_0, ('near', 'side'), [(i, i ^ 3) for i in range(4)])  1.83 us
  transfers between devices with their start and end apart: 11, of which 2 were waited for; matrix products, arithmetic and copies ran while one was open for 0% of the time, Pallas kernels for 13%

profile of v6, /device:TPU:1, one launch (start us, length us, event | category | flops | bytes accessed | tf_op | source)
XLA Modules:
  0.0 55.3 jit_solution(10448422991534943826)
XLA Ops:
  0.6 0.0 copy-start.2
  0.6 7.8 %collective-permute-start.2 = (bf16[4,512]{1,0:T(4,128)(2,1)}, bf16[4,512]{1,0:T(4,128)(2,1)S(1)}, u32[]{:S(2)}, u32[]{:S(2)}) collective-permute-start(bf16[4,512]{1,0:T(4,128)(2,1)} %rows_0.1), channel_id=1, source_target_pairs={{0,8},{8,0},{1,9},{9,1},{2,10},{10,2},{3,11},{11,3},{4,12},{12,4},... | collective-permute-start | bytes 12296 | tf_op jit(solution)/shard_map/ppermute | solution.py:275
  8.5 2.7 %shard_map.106.mid_in = bf16[16,168,128]{2,1,0:T(8,128)(2,1)} custom-call(s32[1,1024]{1,0:T(1,128)} %src_hbm.1, s32[1,1024]{1,0:T(1,128)} %slot_hbm.1, s32[1,512]{1,0:T(1,128)} %hub_hbm.1, bf16[128,512]{1,0:T(8,128)(2,1)} %feats_ref.5), custom_call_target="tpu_custom_call" | custom-call | flops 1073741824 | bytes 2097152 | tf_op jit(solution)/shard_map/pallas_call | solution.py:276
  11.1 0.0 collective-permute-done.2.rows_1
  11.1 0.0 copy-done.2
  11.1 0.8 %shard_map.107 = bf16[16,168,128]{2,1,0:T(8,128)(2,1)} custom-call(bf16[4,512]{1,0:T(4,128)(2,1)S(1)} %copy-done.2, bf16[4,512]{1,0:T(4,128)(2,1)S(1)} %collective-permute-done.2.rows_1, bf16[16,168,128]{2,1,0:T(8,128)(2,1)} %shard_map.106.mid_in), custom_call_target="tpu_custom_call", output_to_operand_aliasing={{}: (2, {})} | custom-call | bytes 1048576 | tf_op jit(solution)/shard_map/pallas_call | solution.py:289
  12.0 0.0 copy-start
  12.0 18.8 %all_to_all.10.mid_ref = bf16[16,168,128]{2,1,0:T(8,128)(2,1)S(1)} all-to-all(bf16[16,168,128]{2,1,0:T(8,128)(2,1)} %shard_map.107), channel_id=1, replica_groups=mesh['role'=4,'x'=4,'far'=2,'near'=2,'side'=2,'core'=2] {'role','x'}, dimensions={0} | all-to-all | bytes 1376256 | tf_op jit(solution)/shard_map/all_to_all | solution.py:299
  30.8 0.0 copy-start.1
  30.8 0.9 %shard_map.108 = (bf16[16,4,640]{2,1,0:T(4,128)(2,1)}, bf16[128,512]{1,0:T(8,128)(2,1)S(1)}) custom-call(bf16[16,168,128]{2,1,0:T(8,128)(2,1)S(1)} %all_to_all.10.mid_ref), custom_call_target="tpu_custom_call" | custom-call | flops 67108864 | bytes 2097152 | tf_op jit(solution)/shard_map/pallas_call | solution.py:314
  31.7 0.0 copy-start.3
  31.7 0.8 %collective-permute-start.3 = (bf16[128,512]{1,0:T(8,128)(2,1)S(1)}, bf16[128,512]{1,0:T(8,128)(2,1)S(1)}, u32[]{:S(2)}, u32[]{:S(2)}) collective-permute-start(bf16[128,512]{1,0:T(8,128)(2,1)S(1)} %get-tuple-element.15.table_0), channel_id=1, source_target_pairs={{0,2},{2,0},{1,3},{3,1},{4,6},{6,4},{5,7},{7,5},{8,10},{10,8},{9,1... | collective-permute-start | bytes 393224 | tf_op jit(solution)/shard_map/ppermute | solution.py:320
  32.5 1.0 %collective-permute-start.4 = (bf16[128,512]{1,0:T(8,128)(2,1)S(1)}, bf16[128,512]{1,0:T(8,128)(2,1)S(1)}, u32[]{:S(2)}, u32[]{:S(2)}) collective-permute-start(bf16[128,512]{1,0:T(8,128)(2,1)S(1)} %get-tuple-element.15.table_0), channel_id=1, source_target_pairs={{0,4},{4,0},{1,5},{5,1},{2,6},{6,2},{3,7},{7,3},{8,12},{12,8},{9,1... | collective-permute-start | bytes 393224 | tf_op jit(solution)/shard_map/ppermute | solution.py:321
  33.5 1.8 %collective-permute-start.5 = (bf16[128,512]{1,0:T(8,128)(2,1)S(1)}, bf16[128,512]{1,0:T(8,128)(2,1)S(1)}, u32[]{:S(2)}, u32[]{:S(2)}) collective-permute-start(bf16[128,512]{1,0:T(8,128)(2,1)S(1)} %get-tuple-element.15.table_0), channel_id=1, source_target_pairs={{0,6},{2,4},{4,2},{6,0},{1,7},{3,5},{5,3},{7,1},{8,14},{10,12},{12... | collective-permute-start | bytes 393224 | tf_op jit(solution)/shard_map/ppermute | solution.py:322
  35.3 0.0 copy-done.1
  35.3 0.0 copy-done.3
  35.3 0.2 shard_map.105
  35.5 2.9 %collective-permute-start = (bf16[16,512]{1,0:T(8,128)(2,1)S(1)}, bf16[16,512]{1,0:T(8,128)(2,1)S(1)}, u32[]{:S(2)}, u32[]{:S(2)}) collective-permute-start(bf16[16,512]{1,0:T(8,128)(2,1)S(1)} %shard_map.105), channel_id=1, source_target_pairs={{0,1},{1,2},{2,3},{3,4},{4,5},{5,6},{6,7},{7,8},{8,9},{9,10},{10,1... | collective-permute-start | bytes 49160 | tf_op jit(solution)/shard_map/ppermute | solution.py:304
  38.4 0.3 collective-permute-start.6
  38.7 6.1 %all-to-all-start.1 = ((bf16[16,4,640]{2,1,0:T(4,128)(2,1)}), bf16[16,4,640]{2,1,0:T(4,128)(2,1)S(1)}, u32[]{:S(2)}, u32[]{:S(2)}) async-start(bf16[16,4,640]{2,1,0:T(4,128)(2,1)} %get-tuple-element.18), calls=%async_computation.1 | async-start | bytes 163840 | tf_op jit(solution)/shard_map/all_to_all | solution.py:323
  44.9 0.0 collective-permute-done.3.table_1
  44.9 0.2 collective-permute-start.7
  45.1 0.0 collective-permute-done.4.table_2
  45.1 1.1 %collective-permute-start.8 = (bf16[128,512]{1,0:T(8,128)(2,1)S(1)}, bf16[128,512]{1,0:T(8,128)(2,1)S(1)}, u32[]{:S(2)}, u32[]{:S(2)}) collective-permute-start(bf16[128,512]{1,0:T(8,128)(2,1)S(1)} %collective-permute-done.4.table_2), channel_id=1, source_target_pairs={{0,1},{1,0},{2,3},{3,2},{4,5},{5,4},{6,7},{7,6},{8,9},{9,8},{10,11... | collective-permute-start | bytes 393224 | tf_op jit(solution)/shard_map/ppermute | solution.py:327
  46.2 0.0 collective-permute-done.5.table_3
  46.2 0.0 collective-permute-start.9
  46.2 0.0 copy-start.4
  46.2 0.0 copy-start.5
  46.2 0.1 pad_add_fusion.where_ref
  46.3 0.0 collective-permute-done.before_ref
  46.3 0.5 collective-permute-start.1
  46.8 0.0 copy-done
  46.8 0.1 copy-done.4
  46.9 0.0 copy-done.5
  46.9 2.7 %shard_map.104 = (bf16[128,1152]{1,0:T(8,128)(2,1)S(1)}, bf16[128,1152]{1,0:T(8,128)(2,1)S(1)}, f32[128,128]{1,0:T(8,128)S(1)}, f32[4,512]{1,0:T(4,128)S(1)}, f32[128,512]{1,0:T(8,128)S(1)}) custom-call(s32[4]{0:T(128)S(1)} %pad_add_fusion.where_ref, s32[1,1024]{1,0:T(1,128)S(1)} %copy-done.4, s32[1,1024]{1,0:T(1,128)S(1)} %copy-done.5, ...), custom_call_target="tpu_custom_call" | custom-call | flops 1073741824 | bytes 2097152 | tf_op jit(solution)/shard_map/pallas_call | solution.py:306
  49.7 0.2 collective-permute-done.1.after_ref
  49.9 0.5 shard_map.109
  50.4 2.6 %all-to-all-done.1.parts_ref = bf16[16,4,640]{2,1,0:T(4,128)(2,1)S(1)} async-done(((bf16[16,4,640]{2,1,0:T(4,128)(2,1)}), bf16[16,4,640]{2,1,0:T(4,128)(2,1)S(1)}, u32[]{:S(2)}, u32[]{:S(2)}) %all-to-all-start.1) | async-done | bytes 81952 | tf_op jit(solution)/shard_map/all_to_all | solution.py:323
  53.0 1.0 %shard_map.111 = bf16[4,512]{1,0:T(4,128)(2,1)} custom-call(bf16[16,4,640]{2,1,0:T(4,128)(2,1)S(1)} %all-to-all-done.1.parts_ref, f32[4,512]{1,0:T(4,128)S(1)} %get-tuple-element.19.linear_ref, bf16[1024,512]{1,0:T(8,128)(2,1)S(1)} %copy-done), custom_call_target="tpu_custom_call" | custom-call | flops 4194304 | bytes 524288 | tf_op jit(solution)/shard_map/pallas_call | solution.py:335
  54.0 0.0 collective-permute-done.6.table_4
  54.0 0.0 collective-permute-done.7.table_5
  54.0 0.0 collective-permute-done.8.table_6
  54.0 0.0 collective-permute-done.9.table_7
  54.0 1.3 %shard_map.110 = bf16[128,512]{1,0:T(8,128)(2,1)} custom-call(bf16[128,1152]{1,0:T(8,128)(2,1)S(1)} %get-tuple-element.11.low_ref, bf16[128,1152]{1,0:T(8,128)(2,1)S(1)} %get-tuple-element.12.high_ref, f32[128,128]{1,0:T(8,128)S(1)} %get-tuple-element.13.degree_ref, f32[128,512]{1,0:T(8,128)S(1)} %get-tuple-element.16.total_ref, ...), custom_call_target="tpu_custom_call" | custom-call | flops 268435456 | bytes 1048576 | tf_op jit(solution)/shard_map/pallas_call | solution.py:332
Async XLA Ops:
  0.6 10.5 %copy-start.2 = (bf16[4,512]{1,0:T(4,128)(2,1)S(1)}, bf16[4,512]{1,0:T(4,128)(2,1)}, u32[]{:S(2)}) copy-start(bf16[4,512]{1,0:T(4,128)(2,1)} %rows_0.1) | copy-start | bytes 12292
  0.6 10.5 %collective-permute-start.2 = (bf16[4,512]{1,0:T(4,128)(2,1)}, bf16[4,512]{1,0:T(4,128)(2,1)S(1)}, u32[]{:S(2)}, u32[]{:S(2)}) collective-permute-start(bf16[4,512]{1,0:T(4,128)(2,1)} %rows_0.1), channel_id=1, source_target_pairs={{0,8},{8,0},{1,9},{9,1},{2,10},{10,2},{3,11},{11,3},{4,12},{12,4},... | collective-permute-start | bytes 12296 | tf_op jit(solution)/shard_map/ppermute | solution.py:275
  12.0 34.8 %copy-start = (bf16[1024,512]{1,0:T(8,128)(2,1)S(1)}, bf16[1024,512]{1,0:T(8,128)(2,1)}, u32[]{:S(2)}) copy-start(bf16[1024,512]{1,0:T(8,128)(2,1)} %weight_ref.7) | copy-start | bytes 3145732
  30.8 4.5 %copy-start.1 = (bf16[128,512]{1,0:T(8,128)(2,1)S(1)}, bf16[128,512]{1,0:T(8,128)(2,1)}, u32[]{:S(2)}) copy-start(bf16[128,512]{1,0:T(8,128)(2,1)} %feats_ref.5) | copy-start | bytes 393220
  31.7 3.7 %copy-start.3 = (s32[1,16]{1,0:T(1,128)S(1)}, s32[1,16]{1,0:T(1,128)}, u32[]{:S(2)}) copy-start(s32[1,16]{1,0:T(1,128)} %bound_ref.1) | copy-start | bytes 196
  31.7 13.2 %collective-permute-start.3 = (bf16[128,512]{1,0:T(8,128)(2,1)S(1)}, bf16[128,512]{1,0:T(8,128)(2,1)S(1)}, u32[]{:S(2)}, u32[]{:S(2)}) collective-permute-start(bf16[128,512]{1,0:T(8,128)(2,1)S(1)} %get-tuple-element.15.table_0), channel_id=1, source_target_pairs={{0,2},{2,0},{1,3},{3,1},{4,6},{6,4},{5,7},{7,5},{8,10},{10,8},{9,1... | collective-permute-start | bytes 393224 | tf_op jit(solution)/shard_map/ppermute | solution.py:320
  32.5 12.6 %collective-permute-start.4 = (bf16[128,512]{1,0:T(8,128)(2,1)S(1)}, bf16[128,512]{1,0:T(8,128)(2,1)S(1)}, u32[]{:S(2)}, u32[]{:S(2)}) collective-permute-start(bf16[128,512]{1,0:T(8,128)(2,1)S(1)} %get-tuple-element.15.table_0), channel_id=1, source_target_pairs={{0,4},{4,0},{1,5},{5,1},{2,6},{6,2},{3,7},{7,3},{8,12},{12,8},{9,1... | collective-permute-start | bytes 393224 | tf_op jit(solution)/shard_map/ppermute | solution.py:321
  33.5 12.7 %collective-permute-start.5 = (bf16[128,512]{1,0:T(8,128)(2,1)S(1)}, bf16[128,512]{1,0:T(8,128)(2,1)S(1)}, u32[]{:S(2)}, u32[]{:S(2)}) collective-permute-start(bf16[128,512]{1,0:T(8,128)(2,1)S(1)} %get-tuple-element.15.table_0), channel_id=1, source_target_pairs={{0,6},{2,4},{4,2},{6,0},{1,7},{3,5},{5,3},{7,1},{8,14},{10,12},{12... | collective-permute-start | bytes 393224 | tf_op jit(solution)/shard_map/ppermute | solution.py:322
  35.5 10.8 %collective-permute-start = (bf16[16,512]{1,0:T(8,128)(2,1)S(1)}, bf16[16,512]{1,0:T(8,128)(2,1)S(1)}, u32[]{:S(2)}, u32[]{:S(2)}) collective-permute-start(bf16[16,512]{1,0:T(8,128)(2,1)S(1)} %shard_map.105), channel_id=1, source_target_pairs={{0,1},{1,2},{2,3},{3,4},{4,5},{5,6},{6,7},{7,8},{8,9},{9,10},{10,1... | collective-permute-start | bytes 49160 | tf_op jit(solution)/shard_map/ppermute | solution.py:304
  38.4 15.6 %collective-permute-start.6 = (bf16[128,512]{1,0:T(8,128)(2,1)S(1)}, bf16[128,512]{1,0:T(8,128)(2,1)S(1)}, u32[]{:S(2)}, u32[]{:S(2)}) collective-permute-start(bf16[128,512]{1,0:T(8,128)(2,1)S(1)} %get-tuple-element.15.table_0), channel_id=1, source_target_pairs={{0,1},{1,0},{2,3},{3,2},{4,5},{5,4},{6,7},{7,6},{8,9},{9,8},{10,11... | collective-permute-start | bytes 393224 | tf_op jit(solution)/shard_map/ppermute | solution.py:327
  38.7 14.3 %all-to-all-start.1 = ((bf16[16,4,640]{2,1,0:T(4,128)(2,1)}), bf16[16,4,640]{2,1,0:T(4,128)(2,1)S(1)}, u32[]{:S(2)}, u32[]{:S(2)}) async-start(bf16[16,4,640]{2,1,0:T(4,128)(2,1)} %get-tuple-element.18), calls=%async_computation.1 | async-start | bytes 163840 | tf_op jit(solution)/shard_map/all_to_all | solution.py:323
  44.9 9.1 %collective-permute-start.7 = (bf16[128,512]{1,0:T(8,128)(2,1)S(1)}, bf16[128,512]{1,0:T(8,128)(2,1)S(1)}, u32[]{:S(2)}, u32[]{:S(2)}) collective-permute-start(bf16[128,512]{1,0:T(8,128)(2,1)S(1)} %collective-permute-done.3.table_1), channel_id=1, source_target_pairs={{0,1},{1,0},{2,3},{3,2},{4,5},{5,4},{6,7},{7,6},{8,9},{9,8},{10,11... | collective-permute-start | bytes 393224 | tf_op jit(solution)/shard_map/ppermute | solution.py:327
  45.1 8.9 %collective-permute-start.8 = (bf16[128,512]{1,0:T(8,128)(2,1)S(1)}, bf16[128,512]{1,0:T(8,128)(2,1)S(1)}, u32[]{:S(2)}, u32[]{:S(2)}) collective-permute-start(bf16[128,512]{1,0:T(8,128)(2,1)S(1)} %collective-permute-done.4.table_2), channel_id=1, source_target_pairs={{0,1},{1,0},{2,3},{3,2},{4,5},{5,4},{6,7},{7,6},{8,9},{9,8},{10,11... | collective-permute-start | bytes 393224 | tf_op jit(solution)/shard_map/ppermute | solution.py:327
  46.2 7.8 %collective-permute-start.9 = (bf16[128,512]{1,0:T(8,128)(2,1)S(1)}, bf16[128,512]{1,0:T(8,128)(2,1)S(1)}, u32[]{:S(2)}, u32[]{:S(2)}) collective-permute-start(bf16[128,512]{1,0:T(8,128)(2,1)S(1)} %collective-permute-done.5.table_3), channel_id=1, source_target_pairs={{0,1},{1,0},{2,3},{3,2},{4,5},{5,4},{6,7},{7,6},{8,9},{9,8},{10,11... | collective-permute-start | bytes 393224 | tf_op jit(solution)/shard_map/ppermute | solution.py:327
  46.2 0.7 %copy-start.4 = (s32[1,1024]{1,0:T(1,128)S(1)}, s32[1,1024]{1,0:T(1,128)}, u32[]{:S(2)}) copy-start(s32[1,1024]{1,0:T(1,128)} %src_ref.1) | copy-start | bytes 12292
  46.2 0.7 %copy-start.5 = (s32[1,1024]{1,0:T(1,128)S(1)}, s32[1,1024]{1,0:T(1,128)}, u32[]{:S(2)}) copy-start(s32[1,1024]{1,0:T(1,128)} %dst_ref.1) | copy-start | bytes 12292
  46.3 3.6 %collective-permute-start.1 = (bf16[16,512]{1,0:T(8,128)(2,1)S(1)}, bf16[16,512]{1,0:T(8,128)(2,1)S(1)}, u32[]{:S(2)}, u32[]{:S(2)}) collective-permute-start(bf16[16,512]{1,0:T(8,128)(2,1)S(1)} %shard_map.105), channel_id=1, source_target_pairs={{1,0},{2,1},{3,2},{4,3},{5,4},{6,5},{7,6},{8,7},{9,8},{10,9},{11,1... | collective-permute-start | bytes 49160 | tf_op jit(solution)/shard_map/ppermute | solution.py:305

commit v7 on v6

--- a/solution.py
+++ b/solution.py
@@ -116,20 +116,17 @@
         copy.wait()
 
 
-def fill_body(rows_0, rows_1, mid_in, mid_ref, wide, block, sems):
+def fill_body(rows_0, rows_1, mid_in, mid_ref, wide, block, sem):
     del mid_in
     for k, rows in enumerate((rows_0, rows_1)):
         wide[4 * k : 4 * k + 4, :] = rows[...].astype(F32)
     for k in range(4):
-        block[8 * k : 8 * k + 8, :] = wide[:, 128 * k : 128 * k + 128].astype(BF16)
-    copies = [
-        pltpu.make_async_copy(block, mid_ref.at[t, pl.ds(GATHERED, 32)], sems.at[t])
-        for t in range(16)
-    ]
-    for copy in copies:
-        copy.start()
-    for copy in copies:
-        copy.wait()
+        part = wide[:, 128 * k : 128 * k + 128].astype(BF16)
+        for t in range(16):
+            block[t, 8 * k : 8 * k + 8, :] = part
+    copy = pltpu.make_async_copy(block, mid_ref.at[:, pl.ds(GATHERED, 32)], sem)
+    copy.start()
+    copy.wait()
 
 
 def reduce_body(mid_ref, out_hbm, table_ref, out_ref, sem):
@@ -172,8 +169,9 @@
     src = src_ref[...]
     targets = onehot(128, dst_ref[...])
     hub = src - 160
-    table = (((hub >> 2) & 1) ^ core) * 4 + (((hub >> 4) & 1) ^ near) * 2 + (((hub >> 3) & 1) ^ side)
-    column = table * 128 + (hub >> 6) * 8 + (((hub >> 5) & 1) ^ far) * 4 + (hub & 3)
+    table = (((hub >> 2) & 1) ^ core) * 4 + (((hub >> 5) & 1) ^ far) * 2
+    table = table + (((hub >> 3) & 1) ^ side)
+    column = table * 128 + (hub >> 6) * 8 + (((hub >> 4) & 1) ^ near) * 4 + (hub & 3)
     column = jnp.where(hub < 0, -1, column)
     degree_ref[...] = jnp.broadcast_to(
         jnp.sum(targets.astype(F32), axis=1, keepdims=True), degree_ref.shape
@@ -272,7 +270,7 @@
     axes = ("core", "side", "near", "far")
     where = jnp.stack([lax.axis_index(axis) for axis in axes]).astype(I32)
     swap = [(0, 1), (1, 0)]
-    gathered = lax.ppermute(hub_feats, "far", swap)
+    gathered = lax.ppermute(hub_feats, "near", swap)
     mid = call(
         slots_body, pltpu.HBM((16, ROWS, 128), BF16), [HBM] * 4, 1 << 30, 2 << 20,
         out_specs=HBM,
@@ -292,8 +290,8 @@
         input_output_aliases={2: 0},
         scratch_shapes=[
             pltpu.VMEM((8, 512), F32),
-            pltpu.VMEM((32, 128), BF16),
-            pltpu.SemaphoreType.DMA((16,)),
+            pltpu.VMEM((16, 32, 128), BF16),
+            pltpu.SemaphoreType.DMA,
         ],
     )(hub_feats, gathered, mid)
     mid = lax.all_to_all(mid, OUTER, 0, 0, tiled=True)
@@ -318,8 +316,8 @@
         scratch_shapes=[pltpu.VMEM((16, 4, 640), BF16), pltpu.SemaphoreType.DMA],
     )(mid)
     table_1 = lax.ppermute(table_0, "side", swap)
-    table_2 = lax.ppermute(table_0, "near", swap)
-    table_3 = lax.ppermute(table_0, ("near", "side"), [(i, i ^ 3) for i in range(4)])
+    table_2 = lax.ppermute(table_0, "far", swap)
+    table_3 = lax.ppermute(table_0, ("far", "side"), [(i, i ^ 3) for i in range(4)])
     parts = lax.all_to_all(parts, INNER, 0, 0, tiled=True)
     tables = [table_0, table_1, table_2, table_3]
     others = []

time: 55.6 us -> 55.5 us (level)
  waiting for transfers between devices: 2.82 us -> 0.99 us
  starting transfers between devices: 22.7 us -> 24 us
    all_to_all x1, waiting for transfers between devices: 2.56 us -> 0.01 us  [on_device(): parts = lax.all_to_all(parts, INNER, 0, 0, tiled=True)]
    ppermute x3, starting transfers between devices: 10.6 us -> 8.19 us  [the longest x1 4 us: on_device(): table_2 = lax.ppermute(table_0, 'far', swap)]
    ppermute x4, starting transfers between devices: 1.64 us -> 3.32 us  [on_device(): others.append(lax.ppermute(table, 'core', swap))]
    ppermute x1, starting transfers between devices: 2.92 us -> 4.44 us  [on_device(): before = lax.ppermute(exports, DOM, forward)]
    ppermute x1, starting transfers between devices: 0.83 us -> 1.72 us  [on_device(): table_1 = lax.ppermute(table_0, 'side', swap)]
    ppermute x3, waiting for transfers between devices: 0.01 us -> 0.88 us  [the longest x1 0.87 us: on_device(): lax.ppermute(table_0, ('far', 'side'), [(i, i ^ 3) for i in range(4)])]
where the time goes in v7:
time: 55.5 us; the launch traced here: 55.2 us
  starting transfers between devices  24 us (43%)
  blocking collectives  18.8 us (34%)
  Pallas kernels  9.93 us (18%)
  waiting for transfers between devices  0.99 us (2%)
  between operations  0.75 us (1%)
  local copies, waits for them, and re-layouts  0.6 us (1%)
    all_to_all x1, blocking collectives, on_device(): mid = lax.all_to_all(mid, OUTER, 0, 0, tiled=True)  18.8 us
    all_to_all x1, starting transfers between devices, on_device(): parts = lax.all_to_all(parts, INNER, 0, 0, tiled=True)  6.33 us
    ppermute x1, starting transfers between devices, on_device(): before = lax.ppermute(exports, DOM, forward)  4.44 us
    ppermute x1, starting transfers between devices, on_device(): table_2 = lax.ppermute(table_0, 'far', swap)  4 us
    ppermute x1, starting transfers between devices, on_device(): gathered = lax.ppermute(hub_feats, 'near', swap)  3.9 us
    ppermute x4, starting transfers between devices, on_device(): others.append(lax.ppermute(table, 'core', swap))  3.32 us
    pallas_call x1, Pallas kernels, on_device(): call(counts_body, (shape(128, 1152), shape(128, 1152), shape(128, 128, dt...  2.75 us
    pallas_call x1, Pallas kernels, on_device(): call(slots_body, pltpu.HBM((16, ROWS, 128), BF16), [HBM] * 4, 1 << 30, 2...  2.66 us
  transfers between devices with their start and end apart: 11, of which 2 were waited for; matrix products, arithmetic and copies ran while one was open for 0% of the time, Pallas kernels for 13%

profile of v7, /device:TPU:1, one launch (start us, length us, event | category | flops | bytes accessed | tf_op | source)
XLA Modules:
  0.0 55.2 jit_solution(9558274062807801207)
XLA Ops:
  0.6 0.0 copy-start.2
  0.6 3.9 %collective-permute-start.2 = (bf16[4,512]{1,0:T(4,128)(2,1)}, bf16[4,512]{1,0:T(4,128)(2,1)S(1)}, u32[]{:S(2)}, u32[]{:S(2)}) collective-permute-start(bf16[4,512]{1,0:T(4,128)(2,1)} %rows_0.1), channel_id=1, source_target_pairs={{0,4},{4,0},{1,5},{5,1},{2,6},{6,2},{3,7},{7,3},{8,12},{12,8},{9,1... | collective-permute-start | bytes 12296 | tf_op jit(solution)/shard_map/ppermute | solution.py:273
  4.5 2.7 %shard_map.106.mid_in = bf16[16,168,128]{2,1,0:T(8,128)(2,1)} custom-call(s32[1,1024]{1,0:T(1,128)} %src_hbm.1, s32[1,1024]{1,0:T(1,128)} %slot_hbm.1, s32[1,512]{1,0:T(1,128)} %hub_hbm.1, bf16[128,512]{1,0:T(8,128)(2,1)} %feats_ref.5), custom_call_target="tpu_custom_call" | custom-call | flops 1073741824 | bytes 2097152 | tf_op jit(solution)/shard_map/pallas_call | solution.py:274
  7.2 0.0 collective-permute-done.2.rows_1
  7.2 0.0 copy-done.2
  7.2 0.7 %shard_map.107 = bf16[16,168,128]{2,1,0:T(8,128)(2,1)} custom-call(bf16[4,512]{1,0:T(4,128)(2,1)S(1)} %copy-done.2, bf16[4,512]{1,0:T(4,128)(2,1)S(1)} %collective-permute-done.2.rows_1, bf16[16,168,128]{2,1,0:T(8,128)(2,1)} %shard_map.106.mid_in), custom_call_target="tpu_custom_call", output_to_operand_aliasing={{}: (2, {})} | custom-call | bytes 1048576 | tf_op jit(solution)/shard_map/pallas_call | solution.py:287
  8.0 0.0 copy-start
  8.0 18.8 %all_to_all.10.mid_ref = bf16[16,168,128]{2,1,0:T(8,128)(2,1)S(1)} all-to-all(bf16[16,168,128]{2,1,0:T(8,128)(2,1)} %shard_map.107), channel_id=1, replica_groups=mesh['role'=4,'x'=4,'far'=2,'near'=2,'side'=2,'core'=2] {'role','x'}, dimensions={0} | all-to-all | bytes 1376256 | tf_op jit(solution)/shard_map/all_to_all | solution.py:297
  26.8 0.0 copy-start.1
  26.8 0.9 %shard_map.108 = (bf16[16,4,640]{2,1,0:T(4,128)(2,1)}, bf16[128,512]{1,0:T(8,128)(2,1)S(1)}) custom-call(bf16[16,168,128]{2,1,0:T(8,128)(2,1)S(1)} %all_to_all.10.mid_ref), custom_call_target="tpu_custom_call" | custom-call | flops 67108864 | bytes 2097152 | tf_op jit(solution)/shard_map/pallas_call | solution.py:312
  27.6 0.0 copy-start.3
  27.6 1.7 %collective-permute-start.3 = (bf16[128,512]{1,0:T(8,128)(2,1)S(1)}, bf16[128,512]{1,0:T(8,128)(2,1)S(1)}, u32[]{:S(2)}, u32[]{:S(2)}) collective-permute-start(bf16[128,512]{1,0:T(8,128)(2,1)S(1)} %get-tuple-element.15.table_0), channel_id=1, source_target_pairs={{0,2},{2,0},{1,3},{3,1},{4,6},{6,4},{5,7},{7,5},{8,10},{10,8},{9,1... | collective-permute-start | bytes 393224 | tf_op jit(solution)/shard_map/ppermute | solution.py:318
  29.4 4.0 %collective-permute-start.4 = (bf16[128,512]{1,0:T(8,128)(2,1)S(1)}, bf16[128,512]{1,0:T(8,128)(2,1)S(1)}, u32[]{:S(2)}, u32[]{:S(2)}) collective-permute-start(bf16[128,512]{1,0:T(8,128)(2,1)S(1)} %get-tuple-element.15.table_0), channel_id=1, source_target_pairs={{0,8},{8,0},{1,9},{9,1},{2,10},{10,2},{3,11},{11,3},{4,12},{12,4},... | collective-permute-start | bytes 393224 | tf_op jit(solution)/shard_map/ppermute | solution.py:319
  33.4 0.3 collective-permute-start.5
  33.7 0.0 copy-done.1
  33.7 0.0 copy-done.3
  33.7 0.2 shard_map.105
  33.8 4.4 %collective-permute-start = (bf16[16,512]{1,0:T(8,128)(2,1)S(1)}, bf16[16,512]{1,0:T(8,128)(2,1)S(1)}, u32[]{:S(2)}, u32[]{:S(2)}) collective-permute-start(bf16[16,512]{1,0:T(8,128)(2,1)S(1)} %shard_map.105), channel_id=1, source_target_pairs={{0,1},{1,2},{2,3},{3,4},{4,5},{5,6},{6,7},{7,8},{8,9},{9,10},{10,1... | collective-permute-start | bytes 49160 | tf_op jit(solution)/shard_map/ppermute | solution.py:302
  38.3 0.0 collective-permute-start.6
  38.3 6.3 %all-to-all-start.1 = ((bf16[16,4,640]{2,1,0:T(4,128)(2,1)}), bf16[16,4,640]{2,1,0:T(4,128)(2,1)S(1)}, u32[]{:S(2)}, u32[]{:S(2)}) async-start(bf16[16,4,640]{2,1,0:T(4,128)(2,1)} %get-tuple-element.18), calls=%async_computation.1 | async-start | bytes 163840 | tf_op jit(solution)/shard_map/all_to_all | solution.py:321
  44.6 0.0 collective-permute-done.3.table_1
  44.6 0.2 collective-permute-start.7
  44.8 0.0 collective-permute-done.4.table_2
  44.8 1.8 %collective-permute-start.8 = (bf16[128,512]{1,0:T(8,128)(2,1)S(1)}, bf16[128,512]{1,0:T(8,128)(2,1)S(1)}, u32[]{:S(2)}, u32[]{:S(2)}) collective-permute-start(bf16[128,512]{1,0:T(8,128)(2,1)S(1)} %collective-permute-done.4.table_2), channel_id=1, source_target_pairs={{0,1},{1,0},{2,3},{3,2},{4,5},{5,4},{6,7},{7,6},{8,9},{9,8},{10,11... | collective-permute-start | bytes 393224 | tf_op jit(solution)/shard_map/ppermute | solution.py:325
  46.6 0.9 %collective-permute-done.5.table_3 = bf16[128,512]{1,0:T(8,128)(2,1)S(1)} collective-permute-done((bf16[128,512]{1,0:T(8,128)(2,1)S(1)}, bf16[128,512]{1,0:T(8,128)(2,1)S(1)}, u32[]{:S(2)}, u32[]{:S(2)}) %collective-permute-start.5) | collective-permute-done | bytes 131104 | tf_op jit(solution)/shard_map/ppermute | solution.py:320
  47.5 1.3 %collective-permute-start.9 = (bf16[128,512]{1,0:T(8,128)(2,1)S(1)}, bf16[128,512]{1,0:T(8,128)(2,1)S(1)}, u32[]{:S(2)}, u32[]{:S(2)}) collective-permute-start(bf16[128,512]{1,0:T(8,128)(2,1)S(1)} %collective-permute-done.5.table_3), channel_id=1, source_target_pairs={{0,1},{1,0},{2,3},{3,2},{4,5},{5,4},{6,7},{7,6},{8,9},{9,8},{10,11... | collective-permute-start | bytes 393224 | tf_op jit(solution)/shard_map/ppermute | solution.py:325
  48.8 0.0 copy-start.4
  48.8 0.0 copy-start.5
  48.8 0.1 pad_add_fusion.where_ref
  48.9 0.0 collective-permute-done.before_ref
  48.9 0.0 collective-permute-start.1
  48.9 0.0 copy-done
  48.9 0.6 %copy-done.4 = s32[1,1024]{1,0:T(1,128)S(1)} copy-done((s32[1,1024]{1,0:T(1,128)S(1)}, s32[1,1024]{1,0:T(1,128)}, u32[]{:S(2)}) %copy-start.4) | copy-done | bytes 4120
  49.5 0.0 copy-done.5
  49.5 2.8 %shard_map.104 = (bf16[128,1152]{1,0:T(8,128)(2,1)S(1)}, bf16[128,1152]{1,0:T(8,128)(2,1)S(1)}, f32[128,128]{1,0:T(8,128)S(1)}, f32[4,512]{1,0:T(4,128)S(1)}, f32[128,512]{1,0:T(8,128)S(1)}) custom-call(s32[4]{0:T(128)S(1)} %pad_add_fusion.where_ref, s32[1,1024]{1,0:T(1,128)S(1)} %copy-done.4, s32[1,1024]{1,0:T(1,128)S(1)} %copy-done.5, ...), custom_call_target="tpu_custom_call" | custom-call | flops 1073741824 | bytes 2097152 | tf_op jit(solution)/shard_map/pallas_call | solution.py:304
  52.3 0.1 collective-permute-done.1.after_ref
  52.4 0.5 shard_map.109
  52.9 0.0 all-to-all-done.1.parts_ref
  52.9 1.0 %shard_map.111 = bf16[4,512]{1,0:T(4,128)(2,1)} custom-call(bf16[16,4,640]{2,1,0:T(4,128)(2,1)S(1)} %all-to-all-done.1.parts_ref, f32[4,512]{1,0:T(4,128)S(1)} %get-tuple-element.19.linear_ref, bf16[1024,512]{1,0:T(8,128)(2,1)S(1)} %copy-done), custom_call_target="tpu_custom_call" | custom-call | flops 4194304 | bytes 524288 | tf_op jit(solution)/shard_map/pallas_call | solution.py:333
  53.9 0.0 collective-permute-done.6.table_4
  53.9 0.0 collective-permute-done.7.table_5
  53.9 0.0 collective-permute-done.8.table_6
  53.9 0.0 collective-permute-done.9.table_7
  53.9 1.3 %shard_map.110 = bf16[128,512]{1,0:T(8,128)(2,1)} custom-call(bf16[128,1152]{1,0:T(8,128)(2,1)S(1)} %get-tuple-element.11.low_ref, bf16[128,1152]{1,0:T(8,128)(2,1)S(1)} %get-tuple-element.12.high_ref, f32[128,128]{1,0:T(8,128)S(1)} %get-tuple-element.13.degree_ref, f32[128,512]{1,0:T(8,128)S(1)} %get-tuple-element.16.total_ref, ...), custom_call_target="tpu_custom_call" | custom-call | flops 268435456 | bytes 1048576 | tf_op jit(solution)/shard_map/pallas_call | solution.py:330
Async XLA Ops:
  0.6 6.6 %copy-start.2 = (bf16[4,512]{1,0:T(4,128)(2,1)S(1)}, bf16[4,512]{1,0:T(4,128)(2,1)}, u32[]{:S(2)}) copy-start(bf16[4,512]{1,0:T(4,128)(2,1)} %rows_0.1) | copy-start | bytes 12292
  0.6 6.6 %collective-permute-start.2 = (bf16[4,512]{1,0:T(4,128)(2,1)}, bf16[4,512]{1,0:T(4,128)(2,1)S(1)}, u32[]{:S(2)}, u32[]{:S(2)}) collective-permute-start(bf16[4,512]{1,0:T(4,128)(2,1)} %rows_0.1), channel_id=1, source_target_pairs={{0,4},{4,0},{1,5},{5,1},{2,6},{6,2},{3,7},{7,3},{8,12},{12,8},{9,1... | collective-permute-start | bytes 12296 | tf_op jit(solution)/shard_map/ppermute | solution.py:273
  8.0 41.0 %copy-start = (bf16[1024,512]{1,0:T(8,128)(2,1)S(1)}, bf16[1024,512]{1,0:T(8,128)(2,1)}, u32[]{:S(2)}) copy-start(bf16[1024,512]{1,0:T(8,128)(2,1)} %weight_ref.7) | copy-start | bytes 3145732
  26.8 6.9 %copy-start.1 = (bf16[128,512]{1,0:T(8,128)(2,1)S(1)}, bf16[128,512]{1,0:T(8,128)(2,1)}, u32[]{:S(2)}) copy-start(bf16[128,512]{1,0:T(8,128)(2,1)} %feats_ref.5) | copy-start | bytes 393220
  27.6 6.0 %copy-start.3 = (s32[1,16]{1,0:T(1,128)S(1)}, s32[1,16]{1,0:T(1,128)}, u32[]{:S(2)}) copy-start(s32[1,16]{1,0:T(1,128)} %bound_ref.1) | copy-start | bytes 196
  27.6 17.0 %collective-permute-start.3 = (bf16[128,512]{1,0:T(8,128)(2,1)S(1)}, bf16[128,512]{1,0:T(8,128)(2,1)S(1)}, u32[]{:S(2)}, u32[]{:S(2)}) collective-permute-start(bf16[128,512]{1,0:T(8,128)(2,1)S(1)} %get-tuple-element.15.table_0), channel_id=1, source_target_pairs={{0,2},{2,0},{1,3},{3,1},{4,6},{6,4},{5,7},{7,5},{8,10},{10,8},{9,1... | collective-permute-start | bytes 393224 | tf_op jit(solution)/shard_map/ppermute | solution.py:318
  29.4 15.4 %collective-permute-start.4 = (bf16[128,512]{1,0:T(8,128)(2,1)S(1)}, bf16[128,512]{1,0:T(8,128)(2,1)S(1)}, u32[]{:S(2)}, u32[]{:S(2)}) collective-permute-start(bf16[128,512]{1,0:T(8,128)(2,1)S(1)} %get-tuple-element.15.table_0), channel_id=1, source_target_pairs={{0,8},{8,0},{1,9},{9,1},{2,10},{10,2},{3,11},{11,3},{4,12},{12,4},... | collective-permute-start | bytes 393224 | tf_op jit(solution)/shard_map/ppermute | solution.py:319
  33.4 14.1 %collective-permute-start.5 = (bf16[128,512]{1,0:T(8,128)(2,1)S(1)}, bf16[128,512]{1,0:T(8,128)(2,1)S(1)}, u32[]{:S(2)}, u32[]{:S(2)}) collective-permute-start(bf16[128,512]{1,0:T(8,128)(2,1)S(1)} %get-tuple-element.15.table_0), channel_id=1, source_target_pairs={{0,10},{2,8},{8,2},{10,0},{1,11},{3,9},{9,3},{11,1},{4,14},{6,12},... | collective-permute-start | bytes 393224 | tf_op jit(solution)/shard_map/ppermute | solution.py:320
  33.8 15.1 %collective-permute-start = (bf16[16,512]{1,0:T(8,128)(2,1)S(1)}, bf16[16,512]{1,0:T(8,128)(2,1)S(1)}, u32[]{:S(2)}, u32[]{:S(2)}) collective-permute-start(bf16[16,512]{1,0:T(8,128)(2,1)S(1)} %shard_map.105), channel_id=1, source_target_pairs={{0,1},{1,2},{2,3},{3,4},{4,5},{5,6},{6,7},{7,8},{8,9},{9,10},{10,1... | collective-permute-start | bytes 49160 | tf_op jit(solution)/shard_map/ppermute | solution.py:302
  38.3 15.6 %collective-permute-start.6 = (bf16[128,512]{1,0:T(8,128)(2,1)S(1)}, bf16[128,512]{1,0:T(8,128)(2,1)S(1)}, u32[]{:S(2)}, u32[]{:S(2)}) collective-permute-start(bf16[128,512]{1,0:T(8,128)(2,1)S(1)} %get-tuple-element.15.table_0), channel_id=1, source_target_pairs={{0,1},{1,0},{2,3},{3,2},{4,5},{5,4},{6,7},{7,6},{8,9},{9,8},{10,11... | collective-permute-start | bytes 393224 | tf_op jit(solution)/shard_map/ppermute | solution.py:325
  38.3 14.6 %all-to-all-start.1 = ((bf16[16,4,640]{2,1,0:T(4,128)(2,1)}), bf16[16,4,640]{2,1,0:T(4,128)(2,1)S(1)}, u32[]{:S(2)}, u32[]{:S(2)}) async-start(bf16[16,4,640]{2,1,0:T(4,128)(2,1)} %get-tuple-element.18), calls=%async_computation.1 | async-start | bytes 163840 | tf_op jit(solution)/shard_map/all_to_all | solution.py:321
  44.6 9.3 %collective-permute-start.7 = (bf16[128,512]{1,0:T(8,128)(2,1)S(1)}, bf16[128,512]{1,0:T(8,128)(2,1)S(1)}, u32[]{:S(2)}, u32[]{:S(2)}) collective-permute-start(bf16[128,512]{1,0:T(8,128)(2,1)S(1)} %collective-permute-done.3.table_1), channel_id=1, source_target_pairs={{0,1},{1,0},{2,3},{3,2},{4,5},{5,4},{6,7},{7,6},{8,9},{9,8},{10,11... | collective-permute-start | bytes 393224 | tf_op jit(solution)/shard_map/ppermute | solution.py:325
  44.8 9.1 %collective-permute-start.8 = (bf16[128,512]{1,0:T(8,128)(2,1)S(1)}, bf16[128,512]{1,0:T(8,128)(2,1)S(1)}, u32[]{:S(2)}, u32[]{:S(2)}) collective-permute-start(bf16[128,512]{1,0:T(8,128)(2,1)S(1)} %collective-permute-done.4.table_2), channel_id=1, source_target_pairs={{0,1},{1,0},{2,3},{3,2},{4,5},{5,4},{6,7},{7,6},{8,9},{9,8},{10,11... | collective-permute-start | bytes 393224 | tf_op jit(solution)/shard_map/ppermute | solution.py:325
  47.5 6.4 %collective-permute-start.9 = (bf16[128,512]{1,0:T(8,128)(2,1)S(1)}, bf16[128,512]{1,0:T(8,128)(2,1)S(1)}, u32[]{:S(2)}, u32[]{:S(2)}) collective-permute-start(bf16[128,512]{1,0:T(8,128)(2,1)S(1)} %collective-permute-done.5.table_3), channel_id=1, source_target_pairs={{0,1},{1,0},{2,3},{3,2},{4,5},{5,4},{6,7},{7,6},{8,9},{9,8},{10,11... | collective-permute-start | bytes 393224 | tf_op jit(solution)/shard_map/ppermute | solution.py:325
  48.8 0.7 %copy-start.4 = (s32[1,1024]{1,0:T(1,128)S(1)}, s32[1,1024]{1,0:T(1,128)}, u32[]{:S(2)}) copy-start(s32[1,1024]{1,0:T(1,128)} %src_ref.1) | copy-start | bytes 12292
  48.8 0.7 %copy-start.5 = (s32[1,1024]{1,0:T(1,128)S(1)}, s32[1,1024]{1,0:T(1,128)}, u32[]{:S(2)}) copy-start(s32[1,1024]{1,0:T(1,128)} %dst_ref.1) | copy-start | bytes 12292
  48.9 3.5 %collective-permute-start.1 = (bf16[16,512]{1,0:T(8,128)(2,1)S(1)}, bf16[16,512]{1,0:T(8,128)(2,1)S(1)}, u32[]{:S(2)}, u32[]{:S(2)}) collective-permute-start(bf16[16,512]{1,0:T(8,128)(2,1)S(1)} %shard_map.105), channel_id=1, source_target_pairs={{1,0},{2,1},{3,2},{4,3},{5,4},{6,5},{7,6},{8,7},{9,8},{10,9},{11,1... | collective-permute-start | bytes 49160 | tf_op jit(solution)/shard_map/ppermute | solution.py:303

commit v8 on v7

--- a/solution.py
+++ b/solution.py
@@ -7,6 +7,7 @@
 from jax.sharding import PartitionSpec as P
 
 
+Z = ("far", "near", "side")
 INNER = ("far", "near", "side", "core")
 OUTER = ("role", "x")
 DOM = ("x", "far", "near", "side", "core")
@@ -27,7 +28,9 @@
 
 def onehot(rows, index, first=0):
     shape = (rows, index.shape[1])
-    return jnp.where(lax.broadcasted_iota(I32, shape, 0) + first == index, 1.0, 0.0).astype(BF16)
+    row = lax.broadcasted_iota(jnp.int16, shape, 0)
+    place = jnp.broadcast_to(index - first, shape).astype(jnp.int16)
+    return jnp.where(row == place, jnp.ones(shape, BF16), jnp.zeros(shape, BF16))
 
 
 def split_count(count):
@@ -163,15 +166,16 @@
     low_ref, high_ref, degree_ref, hub_linear_ref, partial_ref,
 ):
     core = where_ref[0]
-    side = where_ref[1]
-    near = where_ref[2]
-    far = where_ref[3]
+    z = where_ref[1]
     src = src_ref[...]
     targets = onehot(128, dst_ref[...])
     hub = src - 160
-    table = (((hub >> 2) & 1) ^ core) * 4 + (((hub >> 5) & 1) ^ far) * 2
-    table = table + (((hub >> 3) & 1) ^ side)
-    column = table * 128 + (hub >> 6) * 8 + (((hub >> 4) & 1) ^ near) * 4 + (hub & 3)
+    ahead = ((hub >> 3) - z) & 7
+    turn = ahead >> 1
+    table = jnp.where(turn > 1, 5 - turn, turn)
+    part = ahead & 1
+    table = table + (((hub >> 2) & 1) ^ core) * 4
+    column = table * 128 + (hub >> 6) * 8 + part * 4 + (hub & 3)
     column = jnp.where(hub < 0, -1, column)
     degree_ref[...] = jnp.broadcast_to(
         jnp.sum(targets.astype(F32), axis=1, keepdims=True), degree_ref.shape
@@ -267,10 +271,14 @@
     node_feats, hub_feats, weight, edge_src, edge_dst, bound_rows,
     hub_edge_src, hub_edge_slot, slot_hub,
 ):
-    axes = ("core", "side", "near", "far")
-    where = jnp.stack([lax.axis_index(axis) for axis in axes]).astype(I32)
+    where = jnp.stack([lax.axis_index("core"), lax.axis_index(Z)]).astype(I32)
     swap = [(0, 1), (1, 0)]
-    gathered = lax.ppermute(hub_feats, "near", swap)
+    planes = lax.axis_size(Z)
+
+    def from_plane(value, step):
+        return lax.ppermute(value, Z, [(i, (i - step) % planes) for i in range(planes)])
+
+    gathered = from_plane(hub_feats, 1)
     mid = call(
         slots_body, pltpu.HBM((16, ROWS, 128), BF16), [HBM] * 4, 1 << 30, 2 << 20,
         out_specs=HBM,
@@ -315,9 +323,9 @@
         out_specs=(HBM, VMEM),
         scratch_shapes=[pltpu.VMEM((16, 4, 640), BF16), pltpu.SemaphoreType.DMA],
     )(mid)
-    table_1 = lax.ppermute(table_0, "side", swap)
-    table_2 = lax.ppermute(table_0, "far", swap)
-    table_3 = lax.ppermute(table_0, ("far", "side"), [(i, i ^ 3) for i in range(4)])
+    table_1 = from_plane(table_0, 2)
+    table_2 = from_plane(table_0, -2)
+    table_3 = from_plane(table_0, 4)
     parts = lax.all_to_all(parts, INNER, 0, 0, tiled=True)
     tables = [table_0, table_1, table_2, table_3]
     others = []

time: 55.5 us -> 54.6 us (0.984)
  waiting for transfers between devices: 0.99 us -> 0.41 us
  local copies, waits for them, and re-layouts: 0.6 us -> 0.03 us
    ppermute x1, starting transfers between devices: 0.03 us -> 1.76 us  [on_device(): after = lax.ppermute(exports, DOM, backward)]
    all_to_all x1, starting transfers between devices: 6.33 us -> 5.12 us  [on_device(): parts = lax.all_to_all(parts, INNER, 0, 0, tiled=True)]
    ppermute x4, waiting for transfers between devices: 0.88 us -> 0.01 us  [from_plane(): lax.ppermute(value, Z, [(i, (i - step) % planes) for i in range(planes)])]
    ppermute x4, starting transfers between devices: 3.32 us -> 2.68 us  [on_device(): others.append(lax.ppermute(table, 'core', swap))]
    ppermute x1, starting transfers between devices: 4.44 us -> 5.03 us  [on_device(): before = lax.ppermute(exports, DOM, forward)]
    unnamed x12, local copies, waits for them, and re-layouts: 0.6 us -> 0.03 us
where the time goes in v8:
time: 54.6 us; the launch traced here: 54.3 us
  starting transfers between devices  24.4 us (45%)
  blocking collectives  18.8 us (34%)
  Pallas kernels  9.86 us (18%)
  between operations  0.74 us (1%)
    all_to_all x1, blocking collectives, on_device(): mid = lax.all_to_all(mid, OUTER, 0, 0, tiled=True)  18.8 us
    ppermute x4, starting transfers between devices, from_plane(): lax.ppermute(value, Z, [(i, (i - step) % planes) for i in range(planes)])  9.77 us
    all_to_all x1, starting transfers between devices, on_device(): parts = lax.all_to_all(parts, INNER, 0, 0, tiled=True)  5.12 us
    ppermute x1, starting transfers between devices, on_device(): before = lax.ppermute(exports, DOM, forward)  5.03 us
    pallas_call x1, Pallas kernels, on_device(): call(counts_body, (shape(128, 1152), shape(128, 1152), shape(128, 128, dt...  2.7 us
    ppermute x4, starting transfers between devices, on_device(): others.append(lax.ppermute(table, 'core', swap))  2.68 us
    pallas_call x1, Pallas kernels, on_device(): call(slots_body, pltpu.HBM((16, ROWS, 128), BF16), [HBM] * 4, 1 << 30, 2...  2.65 us
    ppermute x1, starting transfers between devices, on_device(): after = lax.ppermute(exports, DOM, backward)  1.76 us
  transfers between devices with their start and end apart: 11, of which 2 were waited for; matrix products, arithmetic and copies ran while one was open for 0% of the time, Pallas kernels for 13%

profile of v8, /device:TPU:1, one launch (start us, length us, event | category | flops | bytes accessed | tf_op | source)
XLA Modules:
  0.0 54.3 jit_solution(1016950885713976762)
XLA Ops:
  0.6 0.0 copy-start.2
  0.6 6.5 %collective-permute-start.2 = (bf16[4,512]{1,0:T(4,128)(2,1)}, bf16[4,512]{1,0:T(4,128)(2,1)S(1)}, u32[]{:S(2)}, u32[]{:S(2)}) collective-permute-start(bf16[4,512]{1,0:T(4,128)(2,1)} %rows_0.1), channel_id=1, source_target_pairs={{0,14},{2,0},{4,2},{6,4},{8,6},{10,8},{12,10},{14,12},{1,15},{3,1}... | collective-permute-start | bytes 12296 | tf_op jit(solution)/shard_map/ppermute | solution.py:279
  7.1 2.7 %shard_map.106.mid_in = bf16[16,168,128]{2,1,0:T(8,128)(2,1)} custom-call(s32[1,1024]{1,0:T(1,128)} %src_hbm.1, s32[1,1024]{1,0:T(1,128)} %slot_hbm.1, s32[1,512]{1,0:T(1,128)} %hub_hbm.1, bf16[128,512]{1,0:T(8,128)(2,1)} %feats_ref.5), custom_call_target="tpu_custom_call" | custom-call | flops 1073741824 | bytes 2097152 | tf_op jit(solution)/shard_map/pallas_call | solution.py:282
  9.8 0.0 collective-permute-done.2.rows_1
  9.8 0.0 copy-done.2
  9.8 0.7 %shard_map.107 = bf16[16,168,128]{2,1,0:T(8,128)(2,1)} custom-call(bf16[4,512]{1,0:T(4,128)(2,1)S(1)} %copy-done.2, bf16[4,512]{1,0:T(4,128)(2,1)S(1)} %collective-permute-done.2.rows_1, bf16[16,168,128]{2,1,0:T(8,128)(2,1)} %shard_map.106.mid_in), custom_call_target="tpu_custom_call", output_to_operand_aliasing={{}: (2, {})} | custom-call | bytes 1048576 | tf_op jit(solution)/shard_map/pallas_call | solution.py:295
  10.5 0.0 copy-start
  10.5 18.8 %all_to_all.10.mid_ref = bf16[16,168,128]{2,1,0:T(8,128)(2,1)S(1)} all-to-all(bf16[16,168,128]{2,1,0:T(8,128)(2,1)} %shard_map.107), channel_id=1, replica_groups=mesh['role'=4,'x'=4,'far'=2,'near'=2,'side'=2,'core'=2] {'role','x'}, dimensions={0} | all-to-all | bytes 1376256 | tf_op jit(solution)/shard_map/all_to_all | solution.py:305
  29.3 0.0 copy-start.1
  29.3 0.9 %shard_map.108 = (bf16[16,4,640]{2,1,0:T(4,128)(2,1)}, bf16[128,512]{1,0:T(8,128)(2,1)S(1)}) custom-call(bf16[16,168,128]{2,1,0:T(8,128)(2,1)S(1)} %all_to_all.10.mid_ref), custom_call_target="tpu_custom_call" | custom-call | flops 67108864 | bytes 2097152 | tf_op jit(solution)/shard_map/pallas_call | solution.py:320
  30.2 0.0 copy-start.3
  30.2 1.1 %collective-permute-start.3 = (bf16[128,512]{1,0:T(8,128)(2,1)S(1)}, bf16[128,512]{1,0:T(8,128)(2,1)S(1)}, u32[]{:S(2)}, u32[]{:S(2)}) collective-permute-start(bf16[128,512]{1,0:T(8,128)(2,1)S(1)} %get-tuple-element.15.table_0), channel_id=1, source_target_pairs={{0,12},{2,14},{4,0},{6,2},{8,4},{10,6},{12,8},{14,10},{1,13},{3,15... | collective-permute-start | bytes 393224 | tf_op jit(solution)/shard_map/ppermute | solution.py:279
  31.3 1.3 %collective-permute-start.4 = (bf16[128,512]{1,0:T(8,128)(2,1)S(1)}, bf16[128,512]{1,0:T(8,128)(2,1)S(1)}, u32[]{:S(2)}, u32[]{:S(2)}) collective-permute-start(bf16[128,512]{1,0:T(8,128)(2,1)S(1)} %get-tuple-element.15.table_0), channel_id=1, source_target_pairs={{0,4},{2,6},{4,8},{6,10},{8,12},{10,14},{12,0},{14,2},{1,5},{3,7},... | collective-permute-start | bytes 393224 | tf_op jit(solution)/shard_map/ppermute | solution.py:279
  32.7 0.9 %collective-permute-start.5 = (bf16[128,512]{1,0:T(8,128)(2,1)S(1)}, bf16[128,512]{1,0:T(8,128)(2,1)S(1)}, u32[]{:S(2)}, u32[]{:S(2)}) collective-permute-start(bf16[128,512]{1,0:T(8,128)(2,1)S(1)} %get-tuple-element.15.table_0), channel_id=1, source_target_pairs={{0,8},{2,10},{4,12},{6,14},{8,0},{10,2},{12,4},{14,6},{1,9},{3,11}... | collective-permute-start | bytes 393224 | tf_op jit(solution)/shard_map/ppermute | solution.py:279
  33.5 0.0 copy-done.1
  33.5 0.0 copy-done.3
  33.5 0.2 shard_map.105
  33.7 5.0 %collective-permute-start = (bf16[16,512]{1,0:T(8,128)(2,1)S(1)}, bf16[16,512]{1,0:T(8,128)(2,1)S(1)}, u32[]{:S(2)}, u32[]{:S(2)}) collective-permute-start(bf16[16,512]{1,0:T(8,128)(2,1)S(1)} %shard_map.105), channel_id=1, source_target_pairs={{0,1},{1,2},{2,3},{3,4},{4,5},{5,6},{6,7},{7,8},{8,9},{9,10},{10,1... | collective-permute-start | bytes 49160 | tf_op jit(solution)/shard_map/ppermute | solution.py:310
  38.7 0.0 collective-permute-start.6
  38.7 0.0 copy-start.5
  38.7 5.1 %all-to-all-start.1 = ((bf16[16,4,640]{2,1,0:T(4,128)(2,1)}), bf16[16,4,640]{2,1,0:T(4,128)(2,1)S(1)}, u32[]{:S(2)}, u32[]{:S(2)}) async-start(bf16[16,4,640]{2,1,0:T(4,128)(2,1)} %get-tuple-element.18), calls=%async_computation.1 | async-start | bytes 163840 | tf_op jit(solution)/shard_map/all_to_all | solution.py:329
  43.8 0.0 copy-start.4
  43.8 0.0 collective-permute-done.3.table_1
  43.9 0.2 collective-permute-start.7
  44.0 0.0 collective-permute-done.4.table_2
  44.1 2.3 %collective-permute-start.8 = (bf16[128,512]{1,0:T(8,128)(2,1)S(1)}, bf16[128,512]{1,0:T(8,128)(2,1)S(1)}, u32[]{:S(2)}, u32[]{:S(2)}) collective-permute-start(bf16[128,512]{1,0:T(8,128)(2,1)S(1)} %collective-permute-done.4.table_2), channel_id=1, source_target_pairs={{0,1},{1,0},{2,3},{3,2},{4,5},{5,4},{6,7},{7,6},{8,9},{9,8},{10,11... | collective-permute-start | bytes 393224 | tf_op jit(solution)/shard_map/ppermute | solution.py:333
  46.3 0.0 collective-permute-done.5.table_3
  46.3 0.2 collective-permute-start.9
  46.5 0.1 pad_add_fusion.where_ref
  46.6 0.0 collective-permute-done.before_ref
  46.6 1.8 %collective-permute-start.1 = (bf16[16,512]{1,0:T(8,128)(2,1)S(1)}, bf16[16,512]{1,0:T(8,128)(2,1)S(1)}, u32[]{:S(2)}, u32[]{:S(2)}) collective-permute-start(bf16[16,512]{1,0:T(8,128)(2,1)S(1)} %shard_map.105), channel_id=1, source_target_pairs={{1,0},{2,1},{3,2},{4,3},{5,4},{6,5},{7,6},{8,7},{9,8},{10,9},{11,1... | collective-permute-start | bytes 49160 | tf_op jit(solution)/shard_map/ppermute | solution.py:311
  48.4 0.0 copy-done
  48.4 0.0 copy-done.5
  48.4 0.0 copy-done.4
  48.4 2.7 %shard_map.104 = (bf16[128,1152]{1,0:T(8,128)(2,1)S(1)}, bf16[128,1152]{1,0:T(8,128)(2,1)S(1)}, f32[128,128]{1,0:T(8,128)S(1)}, f32[4,512]{1,0:T(4,128)S(1)}, f32[128,512]{1,0:T(8,128)S(1)}) custom-call(s32[2]{0:T(128)S(1)} %pad_add_fusion.where_ref, s32[1,1024]{1,0:T(1,128)S(1)} %copy-done.4, s32[1,1024]{1,0:T(1,128)S(1)} %copy-done.5, ...), custom_call_target="tpu_custom_call" | custom-call | flops 1073741824 | bytes 2097152 | tf_op jit(solution)/shard_map/pallas_call | solution.py:312
  51.1 0.3 collective-permute-done.1.after_ref
  51.4 0.5 shard_map.109
  51.9 0.1 all-to-all-done.1.parts_ref
  52.0 1.0 %shard_map.111 = bf16[4,512]{1,0:T(4,128)(2,1)} custom-call(bf16[16,4,640]{2,1,0:T(4,128)(2,1)S(1)} %all-to-all-done.1.parts_ref, f32[4,512]{1,0:T(4,128)S(1)} %get-tuple-element.19.linear_ref, bf16[1024,512]{1,0:T(8,128)(2,1)S(1)} %copy-done), custom_call_target="tpu_custom_call" | custom-call | flops 4194304 | bytes 524288 | tf_op jit(solution)/shard_map/pallas_call | solution.py:341
  53.0 0.0 collective-permute-done.6.table_4
  53.0 0.0 collective-permute-done.7.table_5
  53.0 0.0 collective-permute-done.8.table_6
  53.0 0.0 collective-permute-done.9.table_7
  53.0 1.3 %shard_map.110 = bf16[128,512]{1,0:T(8,128)(2,1)} custom-call(bf16[128,1152]{1,0:T(8,128)(2,1)S(1)} %get-tuple-element.11.low_ref, bf16[128,1152]{1,0:T(8,128)(2,1)S(1)} %get-tuple-element.12.high_ref, f32[128,128]{1,0:T(8,128)S(1)} %get-tuple-element.13.degree_ref, f32[128,512]{1,0:T(8,128)S(1)} %get-tuple-element.16.total_ref, ...), custom_call_target="tpu_custom_call" | custom-call | flops 268435456 | bytes 1048576 | tf_op jit(solution)/shard_map/pallas_call | solution.py:338
Async XLA Ops:
  0.6 9.2 %copy-start.2 = (bf16[4,512]{1,0:T(4,128)(2,1)S(1)}, bf16[4,512]{1,0:T(4,128)(2,1)}, u32[]{:S(2)}) copy-start(bf16[4,512]{1,0:T(4,128)(2,1)} %rows_0.1) | copy-start | bytes 12292
  0.6 9.1 %collective-permute-start.2 = (bf16[4,512]{1,0:T(4,128)(2,1)}, bf16[4,512]{1,0:T(4,128)(2,1)S(1)}, u32[]{:S(2)}, u32[]{:S(2)}) collective-permute-start(bf16[4,512]{1,0:T(4,128)(2,1)} %rows_0.1), channel_id=1, source_target_pairs={{0,14},{2,0},{4,2},{6,4},{8,6},{10,8},{12,10},{14,12},{1,15},{3,1}... | collective-permute-start | bytes 12296 | tf_op jit(solution)/shard_map/ppermute | solution.py:279
  10.5 37.9 %copy-start = (bf16[1024,512]{1,0:T(8,128)(2,1)S(1)}, bf16[1024,512]{1,0:T(8,128)(2,1)}, u32[]{:S(2)}) copy-start(bf16[1024,512]{1,0:T(8,128)(2,1)} %weight_ref.7) | copy-start | bytes 3145732
  29.3 4.2 %copy-start.1 = (bf16[128,512]{1,0:T(8,128)(2,1)S(1)}, bf16[128,512]{1,0:T(8,128)(2,1)}, u32[]{:S(2)}) copy-start(bf16[128,512]{1,0:T(8,128)(2,1)} %feats_ref.5) | copy-start | bytes 393220
  30.2 3.3 %copy-start.3 = (s32[1,16]{1,0:T(1,128)S(1)}, s32[1,16]{1,0:T(1,128)}, u32[]{:S(2)}) copy-start(s32[1,16]{1,0:T(1,128)} %bound_ref.1) | copy-start | bytes 196
  30.2 13.6 %collective-permute-start.3 = (bf16[128,512]{1,0:T(8,128)(2,1)S(1)}, bf16[128,512]{1,0:T(8,128)(2,1)S(1)}, u32[]{:S(2)}, u32[]{:S(2)}) collective-permute-start(bf16[128,512]{1,0:T(8,128)(2,1)S(1)} %get-tuple-element.15.table_0), channel_id=1, source_target_pairs={{0,12},{2,14},{4,0},{6,2},{8,4},{10,6},{12,8},{14,10},{1,13},{3,15... | collective-permute-start | bytes 393224 | tf_op jit(solution)/shard_map/ppermute | solution.py:279
  31.3 12.7 %collective-permute-start.4 = (bf16[128,512]{1,0:T(8,128)(2,1)S(1)}, bf16[128,512]{1,0:T(8,128)(2,1)S(1)}, u32[]{:S(2)}, u32[]{:S(2)}) collective-permute-start(bf16[128,512]{1,0:T(8,128)(2,1)S(1)} %get-tuple-element.15.table_0), channel_id=1, source_target_pairs={{0,4},{2,6},{4,8},{6,10},{8,12},{10,14},{12,0},{14,2},{1,5},{3,7},... | collective-permute-start | bytes 393224 | tf_op jit(solution)/shard_map/ppermute | solution.py:279
  32.7 13.7 %collective-permute-start.5 = (bf16[128,512]{1,0:T(8,128)(2,1)S(1)}, bf16[128,512]{1,0:T(8,128)(2,1)S(1)}, u32[]{:S(2)}, u32[]{:S(2)}) collective-permute-start(bf16[128,512]{1,0:T(8,128)(2,1)S(1)} %get-tuple-element.15.table_0), channel_id=1, source_target_pairs={{0,8},{2,10},{4,12},{6,14},{8,0},{10,2},{12,4},{14,6},{1,9},{3,11}... | collective-permute-start | bytes 393224 | tf_op jit(solution)/shard_map/ppermute | solution.py:279
  33.7 12.9 %collective-permute-start = (bf16[16,512]{1,0:T(8,128)(2,1)S(1)}, bf16[16,512]{1,0:T(8,128)(2,1)S(1)}, u32[]{:S(2)}, u32[]{:S(2)}) collective-permute-start(bf16[16,512]{1,0:T(8,128)(2,1)S(1)} %shard_map.105), channel_id=1, source_target_pairs={{0,1},{1,2},{2,3},{3,4},{4,5},{5,6},{6,7},{7,8},{8,9},{9,10},{10,1... | collective-permute-start | bytes 49160 | tf_op jit(solution)/shard_map/ppermute | solution.py:310
  38.7 14.3 %collective-permute-start.6 = (bf16[128,512]{1,0:T(8,128)(2,1)S(1)}, bf16[128,512]{1,0:T(8,128)(2,1)S(1)}, u32[]{:S(2)}, u32[]{:S(2)}) collective-permute-start(bf16[128,512]{1,0:T(8,128)(2,1)S(1)} %get-tuple-element.15.table_0), channel_id=1, source_target_pairs={{0,1},{1,0},{2,3},{3,2},{4,5},{5,4},{6,7},{7,6},{8,9},{9,8},{10,11... | collective-permute-start | bytes 393224 | tf_op jit(solution)/shard_map/ppermute | solution.py:333
  38.7 9.7 %copy-start.5 = (s32[1,1024]{1,0:T(1,128)S(1)}, s32[1,1024]{1,0:T(1,128)}, u32[]{:S(2)}) copy-start(s32[1,1024]{1,0:T(1,128)} %dst_ref.1) | copy-start | bytes 12292
  38.7 13.3 %all-to-all-start.1 = ((bf16[16,4,640]{2,1,0:T(4,128)(2,1)}), bf16[16,4,640]{2,1,0:T(4,128)(2,1)S(1)}, u32[]{:S(2)}, u32[]{:S(2)}) async-start(bf16[16,4,640]{2,1,0:T(4,128)(2,1)} %get-tuple-element.18), calls=%async_computation.1 | async-start | bytes 163840 | tf_op jit(solution)/shard_map/all_to_all | solution.py:329
  43.8 4.5 %copy-start.4 = (s32[1,1024]{1,0:T(1,128)S(1)}, s32[1,1024]{1,0:T(1,128)}, u32[]{:S(2)}) copy-start(s32[1,1024]{1,0:T(1,128)} %src_ref.1) | copy-start | bytes 12292
  43.9 9.1 %collective-permute-start.7 = (bf16[128,512]{1,0:T(8,128)(2,1)S(1)}, bf16[128,512]{1,0:T(8,128)(2,1)S(1)}, u32[]{:S(2)}, u32[]{:S(2)}) collective-permute-start(bf16[128,512]{1,0:T(8,128)(2,1)S(1)} %collective-permute-done.3.table_1), channel_id=1, source_target_pairs={{0,1},{1,0},{2,3},{3,2},{4,5},{5,4},{6,7},{7,6},{8,9},{9,8},{10,11... | collective-permute-start | bytes 393224 | tf_op jit(solution)/shard_map/ppermute | solution.py:333
  44.1 9.0 %collective-permute-start.8 = (bf16[128,512]{1,0:T(8,128)(2,1)S(1)}, bf16[128,512]{1,0:T(8,128)(2,1)S(1)}, u32[]{:S(2)}, u32[]{:S(2)}) collective-permute-start(bf16[128,512]{1,0:T(8,128)(2,1)S(1)} %collective-permute-done.4.table_2), channel_id=1, source_target_pairs={{0,1},{1,0},{2,3},{3,2},{4,5},{5,4},{6,7},{7,6},{8,9},{9,8},{10,11... | collective-permute-start | bytes 393224 | tf_op jit(solution)/shard_map/ppermute | solution.py:333
  46.3 6.7 %collective-permute-start.9 = (bf16[128,512]{1,0:T(8,128)(2,1)S(1)}, bf16[128,512]{1,0:T(8,128)(2,1)S(1)}, u32[]{:S(2)}, u32[]{:S(2)}) collective-permute-start(bf16[128,512]{1,0:T(8,128)(2,1)S(1)} %collective-permute-done.5.table_3), channel_id=1, source_target_pairs={{0,1},{1,0},{2,3},{3,2},{4,5},{5,4},{6,7},{7,6},{8,9},{9,8},{10,11... | collective-permute-start | bytes 393224 | tf_op jit(solution)/shard_map/ppermute | solution.py:333
  46.6 4.7 %collective-permute-start.1 = (bf16[16,512]{1,0:T(8,128)(2,1)S(1)}, bf16[16,512]{1,0:T(8,128)(2,1)S(1)}, u32[]{:S(2)}, u32[]{:S(2)}) collective-permute-start(bf16[16,512]{1,0:T(8,128)(2,1)S(1)} %shard_map.105), channel_id=1, source_target_pairs={{1,0},{2,1},{3,2},{4,3},{5,4},{6,5},{7,6},{8,7},{9,8},{10,9},{11,1... | collective-permute-start | bytes 49160 | tf_op jit(solution)/shard_map/ppermute | solution.py:311
